TPU v7x, 512 devices: a whole 4x4x16 slice. The times are simulated.
512 devices in a mesh: section: 8 (over x, y_hi), dp: 64 (over y_lo, z, core).
Axes of the slice: x: 4, y: 4 (y_hi: 2, y_lo: 2; y = y_hi * 2 + y_lo), z: 16, core: 2. Of those that a mesh axis runs over, the one named last changes fastest.
Arguments:
- section_in: bfloat16 [8, 4, 64, 128, 1536], P('section', None, 'dp'), may hold values from -6 to 6
- top_grad: bfloat16 [4, 64, 128, 1536], P(None, 'dp'), may hold values from -0.078125 to 0.078125
- seq_lengths: int32 [4, 64], P(None, 'dp'), may hold values from 32 to 128, as said below
- lang_labels: int32 [4, 64], P(None, 'dp'), may hold values from 0 to 28
- norm_gain: float32 [8, 1536], P('section'), may hold values from 0.5 to 1.5
- w_down: bfloat16 [8, 1536, 256], P('section'), may hold values from -0.15625 to 0.15625
- w_up: bfloat16 [8, 256, 1536], P('section'), may hold values from -0.375 to 0.375
- critic_first: bfloat16 [1536, 768], P('section'), may hold values from -0.15625 to 0.15625
- critic_second: bfloat16 [768, 29], replicated, may hold values from -0.21875 to 0.21875
Outputs:
- grad_w_down: float32 [8, 1536, 256], P('section', 'dp')
- grad_w_up: float32 [8, 256, 1536], P('section', None, 'dp')
- grad_norm_gain: float32 [8, 1536], P('section', 'dp')
- grad_critic_first: float32 [1536, 768], P('section', 'dp')
- grad_critic_second: float32 [768, 29], P('dp')
Inputs may be any that keep to these rules, and one draw needn't show every extreme that they name: `seq_lengths`: in every draw some sequence has all 128 tokens valid.
All inputs are finite; a program needn't handle non-finite values.
Results may differ from a plain program's by a relative error of at most 0.023.
Values may be sent and summed in bfloat16 or wider, within the bound.
No kernel may reach another device: no remote copies, remote signals or barrier semaphores. Data moves between devices by JAX's collectives and lax.ppermute only.
A program may use at most 64 MiB of HBM per device.

v0:
```python
import jax
import jax.numpy as jnp
from jax import lax
from jax.sharding import PartitionSpec as P

EPSILON = 1e-06
REVERSAL = 0.5


def from_root(array, axis, root):
    mine = lax.axis_index(axis) == root
    return lax.psum(jnp.where(mine, array, jnp.zeros_like(array)), axis)


def from_behind(block, axis, distance):
    devices = range(lax.axis_size(axis))
    route = [(i - distance, i) for i in devices if i - distance in devices]
    return lax.ppermute(block, axis, route)


def silu_slope(pre_act):
    sigma = jax.nn.sigmoid(pre_act)
    return sigma * (1.0 + pre_act * (1.0 - sigma))


def inner_rows(left, right):
    return lax.dot_general(
        left, right, (((0,), (0,)), ((), ())), preferred_element_type=jnp.float32
    )


def adapter_backward(local_rows, upstream, gain_row, down_proj, up_proj):
    values = local_rows.astype(jnp.float32)
    inv_rms = lax.rsqrt(jnp.mean(values * values, axis=-1, keepdims=True) + EPSILON)
    unit_rows = values * inv_rms
    normed = (unit_rows * gain_row[None, :]).astype(jnp.bfloat16)
    pre_act = jnp.dot(normed, down_proj, preferred_element_type=jnp.float32)
    hidden = jax.nn.silu(pre_act).astype(jnp.bfloat16)
    grad_up = inner_rows(hidden, upstream)
    grad_hidden = jnp.dot(upstream, up_proj.T, preferred_element_type=jnp.float32)
    grad_pre = (grad_hidden * silu_slope(pre_act)).astype(jnp.bfloat16)
    grad_down = inner_rows(normed, grad_pre)
    grad_normed = jnp.dot(grad_pre, down_proj.T, preferred_element_type=jnp.float32)
    grad_gain = jnp.sum(grad_normed * unit_rows, axis=0)
    scaled = grad_normed * gain_row[None, :]
    grad_input = upstream.astype(jnp.float32) + inv_rms * (
        scaled - unit_rows * jnp.mean(scaled * unit_rows, axis=-1, keepdims=True)
    )
    return (grad_input, grad_down, grad_up, grad_gain)


def critic_pass(pooled, lang_labels, critic_first, critic_second, section_place):
    batch_rows = pooled.shape[0] * pooled.shape[1]
    features = pooled.shape[2]
    values = pooled.reshape(batch_rows, features).astype(jnp.float32)
    inv_rms = lax.rsqrt(jnp.mean(values * values, axis=-1, keepdims=True) + EPSILON)
    unit_rows = values * inv_rms
    normed = unit_rows.astype(jnp.bfloat16)
    band_rows = critic_first.shape[0]
    normed_band = lax.dynamic_slice_in_dim(normed, section_place * band_rows, band_rows, 1)
    full_first = lax.all_gather(critic_first, "section", axis=0, tiled=True)
    pre_act = jnp.dot(normed, full_first, preferred_element_type=jnp.float32)
    hidden = jax.nn.silu(pre_act).astype(jnp.bfloat16)
    logits = jnp.dot(hidden, critic_second, preferred_element_type=jnp.float32)
    exponent = jnp.exp(logits)
    probabilities = exponent / jnp.sum(exponent, axis=-1, keepdims=True)
    onehot = (
        lang_labels.reshape(batch_rows)[:, None] == jnp.arange(critic_second.shape[1])[None, :]
    ).astype(jnp.float32)
    grad_logits = (probabilities - onehot).astype(jnp.bfloat16)
    grad_second = inner_rows(hidden, grad_logits)
    grad_hidden = jnp.dot(grad_logits, critic_second.T, preferred_element_type=jnp.float32)
    grad_pre = (grad_hidden * silu_slope(pre_act)).astype(jnp.bfloat16)
    grad_first = inner_rows(normed_band, grad_pre)
    grad_normed = jnp.dot(grad_pre, full_first.T, preferred_element_type=jnp.float32)
    grad_pooled = inv_rms * (
        grad_normed - unit_rows * jnp.mean(grad_normed * unit_rows, axis=-1, keepdims=True)
    )
    return (grad_first, grad_second, grad_pooled)


def body(
    section_in,
    top_grad,
    seq_lengths,
    lang_labels,
    norm_gain,
    w_down,
    w_up,
    critic_first,
    critic_second,
):
    sections = lax.axis_size("section")
    section_place = lax.axis_index("section")
    target = sections // 2
    inputs = section_in[0]
    gain_row = norm_gain[0]
    down_proj = w_down[0]
    up_proj = w_up[0]
    micro_count, seq_dev, seq_len, features = inputs.shape
    token_rows = seq_dev * seq_len
    positions = jnp.arange(seq_len)
    valid_mask = positions[None, None, :] < seq_lengths[:, :, None]
    mask_values = valid_mask.astype(jnp.float32)
    lengths = seq_lengths.astype(jnp.float32)
    totals = jnp.einsum(
        "mnt,mntd->mnd", valid_mask.astype(jnp.bfloat16), inputs, preferred_element_type=jnp.float32
    )
    pooled = (totals / lengths[:, :, None]).astype(jnp.bfloat16)
    pooled = from_root(pooled, "section", target)
    grad_first, grad_second, grad_pooled = critic_pass(
        pooled, lang_labels, critic_first, critic_second, section_place
    )
    is_target = (section_place == target).astype(jnp.float32)
    reversal = (
        -REVERSAL
        * is_target
        * grad_pooled.reshape(micro_count, seq_dev, features)
        / lengths[:, :, None]
    )
    is_last = section_place == sections - 1

    def advance(moment, carry):
        incoming, down_sum, up_sum, gain_sum = carry
        micro_now = moment - (sections - 1 - section_place)
        is_live = (micro_now >= 0) & (micro_now < micro_count)
        slot_index = jnp.clip(micro_now, 0, micro_count - 1)
        local_rows = lax.dynamic_index_in_dim(inputs, slot_index, 0, keepdims=False).reshape(
            token_rows, features
        )
        top_rows = lax.dynamic_index_in_dim(top_grad, slot_index, 0, keepdims=False).reshape(
            token_rows, features
        )
        upstream = jnp.where(is_last, top_rows, incoming)
        reverse_rows = lax.dynamic_index_in_dim(reversal, slot_index, 0, keepdims=False)
        mask_rows = lax.dynamic_index_in_dim(mask_values, slot_index, 0, keepdims=False)
        extra = (reverse_rows[:, None, :] * mask_rows[:, :, None]).reshape(token_rows, features)

        def active(operand):
            grad_input, grad_down, grad_up, grad_gain = adapter_backward(
                local_rows, upstream, gain_row, down_proj, up_proj
            )
            return ((grad_input + extra).astype(jnp.bfloat16), grad_down, grad_up, grad_gain)

        def resting(operand):
            return (
                jnp.zeros_like(incoming),
                jnp.zeros_like(down_sum),
                jnp.zeros_like(up_sum),
                jnp.zeros_like(gain_sum),
            )

        outgoing, grad_down, grad_up, grad_gain = lax.cond(is_live, active, resting, 0)
        received = from_behind(outgoing, "section", -1)
        return (received, down_sum + grad_down, up_sum + grad_up, gain_sum + grad_gain)

    initial = (
        jnp.zeros((token_rows, features), jnp.bfloat16),
        jnp.zeros(down_proj.shape, jnp.float32),
        jnp.zeros(up_proj.shape, jnp.float32),
        jnp.zeros((features,), jnp.float32),
    )
    finished = lax.fori_loop(0, micro_count + sections - 1, advance, initial)
    summed = (
        lax.psum_scatter(finished[1], "dp", scatter_dimension=0, tiled=True),
        lax.psum_scatter(finished[2], "dp", scatter_dimension=1, tiled=True),
        lax.psum_scatter(finished[3], "dp", scatter_dimension=0, tiled=True),
        lax.psum_scatter(grad_first, "dp", scatter_dimension=1, tiled=True),
        lax.psum_scatter(grad_second, "dp", scatter_dimension=0, tiled=True),
    )
    return (summed[0][None], summed[1][None], summed[2][None], summed[3], summed[4])


def solution(mesh):
    return jax.shard_map(
        body,
        mesh=mesh,
        in_specs=(
            P("section", None, "dp", None, None),
            P(None, "dp", None, None),
            P(None, "dp"),
            P(None, "dp"),
            P("section", None),
            P("section", None, None),
            P("section", None, None),
            P("section", None),
            P(),
        ),
        out_specs=(
            P("section", "dp", None),
            P("section", None, "dp"),
            P("section", "dp"),
            P("section", "dp"),
            P("dp", None),
        ),
        check_vma=False,
    )
```

profile of v0, /device:TPU:16, one launch (start us, length us, event | category | flops | bytes accessed | tf_op | source)
XLA Modules:
  0.0 760.2 jit_solution(11671315179703268746)
XLA Ops:
  11.2 40.3 %psum.7 = bf16[4,1536]{1,0:T(4,128)(2,1)S(1)} all-reduce(bf16[4,1536]{1,0:T(4,128)(2,1)S(1)} %fusion.42), channel_id=1, replica_groups=mesh['section'=8,'dp'=64] {'section'}, use_global_device_ids=true, to_apply=%region_0.1 | all-reduce | flops 6144 | bytes 24576 | tf_op jit(solution)/shard_map/psum | solution.py:12
  51.7 33.8 %all-gather.2.cloned.1.call-done = bf16[1536,768]{1,0:T(8,128)(2,1)} async-done(((bf16[192,768]{1,0:T(8,128)(2,1)}), bf16[1536,768]{1,0:T(8,128)(2,1)}) %all-gather.2.cloned.1.call-update) | async-done | bytes 2359312 | tf_op jit(solution)/shard_map/all_gather | solution.py:61
  90.0 202.0 %while.22 = (s32[]{:T(128)}, bf16[128,1536]{1,0:T(8,128)(2,1)}, f32[1536,256]{1,0:T(8,128)}, f32[256,1536]{1,0:T(8,128)}, f32[1536]{0:T(1024)S(1)}, /*index=5*/s...) while((s32[]{:T(128)}, bf16[128,1536]{1,0:T(8,128)(2,1)}, ...), condition=%wide.region_10.11_spmd.clone, body=%wide.region_4.10_spmd.clone.sunk | while | flops 511249024 | bytes 36070916 | solution.py:163
  91.1 4.9 collective-permute-start
  98.8 6.2 collective-permute-done
  106.2 4.0 collective-permute-start
  110.2 2.8 select_add_fusion.6
  112.9 2.8 select_add_fusion.7
  115.8 3.5 collective-permute-done
  120.4 3.1 collective-permute-start
  123.5 2.8 select_add_fusion.6
  126.2 2.8 select_add_fusion.7
  129.1 3.7 collective-permute-done
  136.1 2.8 select_add_fusion.6
  138.9 2.8 select_add_fusion.7
  141.7 4.6 collective-permute-done
  149.3 2.8 select_add_fusion.6
  152.1 2.8 select_add_fusion.7
  154.9 4.9 collective-permute-done
  162.8 2.8 select_add_fusion.6
  165.6 2.8 select_add_fusion.7
  168.4 27.5 %collective-permute-done = bf16[128,1536]{1,0:T(8,128)(2,1)} collective-permute-done((bf16[128,1536]{1,0:T(8,128)(2,1)}, bf16[128,1536]{1,0:T(8,128)(2,1)}, u32[]{:S(2)}, u32[]{:S(2)}) %collective-permute-start) | collective-permute-done | bytes 393248 | tf_op jit(solution)/shard_map/while/body/eval_jaxpr/ppermute | solution.py:18
  196.0 7.4 conditional.3
  205.3 2.8 select_add_fusion.6
  208.0 2.8 select_add_fusion.7
  210.9 4.9 collective-permute-done
  215.8 7.4 conditional.3
  225.1 2.8 select_add_fusion.6
  227.8 2.8 select_add_fusion.7
  230.7 4.9 collective-permute-done
  235.6 7.4 conditional.3
  244.9 2.8 select_add_fusion.6
  247.7 2.8 select_add_fusion.7
  250.5 4.9 collective-permute-done
  255.4 7.4 conditional.3
  264.7 2.8 select_add_fusion.6
  267.5 2.8 select_add_fusion.7
  270.3 8.2 %collective-permute-done = bf16[128,1536]{1,0:T(8,128)(2,1)} collective-permute-done((bf16[128,1536]{1,0:T(8,128)(2,1)}, bf16[128,1536]{1,0:T(8,128)(2,1)}, u32[]{:S(2)}, u32[]{:S(2)}) %collective-permute-start) | collective-permute-done | bytes 393248 | tf_op jit(solution)/shard_map/while/body/eval_jaxpr/ppermute | solution.py:18
  279.6 4.0 collective-permute-start
  283.6 2.8 select_add_fusion.6
  286.4 2.8 select_add_fusion.7
  289.2 2.8 collective-permute-done
  292.0 3.1 copy.17
  296.5 114.0 %fusion.52 = (f32[192,16]{0,1:T(8,128)S(1)}, f32[16,29]{1,0:T(8,128)S(1)}) fusion(f32[192,768]{0,1:T(8,128)S(1)} %fusion.44, f32[768,29]{1,0:T(8,128)S(1)} %fusion.49), kind=kCustom, calls=%all-reduce-scatter.2 | all-reduce-scatter fusion | flops 226305 | bytes 695104
  415.9 14.8 %collective-permute-start.32 = (f32[12,29]{1,0:T(8,128)S(1)}, f32[12,29]{1,0:T(8,128)S(1)}, u32[]{:S(2)}, u32[]{:S(2)}) collective-permute-start(f32[12,29]{1,0:T(8,128)S(1)} %slice.1), channel_id=1, source_target_pairs={{0,16},{1,17},{2,18},{3,19},{4,20},{5,21},{6,22},{7,23},{8,24},{9,... | collective-permute-start | bytes 4184
  434.7 4.8 collective-permute-start.22
  439.5 12.1 %collective-permute-start.23 = (f32[16,29]{1,0:T(8,128)S(1)}, f32[16,29]{1,0:T(8,128)S(1)}, u32[]{:S(2)}, u32[]{:S(2)}) collective-permute-start(f32[16,29]{1,0:T(8,128)S(1)} %get-tuple-element.568), channel_id=1, source_target_pairs={{0,7},{1,8},{2,9},{3,10},{4,11},{5,12},{6,13},{7,14},{8,15},{9,16}... | collective-permute-start | bytes 5576
  451.6 2.7 collective-permute-start.24
  454.4 5.6 collective-permute-start.25
  460.0 6.8 collective-permute-start.26
  470.8 3.1 collective-permute-start.29
  473.8 3.5 collective-permute-start.30
  478.6 4.0 collective-permute-start.1
  482.7 3.0 collective-permute-start.10
  487.6 4.8 collective-permute-start.12
  492.5 4.4 collective-permute-start.13
  498.7 107.5 %all-reduce = f32[1536]{0:T(1024)S(1)} all-reduce(f32[1536]{0:T(1024)S(1)} %get-tuple-element.454), channel_id=4, replica_groups=mesh['section'=8,'dp'=64] {'dp'}, use_global_device_ids=true, to_apply=%region_13.14.clone | all-reduce | flops 1536 | bytes 12288
  608.9 2.3 collective-permute-start.2
  611.2 6.3 collective-permute-start.3
  622.5 4.0 collective-permute-start.6
  626.5 5.1 collective-permute-start.7
  631.6 13.1 %collective-permute-start.8 = (f32[192,16]{0,1:T(8,128)S(1)}, f32[192,16]{0,1:T(8,128)S(1)}, u32[]{:S(2)}, u32[]{:S(2)}) collective-permute-start(f32[192,16]{0,1:T(8,128)S(1)} %get-tuple-element.567), channel_id=1, source_target_pairs={{0,8},{1,9},{2,10},{3,11},{4,12},{5,13},{6,14},{7,15},{8,16},{9,17... | collective-permute-start | bytes 36872
  644.7 2.5 collective-permute-start.9
  651.1 102.6 %reduce-scatter.7.cloned.1.call-done = f32[24,256]{1,0:T(8,128)} async-done(((f32[1536,256]{1,0:T(8,128)}), f32[24,256]{1,0:T(8,128)}) %reduce-scatter.7.cloned.1.call-update) | async-done | bytes 24592 | tf_op jit(solution)/shard_map/reduce_scatter | solution.py:165
  (235 shorter events, 99.4 us)
Async XLA Ops:
  7.2 80.6 %copy-start = (bf16[768,29]{0,1:T(8,128)(2,1)S(1)}, bf16[768,29]{0,1:T(8,128)(2,1)}, u32[]{:S(2)}) copy-start(bf16[768,29]{0,1:T(8,128)(2,1)} %param.21) | copy-start | bytes 133636
  7.2 78.3 %all-gather.2.cloned.1.call-start = ((), (), s32[]{:S(2)}) async-start(), calls=%async_computation.2 | async-start | bytes 2654208 | tf_op jit(solution)/shard_map/all_gather | solution.py:61
  7.9 643.2 %reduce-scatter.9.cloned.1.call-start = ((), (), s32[]{:S(2)}) async-start(), calls=%async_computation.4 | async-start | bytes 1597440 | tf_op jit(solution)/shard_map/reduce_scatter | solution.py:166
  11.1 76.9 %copy-start.6 = (s32[4,1]{0,1:T(1,128)S(1)}, s32[4,1]{0,1:T(1,128)}, u32[]{:S(2)}) copy-start(s32[4,1]{0,1:T(1,128)} %param.16) | copy-start | bytes 52
  85.5 2.7 copy-start.3
  88.0 2.0 copy-start.4
  88.0 2.0 copy-start.5
  91.1 13.9 %collective-permute-start = (bf16[128,1536]{1,0:T(8,128)(2,1)}, bf16[128,1536]{1,0:T(8,128)(2,1)}, u32[]{:S(2)}, u32[]{:S(2)}) collective-permute-start(bf16[128,1536]{1,0:T(8,128)(2,1)} %get-tuple-element.665), channel_id=1, source_target_pairs={{64,0},{128,64},{192,128},{256,192},{320,256},{384,320},{448,384},... | collective-permute-start | bytes 1179656 | tf_op jit(solution)/shard_map/while/body/eval_jaxpr/ppermute | solution.py:18
  106.2 13.1 %collective-permute-start = (bf16[128,1536]{1,0:T(8,128)(2,1)}, bf16[128,1536]{1,0:T(8,128)(2,1)}, u32[]{:S(2)}, u32[]{:S(2)}) collective-permute-start(bf16[128,1536]{1,0:T(8,128)(2,1)} %get-tuple-element.665), channel_id=1, source_target_pairs={{64,0},{128,64},{192,128},{256,192},{320,256},{384,320},{448,384},... | collective-permute-start | bytes 1179656 | tf_op jit(solution)/shard_map/while/body/eval_jaxpr/ppermute | solution.py:18
  120.4 12.4 %collective-permute-start = (bf16[128,1536]{1,0:T(8,128)(2,1)}, bf16[128,1536]{1,0:T(8,128)(2,1)}, u32[]{:S(2)}, u32[]{:S(2)}) collective-permute-start(bf16[128,1536]{1,0:T(8,128)(2,1)} %get-tuple-element.665), channel_id=1, source_target_pairs={{64,0},{128,64},{192,128},{256,192},{320,256},{384,320},{448,384},... | collective-permute-start | bytes 1179656 | tf_op jit(solution)/shard_map/while/body/eval_jaxpr/ppermute | solution.py:18
  133.9 12.4 %collective-permute-start = (bf16[128,1536]{1,0:T(8,128)(2,1)}, bf16[128,1536]{1,0:T(8,128)(2,1)}, u32[]{:S(2)}, u32[]{:S(2)}) collective-permute-start(bf16[128,1536]{1,0:T(8,128)(2,1)} %get-tuple-element.665), channel_id=1, source_target_pairs={{64,0},{128,64},{192,128},{256,192},{320,256},{384,320},{448,384},... | collective-permute-start | bytes 1179656 | tf_op jit(solution)/shard_map/while/body/eval_jaxpr/ppermute | solution.py:18
  147.4 12.4 %collective-permute-start = (bf16[128,1536]{1,0:T(8,128)(2,1)}, bf16[128,1536]{1,0:T(8,128)(2,1)}, u32[]{:S(2)}, u32[]{:S(2)}) collective-permute-start(bf16[128,1536]{1,0:T(8,128)(2,1)} %get-tuple-element.665), channel_id=1, source_target_pairs={{64,0},{128,64},{192,128},{256,192},{320,256},{384,320},{448,384},... | collective-permute-start | bytes 1179656 | tf_op jit(solution)/shard_map/while/body/eval_jaxpr/ppermute | solution.py:18
  160.9 35.0 %collective-permute-start = (bf16[128,1536]{1,0:T(8,128)(2,1)}, bf16[128,1536]{1,0:T(8,128)(2,1)}, u32[]{:S(2)}, u32[]{:S(2)}) collective-permute-start(bf16[128,1536]{1,0:T(8,128)(2,1)} %get-tuple-element.665), channel_id=1, source_target_pairs={{64,0},{128,64},{192,128},{256,192},{320,256},{384,320},{448,384},... | collective-permute-start | bytes 1179656 | tf_op jit(solution)/shard_map/while/body/eval_jaxpr/ppermute | solution.py:18
  196.0 4.2 copy-start.8
  198.8 1.7 copy-start.1
  200.6 1.1 copy-start.2
  203.4 12.4 %collective-permute-start = (bf16[128,1536]{1,0:T(8,128)(2,1)}, bf16[128,1536]{1,0:T(8,128)(2,1)}, u32[]{:S(2)}, u32[]{:S(2)}) collective-permute-start(bf16[128,1536]{1,0:T(8,128)(2,1)} %get-tuple-element.665), channel_id=1, source_target_pairs={{64,0},{128,64},{192,128},{256,192},{320,256},{384,320},{448,384},... | collective-permute-start | bytes 1179656 | tf_op jit(solution)/shard_map/while/body/eval_jaxpr/ppermute | solution.py:18
  215.8 4.2 copy-start.8
  218.7 1.7 copy-start.1
  220.4 1.1 copy-start.2
  223.2 12.4 %collective-permute-start = (bf16[128,1536]{1,0:T(8,128)(2,1)}, bf16[128,1536]{1,0:T(8,128)(2,1)}, u32[]{:S(2)}, u32[]{:S(2)}) collective-permute-start(bf16[128,1536]{1,0:T(8,128)(2,1)} %get-tuple-element.665), channel_id=1, source_target_pairs={{64,0},{128,64},{192,128},{256,192},{320,256},{384,320},{448,384},... | collective-permute-start | bytes 1179656 | tf_op jit(solution)/shard_map/while/body/eval_jaxpr/ppermute | solution.py:18
  235.6 4.2 copy-start.8
  238.5 1.7 copy-start.1
  240.2 1.1 copy-start.2
  243.0 12.4 %collective-permute-start = (bf16[128,1536]{1,0:T(8,128)(2,1)}, bf16[128,1536]{1,0:T(8,128)(2,1)}, u32[]{:S(2)}, u32[]{:S(2)}) collective-permute-start(bf16[128,1536]{1,0:T(8,128)(2,1)} %get-tuple-element.665), channel_id=1, source_target_pairs={{64,0},{128,64},{192,128},{256,192},{320,256},{384,320},{448,384},... | collective-permute-start | bytes 1179656 | tf_op jit(solution)/shard_map/while/body/eval_jaxpr/ppermute | solution.py:18
  255.4 4.2 copy-start.8
  258.3 1.7 copy-start.1
  260.0 1.1 copy-start.2
  262.8 15.7 %collective-permute-start = (bf16[128,1536]{1,0:T(8,128)(2,1)}, bf16[128,1536]{1,0:T(8,128)(2,1)}, u32[]{:S(2)}, u32[]{:S(2)}) collective-permute-start(bf16[128,1536]{1,0:T(8,128)(2,1)} %get-tuple-element.665), channel_id=1, source_target_pairs={{64,0},{128,64},{192,128},{256,192},{320,256},{384,320},{448,384},... | collective-permute-start | bytes 1179656 | tf_op jit(solution)/shard_map/while/body/eval_jaxpr/ppermute | solution.py:18
  279.6 12.4 %collective-permute-start = (bf16[128,1536]{1,0:T(8,128)(2,1)}, bf16[128,1536]{1,0:T(8,128)(2,1)}, u32[]{:S(2)}, u32[]{:S(2)}) collective-permute-start(bf16[128,1536]{1,0:T(8,128)(2,1)} %get-tuple-element.665), channel_id=1, source_target_pairs={{64,0},{128,64},{192,128},{256,192},{320,256},{384,320},{448,384},... | collective-permute-start | bytes 1179656 | tf_op jit(solution)/shard_map/while/body/eval_jaxpr/ppermute | solution.py:18
  295.1 458.6 %reduce-scatter.7.cloned.1.call-start = ((), (), s32[]{:S(2)}) async-start(), calls=%async_computation.3 | async-start | bytes 1597440 | tf_op jit(solution)/shard_map/reduce_scatter | solution.py:165
  295.8 201.0 %copy-start.7 = (u32[512]{0:T(512)S(1)}, u32[512]{0:T(512)}, u32[]{:S(2)}) copy-start(u32[512]{0:T(512)} %constant.153) | copy-start | bytes 6148
  410.5 82.0 %collective-permute-start.16 = (f32[192,12]{0,1:T(8,128)S(1)}, f32[192,12]{0,1:T(8,128)S(1)}, u32[]{:S(2)}, u32[]{:S(2)}) collective-permute-start(f32[192,12]{0,1:T(8,128)S(1)} %slice), channel_id=1, source_target_pairs={{0,16},{1,17},{2,18},{3,19},{4,20},{5,21},{6,22},{7,23},{8,24},{9,... | collective-permute-start | bytes 27656
  411.8 21.6 %collective-permute-start.17 = (f32[16,29]{1,0:T(8,128)S(1)}, f32[16,29]{1,0:T(8,128)S(1)}, u32[]{:S(2)}, u32[]{:S(2)}) collective-permute-start(f32[16,29]{1,0:T(8,128)S(1)} %get-tuple-element.568), channel_id=1, source_target_pairs={{0,1},{1,2},{2,3},{3,4},{4,5},{5,6},{6,7},{7,8},{8,9},{9,10},{10,1... | collective-permute-start | bytes 5576
  413.3 21.3 %collective-permute-start.18 = (f32[16,29]{1,0:T(8,128)S(1)}, f32[16,29]{1,0:T(8,128)S(1)}, u32[]{:S(2)}, u32[]{:S(2)}) collective-permute-start(f32[16,29]{1,0:T(8,128)S(1)} %get-tuple-element.568), channel_id=1, source_target_pairs={{0,2},{1,3},{2,4},{3,5},{4,6},{5,7},{6,8},{7,9},{8,10},{9,11},{10,... | collective-permute-start | bytes 5576
  414.6 24.9 %collective-permute-start.19 = (f32[16,29]{1,0:T(8,128)S(1)}, f32[16,29]{1,0:T(8,128)S(1)}, u32[]{:S(2)}, u32[]{:S(2)}) collective-permute-start(f32[16,29]{1,0:T(8,128)S(1)} %get-tuple-element.568), channel_id=1, source_target_pairs={{0,3},{1,4},{2,5},{3,6},{4,7},{5,8},{6,9},{7,10},{8,11},{9,12},{10... | collective-permute-start | bytes 5576
  415.9 16.1 %collective-permute-start.32 = (f32[12,29]{1,0:T(8,128)S(1)}, f32[12,29]{1,0:T(8,128)S(1)}, u32[]{:S(2)}, u32[]{:S(2)}) collective-permute-start(f32[12,29]{1,0:T(8,128)S(1)} %slice.1), channel_id=1, source_target_pairs={{0,16},{1,17},{2,18},{3,19},{4,20},{5,21},{6,22},{7,23},{8,24},{9,... | collective-permute-start | bytes 4184
  432.1 19.5 %collective-permute-start.20 = (f32[16,29]{1,0:T(8,128)S(1)}, f32[16,29]{1,0:T(8,128)S(1)}, u32[]{:S(2)}, u32[]{:S(2)}) collective-permute-start(f32[16,29]{1,0:T(8,128)S(1)} %get-tuple-element.568), channel_id=1, source_target_pairs={{0,4},{1,5},{2,6},{3,7},{4,8},{5,9},{6,10},{7,11},{8,12},{9,13},{1... | collective-permute-start | bytes 5576
  433.4 21.0 %collective-permute-start.21 = (f32[16,29]{1,0:T(8,128)S(1)}, f32[16,29]{1,0:T(8,128)S(1)}, u32[]{:S(2)}, u32[]{:S(2)}) collective-permute-start(f32[16,29]{1,0:T(8,128)S(1)} %get-tuple-element.568), channel_id=1, source_target_pairs={{0,5},{1,6},{2,7},{3,8},{4,9},{5,10},{6,11},{7,12},{8,13},{9,14},{... | collective-permute-start | bytes 5576
  434.7 25.3 %collective-permute-start.22 = (f32[16,29]{1,0:T(8,128)S(1)}, f32[16,29]{1,0:T(8,128)S(1)}, u32[]{:S(2)}, u32[]{:S(2)}) collective-permute-start(f32[16,29]{1,0:T(8,128)S(1)} %get-tuple-element.568), channel_id=1, source_target_pairs={{0,6},{1,7},{2,8},{3,9},{4,10},{5,11},{6,12},{7,13},{8,14},{9,15},... | collective-permute-start | bytes 5576
  439.5 27.3 %collective-permute-start.23 = (f32[16,29]{1,0:T(8,128)S(1)}, f32[16,29]{1,0:T(8,128)S(1)}, u32[]{:S(2)}, u32[]{:S(2)}) collective-permute-start(f32[16,29]{1,0:T(8,128)S(1)} %get-tuple-element.568), channel_id=1, source_target_pairs={{0,7},{1,8},{2,9},{3,10},{4,11},{5,12},{6,13},{7,14},{8,15},{9,16}... | collective-permute-start | bytes 5576
  451.6 17.2 %collective-permute-start.24 = (f32[16,29]{1,0:T(8,128)S(1)}, f32[16,29]{1,0:T(8,128)S(1)}, u32[]{:S(2)}, u32[]{:S(2)}) collective-permute-start(f32[16,29]{1,0:T(8,128)S(1)} %get-tuple-element.568), channel_id=1, source_target_pairs={{0,8},{1,9},{2,10},{3,11},{4,12},{5,13},{6,14},{7,15},{8,16},{9,17... | collective-permute-start | bytes 5576
  454.4 16.4 %collective-permute-start.25 = (f32[16,29]{1,0:T(8,128)S(1)}, f32[16,29]{1,0:T(8,128)S(1)}, u32[]{:S(2)}, u32[]{:S(2)}) collective-permute-start(f32[16,29]{1,0:T(8,128)S(1)} %get-tuple-element.568), channel_id=1, source_target_pairs={{0,9},{1,10},{2,11},{3,12},{4,13},{5,14},{6,15},{7,16},{8,17},{9,1... | collective-permute-start | bytes 5576
  460.0 13.8 %collective-permute-start.26 = (f32[16,29]{1,0:T(8,128)S(1)}, f32[16,29]{1,0:T(8,128)S(1)}, u32[]{:S(2)}, u32[]{:S(2)}) collective-permute-start(f32[16,29]{1,0:T(8,128)S(1)} %get-tuple-element.568), channel_id=1, source_target_pairs={{0,10},{1,11},{2,12},{3,13},{4,14},{5,15},{6,16},{7,17},{8,18},{9,... | collective-permute-start | bytes 5576
  466.8 10.5 %collective-permute-start.27 = (f32[16,29]{1,0:T(8,128)S(1)}, f32[16,29]{1,0:T(8,128)S(1)}, u32[]{:S(2)}, u32[]{:S(2)}) collective-permute-start(f32[16,29]{1,0:T(8,128)S(1)} %get-tuple-element.568), channel_id=1, source_target_pairs={{0,11},{1,12},{2,13},{3,14},{4,15},{5,16},{6,17},{7,18},{8,19},{9,... | collective-permute-start | bytes 5576
  468.8 9.9 %collective-permute-start.28 = (f32[16,29]{1,0:T(8,128)S(1)}, f32[16,29]{1,0:T(8,128)S(1)}, u32[]{:S(2)}, u32[]{:S(2)}) collective-permute-start(f32[16,29]{1,0:T(8,128)S(1)} %get-tuple-element.568), channel_id=1, source_target_pairs={{0,12},{1,13},{2,14},{3,15},{4,16},{5,17},{6,18},{7,19},{8,20},{9,... | collective-permute-start | bytes 5576
  470.8 11.9 %collective-permute-start.29 = (f32[16,29]{1,0:T(8,128)S(1)}, f32[16,29]{1,0:T(8,128)S(1)}, u32[]{:S(2)}, u32[]{:S(2)}) collective-permute-start(f32[16,29]{1,0:T(8,128)S(1)} %get-tuple-element.568), channel_id=1, source_target_pairs={{0,13},{1,14},{2,15},{3,16},{4,17},{5,18},{6,19},{7,20},{8,21},{9,... | collective-permute-start | bytes 5576
  473.8 11.9 %collective-permute-start.30 = (f32[16,29]{1,0:T(8,128)S(1)}, f32[16,29]{1,0:T(8,128)S(1)}, u32[]{:S(2)}, u32[]{:S(2)}) collective-permute-start(f32[16,29]{1,0:T(8,128)S(1)} %get-tuple-element.568), channel_id=1, source_target_pairs={{0,14},{1,15},{2,16},{3,17},{4,18},{5,19},{6,20},{7,21},{8,22},{9,... | collective-permute-start | bytes 5576
  477.3 10.3 %collective-permute-start.31 = (f32[16,29]{1,0:T(8,128)S(1)}, f32[16,29]{1,0:T(8,128)S(1)}, u32[]{:S(2)}, u32[]{:S(2)}) collective-permute-start(f32[16,29]{1,0:T(8,128)S(1)} %get-tuple-element.568), channel_id=1, source_target_pairs={{0,15},{1,16},{2,17},{3,18},{4,19},{5,20},{6,21},{7,22},{8,23},{9,... | collective-permute-start | bytes 5576
  478.6 127.6 %collective-permute-start.1 = (f32[192,16]{0,1:T(8,128)S(1)}, f32[192,16]{0,1:T(8,128)S(1)}, u32[]{:S(2)}, u32[]{:S(2)}) collective-permute-start(f32[192,16]{0,1:T(8,128)S(1)} %get-tuple-element.567), channel_id=1, source_target_pairs={{0,1},{1,2},{2,3},{3,4},{4,5},{5,6},{6,7},{7,8},{8,9},{9,10},{10,1... | collective-permute-start | bytes 36872
  482.7 124.9 %collective-permute-start.10 = (f32[192,16]{0,1:T(8,128)S(1)}, f32[192,16]{0,1:T(8,128)S(1)}, u32[]{:S(2)}, u32[]{:S(2)}) collective-permute-start(f32[192,16]{0,1:T(8,128)S(1)} %get-tuple-element.567), channel_id=1, source_target_pairs={{0,10},{1,11},{2,12},{3,13},{4,14},{5,15},{6,16},{7,17},{8,18},{9,... | collective-permute-start | bytes 36872
  485.7 123.2 %collective-permute-start.11 = (f32[192,16]{0,1:T(8,128)S(1)}, f32[192,16]{0,1:T(8,128)S(1)}, u32[]{:S(2)}, u32[]{:S(2)}) collective-permute-start(f32[192,16]{0,1:T(8,128)S(1)} %get-tuple-element.567), channel_id=1, source_target_pairs={{0,11},{1,12},{2,13},{3,14},{4,15},{5,16},{6,17},{7,18},{8,19},{9,... | collective-permute-start | bytes 36872
  487.6 123.6 %collective-permute-start.12 = (f32[192,16]{0,1:T(8,128)S(1)}, f32[192,16]{0,1:T(8,128)S(1)}, u32[]{:S(2)}, u32[]{:S(2)}) collective-permute-start(f32[192,16]{0,1:T(8,128)S(1)} %get-tuple-element.567), channel_id=1, source_target_pairs={{0,12},{1,13},{2,14},{3,15},{4,16},{5,17},{6,18},{7,19},{8,20},{9,... | collective-permute-start | bytes 36872
  492.5 125.0 %collective-permute-start.13 = (f32[192,16]{0,1:T(8,128)S(1)}, f32[192,16]{0,1:T(8,128)S(1)}, u32[]{:S(2)}, u32[]{:S(2)}) collective-permute-start(f32[192,16]{0,1:T(8,128)S(1)} %get-tuple-element.567), channel_id=1, source_target_pairs={{0,13},{1,14},{2,15},{3,16},{4,17},{5,18},{6,19},{7,20},{8,21},{9,... | collective-permute-start | bytes 36872
  606.3 14.9 %collective-permute-start.14 = (f32[192,16]{0,1:T(8,128)S(1)}, f32[192,16]{0,1:T(8,128)S(1)}, u32[]{:S(2)}, u32[]{:S(2)}) collective-permute-start(f32[192,16]{0,1:T(8,128)S(1)} %get-tuple-element.567), channel_id=1, source_target_pairs={{0,14},{1,15},{2,16},{3,17},{4,18},{5,19},{6,20},{7,21},{8,22},{9,... | collective-permute-start | bytes 36872
  607.6 14.9 %collective-permute-start.15 = (f32[192,16]{0,1:T(8,128)S(1)}, f32[192,16]{0,1:T(8,128)S(1)}, u32[]{:S(2)}, u32[]{:S(2)}) collective-permute-start(f32[192,16]{0,1:T(8,128)S(1)} %get-tuple-element.567), channel_id=1, source_target_pairs={{0,15},{1,16},{2,17},{3,18},{4,19},{5,20},{6,21},{7,22},{8,23},{9,... | collective-permute-start | bytes 36872
  608.9 17.6 %collective-permute-start.2 = (f32[192,16]{0,1:T(8,128)S(1)}, f32[192,16]{0,1:T(8,128)S(1)}, u32[]{:S(2)}, u32[]{:S(2)}) collective-permute-start(f32[192,16]{0,1:T(8,128)S(1)} %get-tuple-element.567), channel_id=1, source_target_pairs={{0,2},{1,3},{2,4},{3,5},{4,6},{5,7},{6,8},{7,9},{8,10},{9,11},{10,... | collective-permute-start | bytes 36872
  611.2 20.4 %collective-permute-start.3 = (f32[192,16]{0,1:T(8,128)S(1)}, f32[192,16]{0,1:T(8,128)S(1)}, u32[]{:S(2)}, u32[]{:S(2)}) collective-permute-start(f32[192,16]{0,1:T(8,128)S(1)} %get-tuple-element.567), channel_id=1, source_target_pairs={{0,3},{1,4},{2,5},{3,6},{4,7},{5,8},{6,9},{7,10},{8,11},{9,12},{10... | collective-permute-start | bytes 36872
  617.5 27.2 %collective-permute-start.4 = (f32[192,16]{0,1:T(8,128)S(1)}, f32[192,16]{0,1:T(8,128)S(1)}, u32[]{:S(2)}, u32[]{:S(2)}) collective-permute-start(f32[192,16]{0,1:T(8,128)S(1)} %get-tuple-element.567), channel_id=1, source_target_pairs={{0,4},{1,5},{2,6},{3,7},{4,8},{5,9},{6,10},{7,11},{8,12},{9,13},{1... | collective-permute-start | bytes 36872
  621.2 26.7 %collective-permute-start.5 = (f32[192,16]{0,1:T(8,128)S(1)}, f32[192,16]{0,1:T(8,128)S(1)}, u32[]{:S(2)}, u32[]{:S(2)}) collective-permute-start(f32[192,16]{0,1:T(8,128)S(1)} %get-tuple-element.567), channel_id=1, source_target_pairs={{0,5},{1,6},{2,7},{3,8},{4,9},{5,10},{6,11},{7,12},{8,13},{9,14},{... | collective-permute-start | bytes 36872
  622.5 25.4 %collective-permute-start.6 = (f32[192,16]{0,1:T(8,128)S(1)}, f32[192,16]{0,1:T(8,128)S(1)}, u32[]{:S(2)}, u32[]{:S(2)}) collective-permute-start(f32[192,16]{0,1:T(8,128)S(1)} %get-tuple-element.567), channel_id=1, source_target_pairs={{0,6},{1,7},{2,8},{3,9},{4,10},{5,11},{6,12},{7,13},{8,14},{9,15},... | collective-permute-start | bytes 36872
  626.5 21.4 %collective-permute-start.7 = (f32[192,16]{0,1:T(8,128)S(1)}, f32[192,16]{0,1:T(8,128)S(1)}, u32[]{:S(2)}, u32[]{:S(2)}) collective-permute-start(f32[192,16]{0,1:T(8,128)S(1)} %get-tuple-element.567), channel_id=1, source_target_pairs={{0,7},{1,8},{2,9},{3,10},{4,11},{5,12},{6,13},{7,14},{8,15},{9,16}... | collective-permute-start | bytes 36872
  631.6 16.3 %collective-permute-start.8 = (f32[192,16]{0,1:T(8,128)S(1)}, f32[192,16]{0,1:T(8,128)S(1)}, u32[]{:S(2)}, u32[]{:S(2)}) collective-permute-start(f32[192,16]{0,1:T(8,128)S(1)} %get-tuple-element.567), channel_id=1, source_target_pairs={{0,8},{1,9},{2,10},{3,11},{4,12},{5,13},{6,14},{7,15},{8,16},{9,17... | collective-permute-start | bytes 36872
  644.7 4.0 collective-permute-start.9
Sparse Core Ops, SparseCore 0:
  11.2 74.2 all-gather.1
  295.2 232.3 reduce-scatter.8
  531.0 222.6 reduce-scatter.6
where the time goes:
time: 763 us; the launch traced here: 760 us
  blocking collectives  262 us (34%)
  waiting for transfers between devices  216 us (28%)
  starting transfers between devices  153 us (20%)
  other arithmetic  75.8 us (10%)
  matrix products  19.2 us (3%)
  local copies, waits for them, and re-layouts  18.4 us (2%)
  between operations  15.7 us (2%)
    unnamed x2, blocking collectives  222 us
    unnamed x32, starting transfers between devices  123 us
    reduce_scatter x1, waiting for transfers between devices, body(): lax.psum_scatter(finished[1], 'dp', scatter_dimension=0, tiled=True)  103 us
    ppermute x11, waiting for transfers between devices, from_behind(): return lax.ppermute(block, axis, route)  75.9 us
    psum x1, blocking collectives, from_root(): return lax.psum(jnp.where(mine, array, jnp.zeros_like(array)), axis)  40.3 us
    all_gather x1, waiting for transfers between devices, critic_pass(): full_first = lax.all_gather(critic_first, 'section', axis=0, tiled=True)  33.8 us
    ppermute x11, starting transfers between devices, from_behind(): return lax.ppermute(block, axis, route)  29.7 us
    add x11, other arithmetic, advance(): up_sum + grad_up  29.6 us
  transfers between devices with their start and end apart: 46, of which 15 were waited for; matrix products, arithmetic and copies ran while one was open for 24% of the time, Pallas kernels for 0%

commit v1 on v0

v1 whole, which is shorter than its diff:
```python
import functools

import jax
import jax.numpy as jnp
from jax import lax
from jax.experimental import pallas as pl
from jax.experimental.pallas import tpu as pltpu
from jax.sharding import Mesh, PartitionSpec as P


EPSILON = 1e-06
REVERSAL = 0.5
SECTIONS = 8
CHUNK = 64
DELAY = 2
SEC = ("x", "yh")
F32 = jnp.float32
BF16 = jnp.bfloat16
VM = pl.BlockSpec(memory_space=pltpu.VMEM)
SM = pl.BlockSpec(memory_space=pltpu.SMEM)


def silu_slope(pre_act):
    sigma = jax.nn.sigmoid(pre_act)
    return sigma * (1.0 + pre_act * (1.0 - sigma))


def call(kernel, out_shape, in_specs, args, flops, moved, aliases=None, scratch=(), limit=24):
    return pl.pallas_call(
        kernel,
        out_shape=out_shape,
        in_specs=in_specs,
        out_specs=jax.tree.map(lambda _: VM, out_shape),
        input_output_aliases=aliases or {},
        scratch_shapes=scratch,
        compiler_params=pltpu.CompilerParams(vmem_limit_bytes=limit << 20),
        cost_estimate=pl.CostEstimate(flops=flops, bytes_accessed=moved, transcendentals=0),
    )(*args)


def prepare_kernel(
    lens_ref, core_ref, _labels, x_ref, gain_ref, wd_ref, wu_ref, first_ref, low_ref, xn_ref, h_ref, a_ref, q_ref, pooled_ref, wut_ref, wdt_ref, mine_ref, second_ref, _g, _da
):
    micros, seq_len = 4, 128
    gain = gain_ref[0:1, :]
    half = first_ref.shape[1] // 2
    for c in range(2):

        @pl.when(core_ref[0] == c)
        def _():
            mine_ref[...] = first_ref[:, c * half : (c + 1) * half]

    second_ref[...] = low_ref[...]
    wut_ref[...] = wu_ref[...].T
    wdt_ref[...] = wd_ref[...].T
    pooled_ref[...] = jnp.zeros_like(pooled_ref)
    positions = lax.broadcasted_iota(jnp.int32, (seq_len, 1), 0)
    for m in range(micros):
        rows = pl.ds(m * seq_len, seq_len)
        values = x_ref[rows, :].astype(F32)
        count = lens_ref[m, 0]
        total = jnp.sum(jnp.where(positions < count, values, 0.0), axis=0, keepdims=True)
        pooled_ref[m : m + 1, :] = total / count.astype(F32)
        q = lax.rsqrt(jnp.mean(values * values, axis=-1, keepdims=True) + EPSILON)
        normed = (values * q * gain).astype(BF16)
        xn_ref[rows, :] = normed
        a = jnp.dot(normed, wd_ref[...], preferred_element_type=F32)
        a_ref[rows, :] = a
        h_ref[rows, :] = (a * jax.nn.sigmoid(a)).astype(BF16)
        q_ref[rows, :] = jnp.broadcast_to(q, (seq_len, 128))


def step_kernel(step, chunks, has_top, has_in, has_rev, *refs):
    refs = list(refs)
    sec_ref, lens_ref, x_ref, a_ref, q_ref, gain_ref, wut_ref, wdt_ref = refs[:8]
    refs = refs[8:]
    top_ref = refs.pop(0) if has_top else None
    in_ref = refs.pop(0) if has_in else None
    rev_ref = refs.pop(0) if has_rev else None
    _, _, out_ref, g_ref, da_ref = refs
    features = x_ref.shape[1]
    sec = sec_ref[0]
    place = step - DELAY * (SECTIONS - 1 - sec)
    live = (place >= 0) & (place < chunks)
    place = jnp.clip(place, 0, chunks - 1)
    rows = pl.ds(pl.multiple_of(place * CHUNK, CHUNK), CHUNK)

    if has_top:

        @pl.when(live & (sec == SECTIONS - 1))
        def _():
            g_ref[rows, :] = top_ref[rows, :]

    if has_in:

        @pl.when(live & (sec < SECTIONS - 1))
        def _():
            g_ref[rows, :] = in_ref[...]

    if has_rev:

        @pl.when(live & (sec == SECTIONS // 2 - 1))
        def _():
            per = 128 // CHUNK
            micro = lax.div(place, per)
            first = lax.rem(place, per) * CHUNK
            positions = lax.broadcasted_iota(jnp.int32, (CHUNK, 1), 0) + first
            extra = jnp.where(positions < lens_ref[micro, 0], rev_ref[pl.ds(micro, 1), :], 0.0)
            g_ref[rows, :] = (in_ref[...].astype(F32) + extra).astype(BF16)

    @pl.when(live)
    def _():
        g = g_ref[rows, :]
        a = a_ref[rows, :]
        q = q_ref[rows, 0:1]
        dh = jnp.dot(g, wut_ref[...], preferred_element_type=F32)
        da = (dh * silu_slope(a)).astype(BF16)
        da_ref[rows, :] = da
        mean = jnp.sum(da.astype(F32) * a, axis=-1, keepdims=True) * (1.0 / features)
        dxn = jnp.dot(da, wdt_ref[...], preferred_element_type=F32)
        x = x_ref[rows, :].astype(F32)
        out = g.astype(F32) + q * (dxn * gain_ref[0:1, :]) - x * (q * q * mean)
        out_ref[...] = out.astype(BF16)


def per_row(ref, shape):
    rows = lax.broadcasted_iota(jnp.int32, shape, 0)
    column = jnp.ones(shape, jnp.int32)
    for m in range(4):
        column = jnp.where(rows == m, ref[m, 0], column)
    return column


def critic_kernel(
    sec_ref, core_ref, labels_ref, lens_ref, pooled_ref, own_ref, other_ref, second_ref, lines_ref, rev_ref, hold
):
    half = own_ref.shape[1]
    channels = 2 * half
    languages = second_ref.shape[1]

    @pl.when(sec_ref[0] == SECTIONS // 2 - 1)
    def _():
        pooled = pooled_ref[...].astype(BF16).astype(F32)
        r = lax.rsqrt(jnp.mean(pooled * pooled, axis=-1, keepdims=True) + EPSILON)
        unit = pooled * r
        normed = unit.astype(BF16)
        core = core_ref[0]
        pre_own = jnp.dot(normed, own_ref[...], preferred_element_type=F32)
        pre_other = jnp.dot(normed, other_ref[...], preferred_element_type=F32)
        low = jnp.where(core == 0, pre_own, pre_other)
        high = jnp.where(core == 0, pre_other, pre_own)
        pre = jnp.concatenate([low, high], axis=1)
        hidden = (pre * jax.nn.sigmoid(pre)).astype(BF16)
        second = second_ref[...]
        logits = jnp.dot(hidden, second, preferred_element_type=F32)
        exponent = jnp.exp(logits)
        probs = exponent / jnp.sum(exponent, axis=-1, keepdims=True)
        lanes = lax.broadcasted_iota(jnp.int32, logits.shape, 1)
        onehot = jnp.where(lanes == per_row(labels_ref, logits.shape), 1.0, 0.0)
        valid = lax.broadcasted_iota(jnp.int32, logits.shape, 0) < 4
        grad_logits = jnp.where(valid, probs - onehot, 0.0).astype(BF16)
        dims = (((1,), (1,)), ((), ()))
        grad_hidden = lax.dot_general(grad_logits, second, dims, preferred_element_type=F32)
        grad_pre = (grad_hidden * silu_slope(pre)).astype(BF16)
        hold[...] = jnp.zeros_like(hold)
        hold[0:8, :] = normed.astype(F32)
        hold[8:16, 0:channels] = grad_pre.astype(F32)
        hold[8:16, channels:] = hidden.astype(F32)
        hold[16:24, 0:languages] = grad_logits.astype(F32)
        lines_ref[...] = hold[...].astype(BF16)
        low = grad_pre[:, :half]
        high = grad_pre[:, half:]
        mine = jnp.where(core == 0, low, high)
        theirs = jnp.where(core == 0, high, low)
        grad_normed = lax.dot_general(mine, own_ref[...], dims, preferred_element_type=F32)
        grad_normed += lax.dot_general(theirs, other_ref[...], dims, preferred_element_type=F32)
        mean = jnp.mean(grad_normed * unit, axis=-1, keepdims=True)
        grad_pooled = r * (grad_normed - unit * mean)
        rev_ref[...] = -REVERSAL * grad_pooled / per_row(lens_ref, (8, 1)).astype(F32)


def unpack_kernel(sec_ref, band_rows, n_dp, lines_ref, nb_ref, gp_ref, hid_ref, gl_ref):
    features = lines_ref.shape[1]
    channels = features // 2
    padded = gp_ref.shape[1] // n_dp
    share = channels // n_dp

    def grow(block):
        return jnp.concatenate([block, jnp.zeros_like(block)], axis=0).astype(BF16)

    def pick(shape, test):
        rows = lax.broadcasted_iota(jnp.int32, shape, 0)
        columns = lax.broadcasted_iota(jnp.int32, shape, 1)
        return jnp.where(test(rows, columns), 1.0, 0.0).astype(BF16)

    lines = lines_ref[...].astype(F32)
    base = sec_ref[0] * band_rows
    band = pick((features, 256), lambda i, j: (i == j + base) & (j < band_rows))
    nb_ref[...] = jnp.dot(grow(lines[0:8]), band, preferred_element_type=F32).astype(BF16)
    wide = (channels, n_dp * padded)
    columns = lax.broadcasted_iota(jnp.int32, (1, wide[1]), 1)
    slot = lax.div(columns, padded)
    inside = columns - slot * padded
    source = jnp.where(inside < share, slot * share + inside, -1)
    spread = jnp.where(lax.broadcasted_iota(jnp.int32, wide, 0) == source, 1.0, 0.0).astype(BF16)
    both = grow(lines[8:16])
    gp_ref[...] = jnp.dot(both[:, :channels], spread, preferred_element_type=F32).astype(BF16)
    hid_ref[...] = jnp.dot(both[:, channels:], spread, preferred_element_type=F32).astype(BF16)
    shift = pick((128, 128), lambda i, j: j == i + 64)
    gl_ref[...] = jnp.dot(grow(lines[16:24, :128]), shift, preferred_element_type=F32).astype(BF16)


def finish_kernel(parts, place_ref, xn_ref, g_ref, h_ref, da_ref, nb_ref, gl_ref, gp_ref, hid_ref, *refs):
    outs, (down, up, crit) = refs[:-3], refs[-3:]
    n_yl, n_z, n_c = parts
    features = xn_ref.shape[1]
    dims = (((0,), (0,)), ((), ()))
    width = 256
    for k in range(features // width):
        cols = pl.ds(k * width, width)
        down[cols, :] = lax.dot_general(xn_ref[:, cols], da_ref[...], dims, preferred_element_type=F32)
        up[cols, :] = lax.dot_general(g_ref[:, cols], h_ref[...], dims, preferred_element_type=F32)
    crit[:, :128] = lax.dot_general(gp_ref[...], nb_ref[:, :128], dims, preferred_element_type=F32)
    crit[:, 128:] = lax.dot_general(
        gp_ref[...], nb_ref[:, 128:], dims, preferred_element_type=F32
    ) + lax.dot_general(hid_ref[...], gl_ref[...], dims, preferred_element_type=F32)
    span = features // (n_yl * n_z * n_c)
    cspan = crit.shape[0] // (n_yl * n_z * n_c)
    my_yl, my_c = place_ref[0], place_ref[1]

    def pack(z, _):
        for dy in range(n_yl):
            for dc in range(n_c):
                yl = my_yl if dy == 0 else n_yl - 1 - my_yl
                c = my_c if dc == 0 else n_c - 1 - my_c
                dest = (yl * n_z + z) * n_c + c
                wide = pl.ds(pl.multiple_of(dest * span, 8), span)
                thin = pl.ds(pl.multiple_of(dest * cspan, 8), cspan)
                piece = jnp.concatenate([down[wide, :], up[wide, :], crit[thin, :]], axis=0)
                outs[dc * n_yl + dy][z] = piece.astype(BF16)
        return 0

    lax.fori_loop(0, n_z, pack, 0)


def join_kernel(sec_ref, *refs):
    *parts, out_ref = refs
    rows = parts[0].shape[0]

    @pl.when(sec_ref[0] % 2 == 1)
    def _():
        for i, ref in enumerate(parts):
            out_ref[i * rows : (i + 1) * rows, :] = ref[...]


def after(value, token):
    return lax.optimization_barrier((value, token))[0]


def swap(block, axis, size):
    return lax.ppermute(block, axis, [(i, size - 1 - i) for i in range(size)])


def body(parts, *args):
    return whole(parts, *args)


def whole(parts, section_in, top_grad, seq_lengths, lang_labels, norm_gain, w_down, w_up, critic_first, critic_second):
    n_yl, n_z, n_c = parts
    n_dp = n_yl * n_z * n_c
    sec = lax.axis_index(SEC)
    core = lax.axis_index("c")
    micros, seq_len, features = 4, 128, section_in.shape[-1]
    rank = w_down.shape[-1]
    rows = micros * seq_len
    chunks = rows // CHUNK
    x = section_in.reshape(rows, features)
    top = top_grad.reshape(rows, features)
    gain = norm_gain.reshape(1, features)
    wd = w_down[0]
    sec_s = sec.reshape(1).astype(jnp.int32)
    core_s = core.reshape(1).astype(jnp.int32)
    channels = critic_first.shape[1]
    half = channels // 2
    sds = jax.ShapeDtypeStruct

    xn, h, a, q, pooled, wut, wdt, mine, second, grads, inner = call(
        prepare_kernel,
        (
            sds((rows, features), BF16),
            sds((rows, rank), BF16),
            sds((rows, rank), F32),
            sds((rows, 128), F32),
            sds((8, features), F32),
            sds((features, rank), BF16),
            sds((rank, features), BF16),
            sds((critic_first.shape[0], half), BF16),
            sds(critic_second.shape, BF16),
            sds((rows, features), BF16),
            sds((rows, rank), BF16),
        ),
        [SM] * 3 + [VM] * 6,
        (seq_lengths, core_s, lang_labels, x, gain, wd, w_up[0], critic_first, critic_second),
        2 * rows * features * rank,
        8 << 20,
        limit=10,
    )

    three = SECTIONS // 2 - 1
    held = {}
    band_rows = critic_first.shape[0]
    share = channels // n_dp
    padded = -(-share // 16) * 16

    def join(token, *pieces):
        return call(
            join_kernel,
            sds((len(pieces) * pieces[0].shape[0], half), BF16),
            [SM] + [VM] * len(pieces),
            (after(sec_s, token), *pieces),
            0,
            2 << 20,
            limit=4,
        )

    def side_work(step, token):
        if step == 0:
            held["even"] = lax.ppermute(after(mine, token), SEC, [(i, i + 1) for i in range(0, SECTIONS, 2)])
        elif step == 1:
            held["pooled"] = lax.ppermute(after(pooled, token), SEC, [(4, three)])
        elif step == 2:
            held["pair"] = join(token, held["even"], mine)
            held["far"] = [lax.ppermute(held["pair"], SEC, [(i, three)]) for i in (1, 5, 7)]
        elif step == 5:
            held["own"] = join(token, held["far"][0], held["pair"], *held["far"][1:])
            pairs = [(three * 2, three * 2 + 1), (three * 2 + 1, three * 2)]
            held["other"] = lax.ppermute(held["own"], SEC + ("c",), pairs)
        elif step == 7:
            held["lines"], held["rev"] = call(
                critic_kernel,
                (sds((32, features), BF16), sds((8, features), F32)),
                [SM] * 4 + [VM] * 4,
                (
                    after(sec_s, token),
                    core_s,
                    lang_labels,
                    seq_lengths,
                    held["pooled"],
                    held["own"],
                    held["other"],
                    second,
                ),
                1 << 27,
                4 << 20,
                scratch=[pltpu.VMEM((32, features), F32)],
                limit=8,
            )
        elif step in (9, 12, 15):
            lines = after(held["lines"], token)
            if step == 9:
                moved = lax.ppermute(lines, SEC, [(3, 7)])
                gets = sec == 7
            elif step == 12:
                moved = lax.ppermute(lines, SEC, [(3, 1), (7, 5)])
                gets = (sec == 1) | (sec == 5)
            else:
                moved = lax.ppermute(lines, SEC, [(i + 1, i) for i in range(0, SECTIONS, 2)])
                gets = sec % 2 == 0
            held["lines"] = jnp.where(gets, moved, lines)
        elif step == 18:
            held["critic"] = call(
                lambda sec_ref, *refs: unpack_kernel(sec_ref, band_rows, n_dp, *refs),
                (
                    sds((16, 256), BF16),
                    sds((16, n_dp * padded), BF16),
                    sds((16, n_dp * padded), BF16),
                    sds((16, 128), BF16),
                ),
                [SM, VM],
                (after(sec_s, token), held["lines"]),
                1 << 26,
                1 << 20,
                limit=12,
            )

    steps = DELAY * (SECTIONS - 1) + chunks
    received = {}
    route = [(i, i - 1) for i in range(1, SECTIONS)]
    for step in range(steps):
        has_top = step < chunks
        has_in = step >= DELAY
        first_rev = DELAY * (SECTIONS - 1 - three)
        has_rev = first_rev <= step < first_rev + chunks
        args = [sec_s, seq_lengths, x, a, q, gain, wut, wdt]
        specs = [SM, SM] + [VM] * 6
        if has_top:
            args.append(top)
        if has_in:
            args.append(received.pop(step - DELAY))
        if has_rev:
            args.append(held["rev"])
        args += [grads, inner]
        specs += [VM] * (len(args) - len(specs))
        outgoing, grads, inner = call(
            functools.partial(step_kernel, step, chunks, has_top, has_in, has_rev),
            (sds((CHUNK, features), BF16), sds((rows, features), BF16), sds((rows, rank), BF16)),
            specs,
            tuple(args),
            4 * CHUNK * features * rank,
            3 << 20,
            aliases={len(args) - 2: 1, len(args) - 1: 2},
            limit=6,
        )
        if step < steps - DELAY:
            received[step] = lax.ppermute(outgoing, SEC, route)
        side_work(step, outgoing)

    band, gp, hid, gl = held["critic"]
    span = features // n_dp
    piece = sds((n_z, 2 * span + padded, rank), BF16)
    place = jnp.stack([lax.axis_index("yl"), core]).astype(jnp.int32)
    packed = call(
        functools.partial(finish_kernel, parts),
        (piece,) * (n_yl * n_c),
        [SM] + [VM] * 8,
        (place, xn, grads, h, inner, band, gl, gp, hid),
        4 * rows * features * rank,
        8 << 20,
        scratch=[pltpu.VMEM((features, rank), F32)] * 2 + [pltpu.VMEM((n_dp * padded, rank), F32)],
        limit=16,
    )

    def add(left, right):
        return (left.astype(F32) + right.astype(F32)).astype(BF16)

    kept, sent = packed[:n_yl], packed[n_yl:]
    halves = [None] * n_yl
    for i in reversed(range(n_yl)):
        halves[i] = add(kept[i], swap(sent[i], "c", n_c))
    summed = halves[0]
    if n_yl == 2:
        summed = add(summed, swap(halves[1], "yl", n_yl))
    if n_z > 1:
        summed = lax.all_to_all(summed, "z", 0, 0, tiled=True)
    total = jnp.sum(summed.astype(F32), axis=0)
    down = total[:span]
    up = total[span : 2 * span].T
    crit = total[2 * span : 2 * span + share]
    dp_place = lax.axis_index(("yl", "z", "c"))
    wd_own = lax.dynamic_slice_in_dim(wd, dp_place * span, span, 0).astype(F32)
    gain_own = lax.dynamic_slice_in_dim(gain[0], dp_place * span, span, 0)
    grad_gain = jnp.sum(down * wd_own, axis=1) / gain_own
    first = crit[:, :band_rows].T
    second_grad = crit[:, 192 : 192 + critic_second.shape[1]]
    return (down[None], up[None], grad_gain[None], first, second_grad)


def solution(mesh):
    n_dp = mesh.shape["dp"]
    parts = (2, n_dp // 4, 2) if n_dp >= 8 else (1, n_dp // 2, 2)
    fine = Mesh(mesh.devices.reshape((SECTIONS // 2, 2) + parts), SEC + ("yl", "z", "c"))
    dp = ("yl", "z", "c")
    return jax.shard_map(
        functools.partial(body, parts),
        mesh=fine,
        in_specs=(
            P(SEC, None, dp, None, None),
            P(None, dp, None, None),
            P(None, dp),
            P(None, dp),
            P(SEC, None),
            P(SEC, None, None),
            P(SEC, None, None),
            P(SEC, None),
            P(),
        ),
        out_specs=(P(SEC, dp, None), P(SEC, None, dp), P(SEC, dp), P(SEC, dp), P(dp, None)),
        check_vma=False,
    )
```

time: 763 us -> 257 us (0.34)
  the two profiles are of different devices: /device:TPU:16 before, /device:TPU:6 now
where the time goes in v1:
time: 257 us; the launch traced here: 256 us
  starting transfers between devices  135 us (53%)
  waiting for transfers between devices  62.7 us (24%)
  Pallas kernels  30.6 us (12%)
  local copies, waits for them, and re-layouts  19.9 us (8%)
  other arithmetic  5.88 us (2%)
    ppermute x20, starting transfers between devices, whole(): received[step] = lax.ppermute(outgoing, SEC, route)  104 us
    pallas_call x28, Pallas kernels, call(): pl.pallas_call(kernel, out_shape=out_shape, in_specs=in_specs, out_specs=...  30.6 us
    all_to_all x1, waiting for transfers between devices, whole(): summed = lax.all_to_all(summed, 'z', 0, 0, tiled=True)  28.2 us
    ppermute x20, waiting for transfers between devices, whole(): received[step] = lax.ppermute(outgoing, SEC, route)  21.3 us
    unnamed x61, local copies, waits for them, and re-layouts  18.7 us
    all_to_all x1, starting transfers between devices, whole(): summed = lax.all_to_all(summed, 'z', 0, 0, tiled=True)  15.2 us
    ppermute x3, waiting for transfers between devices, swap(): return lax.ppermute(block, axis, [(i, size - 1 - i) for i in range(size)])  13.1 us
    ppermute x3, starting transfers between devices, swap(): return lax.ppermute(block, axis, [(i, size - 1 - i) for i in range(size)])  6.9 us
  transfers between devices with their start and end apart: 33, of which 10 were waited for; matrix products, arithmetic and copies ran while one was open for 1% of the time, Pallas kernels for 10%

profile of v1, /device:TPU:6, one launch (start us, length us, event | category | flops | bytes accessed | tf_op | source)
XLA Modules:
  0.0 255.6 jit_solution(5915483098348647722)
XLA Ops:
  2.1 1.7 copy.60.low_ref
  3.8 1.4 copy-done
  5.9 1.1 copy-done.23
  7.0 1.1 copy-done.24
  10.0 2.1 shard_map.128
  13.4 5.4 %collective-permute-start.1 = (bf16[64,1536]{1,0:T(8,128)(2,1)S(1)}, bf16[64,1536]{1,0:T(8,128)(2,1)S(1)}, u32[]{:S(2)}, u32[]{:S(2)}) collective-permute-start(bf16[64,1536]{1,0:T(8,128)(2,1)S(1)} %get-tuple-element.109), channel_id=1, source_target_pairs={{64,0},{128,64},{192,128},{256,192},{320,256},{384,320},{448,384},... | collective-permute-start | bytes 589832 | tf_op jit(solution)/shard_map/ppermute | solution.py:415
  18.7 2.0 collective-permute-start.8
  21.3 1.9 collective-permute-start
  23.4 1.3 shard_map.131
  26.7 14.8 %collective-permute-start.3 = (bf16[64,1536]{1,0:T(8,128)(2,1)S(1)}, bf16[64,1536]{1,0:T(8,128)(2,1)S(1)}, u32[]{:S(2)}, u32[]{:S(2)}) collective-permute-start(bf16[64,1536]{1,0:T(8,128)(2,1)S(1)} %get-tuple-element.115), channel_id=1, source_target_pairs={{64,0},{128,64},{192,128},{256,192},{320,256},{384,320},{448,384},... | collective-permute-start | bytes 589832 | tf_op jit(solution)/shard_map/ppermute | solution.py:415
  41.5 1.3 shard_map.132
  42.8 1.9 collective-permute-start.2
  44.7 1.8 collective-permute-done.3.refs_9_
  46.6 1.3 shard_map.133
  47.8 4.6 %collective-permute-done.2.refs_9_ = bf16[64,1536]{1,0:T(8,128)(2,1)S(1)} collective-permute-done((bf16[64,1536]{1,0:T(8,128)(2,1)S(1)}, bf16[64,1536]{1,0:T(8,128)(2,1)S(1)}, u32[]{:S(2)}, u32[]{:S(2)}) %collective-permute-start.2) | collective-permute-done | bytes 196640 | tf_op jit(solution)/shard_map/ppermute | solution.py:415
  52.5 1.3 shard_map.134
  54.5 4.2 %collective-permute-start.5 = (bf16[64,1536]{1,0:T(8,128)(2,1)S(1)}, bf16[64,1536]{1,0:T(8,128)(2,1)S(1)}, u32[]{:S(2)}, u32[]{:S(2)}) collective-permute-start(bf16[64,1536]{1,0:T(8,128)(2,1)S(1)} %get-tuple-element.121), channel_id=1, source_target_pairs={{64,0},{128,64},{192,128},{256,192},{320,256},{384,320},{448,384},... | collective-permute-start | bytes 589832 | tf_op jit(solution)/shard_map/ppermute | solution.py:415
  58.7 1.9 collective-permute-start.4
  60.7 3.3 %collective-permute-done.5.refs_9_ = bf16[64,1536]{1,0:T(8,128)(2,1)S(1)} collective-permute-done((bf16[64,1536]{1,0:T(8,128)(2,1)S(1)}, bf16[64,1536]{1,0:T(8,128)(2,1)S(1)}, u32[]{:S(2)}, u32[]{:S(2)}) %collective-permute-start.5) | collective-permute-done | bytes 196640 | tf_op jit(solution)/shard_map/ppermute | solution.py:415
  64.0 1.3 shard_map.135
  65.3 6.8 %collective-permute-start.13 = (bf16[64,1536]{1,0:T(8,128)(2,1)S(1)}, bf16[64,1536]{1,0:T(8,128)(2,1)S(1)}, u32[]{:S(2)}, u32[]{:S(2)}) collective-permute-start(bf16[64,1536]{1,0:T(8,128)(2,1)S(1)} %get-tuple-element.136), channel_id=1, source_target_pairs={{64,0},{128,64},{192,128},{256,192},{320,256},{384,320},{448,384},... | collective-permute-start | bytes 589832 | tf_op jit(solution)/shard_map/ppermute | solution.py:415
  72.1 1.3 shard_map.136
  73.3 1.9 collective-permute-start.6
  76.0 1.3 shard_map.139
  77.3 1.3 shard_map.140
  78.6 6.8 %collective-permute-start.15 = (bf16[64,1536]{1,0:T(8,128)(2,1)S(1)}, bf16[64,1536]{1,0:T(8,128)(2,1)S(1)}, u32[]{:S(2)}, u32[]{:S(2)}) collective-permute-start(bf16[64,1536]{1,0:T(8,128)(2,1)S(1)} %get-tuple-element.142), channel_id=1, source_target_pairs={{64,0},{128,64},{192,128},{256,192},{320,256},{384,320},{448,384},... | collective-permute-start | bytes 589832 | tf_op jit(solution)/shard_map/ppermute | solution.py:415
  85.4 1.3 shard_map.141
  86.7 6.4 %collective-permute-start.14 = (bf16[64,1536]{1,0:T(8,128)(2,1)S(1)}, bf16[64,1536]{1,0:T(8,128)(2,1)S(1)}, u32[]{:S(2)}, u32[]{:S(2)}) collective-permute-start(bf16[64,1536]{1,0:T(8,128)(2,1)S(1)} %get-tuple-element.141), channel_id=1, source_target_pairs={{64,0},{128,64},{192,128},{256,192},{320,256},{384,320},{448,384},... | collective-permute-start | bytes 589832 | tf_op jit(solution)/shard_map/ppermute | solution.py:415
  93.7 9.0 %collective-permute-start.17 = (bf16[64,1536]{1,0:T(8,128)(2,1)S(1)}, bf16[64,1536]{1,0:T(8,128)(2,1)S(1)}, u32[]{:S(2)}, u32[]{:S(2)}) collective-permute-start(bf16[64,1536]{1,0:T(8,128)(2,1)S(1)} %get-tuple-element.148), channel_id=1, source_target_pairs={{64,0},{128,64},{192,128},{256,192},{320,256},{384,320},{448,384},... | collective-permute-start | bytes 589832 | tf_op jit(solution)/shard_map/ppermute | solution.py:415
  103.3 4.3 %collective-permute-start.16 = (bf16[64,1536]{1,0:T(8,128)(2,1)S(1)}, bf16[64,1536]{1,0:T(8,128)(2,1)S(1)}, u32[]{:S(2)}, u32[]{:S(2)}) collective-permute-start(bf16[64,1536]{1,0:T(8,128)(2,1)S(1)} %get-tuple-element.147), channel_id=1, source_target_pairs={{64,0},{128,64},{192,128},{256,192},{320,256},{384,320},{448,384},... | collective-permute-start | bytes 589832 | tf_op jit(solution)/shard_map/ppermute | solution.py:415
  107.6 1.3 shard_map.144
  108.9 6.8 %collective-permute-start.19 = (bf16[64,1536]{1,0:T(8,128)(2,1)}, bf16[64,1536]{1,0:T(8,128)(2,1)}, u32[]{:S(2)}, u32[]{:S(2)}) collective-permute-start(bf16[64,1536]{1,0:T(8,128)(2,1)} %get-tuple-element.154), channel_id=1, source_target_pairs={{64,0},{128,64},{192,128},{256,192},{320,256},{384,320},{448,384},... | collective-permute-start | bytes 589832 | tf_op jit(solution)/shard_map/ppermute | solution.py:415
  115.8 1.3 shard_map.145
  117.0 3.4 %collective-permute-start.18 = (bf16[64,1536]{1,0:T(8,128)(2,1)}, bf16[64,1536]{1,0:T(8,128)(2,1)}, u32[]{:S(2)}, u32[]{:S(2)}) collective-permute-start(bf16[64,1536]{1,0:T(8,128)(2,1)} %get-tuple-element.153), channel_id=1, source_target_pairs={{64,0},{128,64},{192,128},{256,192},{320,256},{384,320},{448,384},... | collective-permute-start | bytes 589832 | tf_op jit(solution)/shard_map/ppermute | solution.py:415
  120.5 1.3 collective-permute-start.26
  121.8 1.1 copy-done.3
  122.9 1.1 copy-done.7
  126.0 1.6 shard_map.146
  127.7 1.8 shard_map.147
  129.5 7.5 %collective-permute-start.20 = (bf16[64,1536]{1,0:T(8,128)(2,1)}, bf16[64,1536]{1,0:T(8,128)(2,1)}, u32[]{:S(2)}, u32[]{:S(2)}) collective-permute-start(bf16[64,1536]{1,0:T(8,128)(2,1)} %get-tuple-element.159), channel_id=1, source_target_pairs={{64,0},{128,64},{192,128},{256,192},{320,256},{384,320},{448,384},... | collective-permute-start | bytes 589832 | tf_op jit(solution)/shard_map/ppermute | solution.py:415
  137.0 2.2 collective-permute-start.21
  139.2 1.6 broadcast_select_fusion
  140.7 1.3 collective-permute-start.27
  142.0 4.4 %collective-permute-done.21.refs_8_ = bf16[64,1536]{1,0:T(8,128)(2,1)} collective-permute-done((bf16[64,1536]{1,0:T(8,128)(2,1)}, bf16[64,1536]{1,0:T(8,128)(2,1)}, u32[]{:S(2)}, u32[]{:S(2)}) %collective-permute-start.21) | collective-permute-done | bytes 196640 | tf_op jit(solution)/shard_map/ppermute | solution.py:415
  146.4 1.1 copy-done.4
  147.5 1.1 copy-done.8
  151.7 1.1 shard_map.149
  152.8 3.6 %collective-permute-start.22 = (bf16[64,1536]{1,0:T(8,128)(2,1)S(1)}, bf16[64,1536]{1,0:T(8,128)(2,1)S(1)}, u32[]{:S(2)}, u32[]{:S(2)}) collective-permute-start(bf16[64,1536]{1,0:T(8,128)(2,1)S(1)} %get-tuple-element.165), channel_id=1, source_target_pairs={{64,0},{128,64},{192,128},{256,192},{320,256},{384,320},{448,384},... | collective-permute-start | bytes 589832 | tf_op jit(solution)/shard_map/ppermute | solution.py:415
  156.4 5.9 %collective-permute-start.23 = (bf16[64,1536]{1,0:T(8,128)(2,1)S(1)}, bf16[64,1536]{1,0:T(8,128)(2,1)S(1)}, u32[]{:S(2)}, u32[]{:S(2)}) collective-permute-start(bf16[64,1536]{1,0:T(8,128)(2,1)S(1)} %get-tuple-element.166), channel_id=1, source_target_pairs={{64,0},{128,64},{192,128},{256,192},{320,256},{384,320},{448,384},... | collective-permute-start | bytes 589832 | tf_op jit(solution)/shard_map/ppermute | solution.py:415
  163.2 1.3 collective-permute-start.28
  164.6 1.6 collective-permute-done.23.refs_8_
  167.4 6.2 %collective-permute-start.24 = (bf16[64,1536]{1,0:T(8,128)(2,1)S(1)}, bf16[64,1536]{1,0:T(8,128)(2,1)S(1)}, u32[]{:S(2)}, u32[]{:S(2)}) collective-permute-start(bf16[64,1536]{1,0:T(8,128)(2,1)S(1)} %get-tuple-element.171), channel_id=1, source_target_pairs={{64,0},{128,64},{192,128},{256,192},{320,256},{384,320},{448,384},... | collective-permute-start | bytes 589832 | tf_op jit(solution)/shard_map/ppermute | solution.py:415
  173.6 2.9 %collective-permute-start.25 = (bf16[64,1536]{1,0:T(8,128)(2,1)S(1)}, bf16[64,1536]{1,0:T(8,128)(2,1)S(1)}, u32[]{:S(2)}, u32[]{:S(2)}) collective-permute-start(bf16[64,1536]{1,0:T(8,128)(2,1)S(1)} %get-tuple-element.172), channel_id=1, source_target_pairs={{64,0},{128,64},{192,128},{256,192},{320,256},{384,320},{448,384},... | collective-permute-start | bytes 589832 | tf_op jit(solution)/shard_map/ppermute | solution.py:415
  177.5 5.2 %collective-permute-done.25.refs_8_ = bf16[64,1536]{1,0:T(8,128)(2,1)S(1)} collective-permute-done((bf16[64,1536]{1,0:T(8,128)(2,1)S(1)}, bf16[64,1536]{1,0:T(8,128)(2,1)S(1)}, u32[]{:S(2)}, u32[]{:S(2)}) %collective-permute-start.25) | collective-permute-done | bytes 196640 | tf_op jit(solution)/shard_map/ppermute | solution.py:415
  182.7 1.3 shard_map.152
  184.0 1.3 shard_map.153
  185.4 2.1 shard_map.155
  187.5 1.9 collective-permute-start.30
  189.4 2.4 collective-permute-start.29
  192.0 2.6 %collective-permute-start.31 = (bf16[16,64,256]{2,1,0:T(8,128)(2,1)S(1)}, bf16[16,64,256]{2,1,0:T(8,128)(2,1)S(1)}, u32[]{:S(2)}, u32[]{:S(2)}) collective-permute-start(bf16[16,64,256]{2,1,0:T(8,128)(2,1)S(1)} %add_convert_fusion.1), channel_id=1, source_target_pairs={{0,32},{32,0},{1,33},{33,1},{2,34},{34,2},{3,35},{35,3},{4,36},{36... | collective-permute-start | bytes 1572872 | tf_op jit(solution)/shard_map/ppermute | solution.py:261
  194.6 13.1 %collective-permute-done.31 = bf16[16,64,256]{2,1,0:T(8,128)(2,1)S(1)} collective-permute-done((bf16[16,64,256]{2,1,0:T(8,128)(2,1)S(1)}, bf16[16,64,256]{2,1,0:T(8,128)(2,1)S(1)}, u32[]{:S(2)}, u32[]{:S(2)}) %collective-permute-start.31) | collective-permute-done | bytes 524320 | tf_op jit(solution)/shard_map/ppermute | solution.py:261
  208.8 15.2 %all-to-all-start = ((bf16[16,64,256]{2,1,0:T(8,128)(2,1)}), bf16[16,64,256]{2,1,0:T(8,128)(2,1)S(1)}, u32[]{:S(2)}, u32[]{:S(2)}) async-start(bf16[16,64,256]{2,1,0:T(8,128)(2,1)} %add_convert_fusion), calls=%async_computation | async-start | bytes 1048576 | tf_op jit(solution)/shard_map/all_to_all | solution.py:444
  224.0 28.2 %all-to-all-done = bf16[16,64,256]{2,1,0:T(8,128)(2,1)S(1)} async-done(((bf16[16,64,256]{2,1,0:T(8,128)(2,1)}), bf16[16,64,256]{2,1,0:T(8,128)(2,1)S(1)}, u32[]{:S(2)}, u32[]{:S(2)}) %all-to-all-start) | async-done | bytes 524320 | tf_op jit(solution)/shard_map/all_to_all | solution.py:444
  253.6 1.4 fusion
  (102 shorter events, 22.1 us)
Async XLA Ops:
  3.8 1.4 copy-start
  5.2 0.7 copy-start.19
  5.9 1.1 copy-start.23
  7.0 1.1 copy-start.24
  8.1 0.9 copy-start.25
  9.1 1.0 copy-start.26
  10.0 2.1 copy-start.1
  10.0 2.1 copy-start.18
  10.0 2.1 copy-start.20
  12.1 1.1 copy-start.21
  12.1 1.2 copy-start.27
  12.1 103.6 %copy-start.2 = (bf16[1536,256]{1,0:T(8,128)(2,1)}, bf16[1536,256]{1,0:T(8,128)(2,1)S(1)}, u32[]{:S(2)}) copy-start(bf16[1536,256]{1,0:T(8,128)(2,1)S(1)} %get-tuple-element.102.refs_6_) | copy-start | bytes 2359300
  12.1 103.6 %copy-start.6 = (bf16[256,1536]{1,0:T(8,128)(2,1)}, bf16[256,1536]{1,0:T(8,128)(2,1)S(1)}, u32[]{:S(2)}) copy-start(bf16[256,1536]{1,0:T(8,128)(2,1)S(1)} %get-tuple-element.103.refs_7_) | copy-start | bytes 2359300
  12.1 103.6 %copy-start.10 = (f32[512,256]{1,0:T(8,128)}, f32[512,256]{1,0:T(8,128)S(1)}, u32[]{:S(2)}) copy-start(f32[512,256]{1,0:T(8,128)S(1)} %get-tuple-element.100.refs_3_) | copy-start | bytes 1572868
  12.1 103.6 %copy-start.14 = (f32[512,128]{1,0:T(8,128)}, f32[512,128]{1,0:T(8,128)S(1)}, u32[]{:S(2)}) copy-start(f32[512,128]{1,0:T(8,128)S(1)} %get-tuple-element.101.refs_4_) | copy-start | bytes 786436
  13.4 10.0 %collective-permute-start.1 = (bf16[64,1536]{1,0:T(8,128)(2,1)S(1)}, bf16[64,1536]{1,0:T(8,128)(2,1)S(1)}, u32[]{:S(2)}, u32[]{:S(2)}) collective-permute-start(bf16[64,1536]{1,0:T(8,128)(2,1)S(1)} %get-tuple-element.109), channel_id=1, source_target_pairs={{64,0},{128,64},{192,128},{256,192},{320,256},{384,320},{448,384},... | collective-permute-start | bytes 589832 | tf_op jit(solution)/shard_map/ppermute | solution.py:415
  18.7 5.9 %collective-permute-start.8 = (bf16[192,384]{1,0:T(8,128)(2,1)S(1)}, bf16[192,384]{1,0:T(8,128)(2,1)S(1)}, u32[]{:S(2)}, u32[]{:S(2)}) collective-permute-start(bf16[192,384]{1,0:T(8,128)(2,1)S(1)} %get-tuple-element.133.refs_1_), channel_id=1, source_target_pairs={{0,64},{128,192},{256,320},{384,448},{1,65},{129,193},{257,321},{3... | collective-permute-start | bytes 442376 | tf_op jit(solution)/shard_map/ppermute | solution.py:328
  21.3 20.2 %collective-permute-start = (bf16[64,1536]{1,0:T(8,128)(2,1)S(1)}, bf16[64,1536]{1,0:T(8,128)(2,1)S(1)}, u32[]{:S(2)}, u32[]{:S(2)}) collective-permute-start(bf16[64,1536]{1,0:T(8,128)(2,1)S(1)} %get-tuple-element.108), channel_id=1, source_target_pairs={{64,0},{128,64},{192,128},{256,192},{320,256},{384,320},{448,384},... | collective-permute-start | bytes 589832 | tf_op jit(solution)/shard_map/ppermute | solution.py:415
  24.7 29.0 %collective-permute-start.11 = (bf16[384,384]{1,0:T(8,128)(2,1)S(1)}, bf16[384,384]{1,0:T(8,128)(2,1)S(1)}, u32[]{:S(2)}, u32[]{:S(2)}) collective-permute-start(bf16[384,384]{1,0:T(8,128)(2,1)S(1)} %shard_map.137.refs_1_), channel_id=1, source_target_pairs={{448,192},{449,193},{450,194},{451,195},{452,196},{453,197},{454,1... | collective-permute-start | bytes 884744 | tf_op jit(solution)/shard_map/ppermute | solution.py:333
  25.4 28.4 %collective-permute-start.10 = (bf16[384,384]{1,0:T(8,128)(2,1)S(1)}, bf16[384,384]{1,0:T(8,128)(2,1)S(1)}, u32[]{:S(2)}, u32[]{:S(2)}) collective-permute-start(bf16[384,384]{1,0:T(8,128)(2,1)S(1)} %shard_map.137.refs_1_), channel_id=1, source_target_pairs={{320,192},{321,193},{322,194},{323,195},{324,196},{325,197},{326,1... | collective-permute-start | bytes 884744 | tf_op jit(solution)/shard_map/ppermute | solution.py:333
  26.1 27.7 %collective-permute-start.9 = (bf16[384,384]{1,0:T(8,128)(2,1)S(1)}, bf16[384,384]{1,0:T(8,128)(2,1)S(1)}, u32[]{:S(2)}, u32[]{:S(2)}) collective-permute-start(bf16[384,384]{1,0:T(8,128)(2,1)S(1)} %shard_map.137.refs_1_), channel_id=1, source_target_pairs={{64,192},{65,193},{66,194},{67,195},{68,196},{69,197},{70,198},{71... | collective-permute-start | bytes 884744 | tf_op jit(solution)/shard_map/ppermute | solution.py:333
  26.7 19.8 %collective-permute-start.3 = (bf16[64,1536]{1,0:T(8,128)(2,1)S(1)}, bf16[64,1536]{1,0:T(8,128)(2,1)S(1)}, u32[]{:S(2)}, u32[]{:S(2)}) collective-permute-start(bf16[64,1536]{1,0:T(8,128)(2,1)S(1)} %get-tuple-element.115), channel_id=1, source_target_pairs={{64,0},{128,64},{192,128},{256,192},{320,256},{384,320},{448,384},... | collective-permute-start | bytes 589832 | tf_op jit(solution)/shard_map/ppermute | solution.py:415
  42.8 9.7 %collective-permute-start.2 = (bf16[64,1536]{1,0:T(8,128)(2,1)S(1)}, bf16[64,1536]{1,0:T(8,128)(2,1)S(1)}, u32[]{:S(2)}, u32[]{:S(2)}) collective-permute-start(bf16[64,1536]{1,0:T(8,128)(2,1)S(1)} %get-tuple-element.114), channel_id=1, source_target_pairs={{64,0},{128,64},{192,128},{256,192},{320,256},{384,320},{448,384},... | collective-permute-start | bytes 589832 | tf_op jit(solution)/shard_map/ppermute | solution.py:415
  53.8 22.2 %collective-permute-start.12 = (bf16[1536,384]{1,0:T(8,128)(2,1)S(1)}, bf16[1536,384]{1,0:T(8,128)(2,1)S(1)}, u32[]{:S(2)}, u32[]{:S(2)}) collective-permute-start(bf16[1536,384]{1,0:T(8,128)(2,1)S(1)} %shard_map.138.own_ref), channel_id=1, source_target_pairs={{192,193},{193,192},{194,195},{195,194},{196,197},{197,196},{198,1... | collective-permute-start | bytes 3538952 | tf_op jit(solution)/shard_map/ppermute | solution.py:337
  54.5 9.5 %collective-permute-start.5 = (bf16[64,1536]{1,0:T(8,128)(2,1)S(1)}, bf16[64,1536]{1,0:T(8,128)(2,1)S(1)}, u32[]{:S(2)}, u32[]{:S(2)}) collective-permute-start(bf16[64,1536]{1,0:T(8,128)(2,1)S(1)} %get-tuple-element.121), channel_id=1, source_target_pairs={{64,0},{128,64},{192,128},{256,192},{320,256},{384,320},{448,384},... | collective-permute-start | bytes 589832 | tf_op jit(solution)/shard_map/ppermute | solution.py:415
  58.7 13.3 %collective-permute-start.4 = (bf16[64,1536]{1,0:T(8,128)(2,1)S(1)}, bf16[64,1536]{1,0:T(8,128)(2,1)S(1)}, u32[]{:S(2)}, u32[]{:S(2)}) collective-permute-start(bf16[64,1536]{1,0:T(8,128)(2,1)S(1)} %get-tuple-element.120), channel_id=1, source_target_pairs={{64,0},{128,64},{192,128},{256,192},{320,256},{384,320},{448,384},... | collective-permute-start | bytes 589832 | tf_op jit(solution)/shard_map/ppermute | solution.py:415
  65.3 12.1 %collective-permute-start.13 = (bf16[64,1536]{1,0:T(8,128)(2,1)S(1)}, bf16[64,1536]{1,0:T(8,128)(2,1)S(1)}, u32[]{:S(2)}, u32[]{:S(2)}) collective-permute-start(bf16[64,1536]{1,0:T(8,128)(2,1)S(1)} %get-tuple-element.136), channel_id=1, source_target_pairs={{64,0},{128,64},{192,128},{256,192},{320,256},{384,320},{448,384},... | collective-permute-start | bytes 589832 | tf_op jit(solution)/shard_map/ppermute | solution.py:415
  73.3 12.0 %collective-permute-start.6 = (bf16[64,1536]{1,0:T(8,128)(2,1)S(1)}, bf16[64,1536]{1,0:T(8,128)(2,1)S(1)}, u32[]{:S(2)}, u32[]{:S(2)}) collective-permute-start(bf16[64,1536]{1,0:T(8,128)(2,1)S(1)} %get-tuple-element.126), channel_id=1, source_target_pairs={{64,0},{128,64},{192,128},{256,192},{320,256},{384,320},{448,384},... | collective-permute-start | bytes 589832 | tf_op jit(solution)/shard_map/ppermute | solution.py:415
  75.3 0.7 collective-permute-start.7
  78.6 14.5 %collective-permute-start.15 = (bf16[64,1536]{1,0:T(8,128)(2,1)S(1)}, bf16[64,1536]{1,0:T(8,128)(2,1)S(1)}, u32[]{:S(2)}, u32[]{:S(2)}) collective-permute-start(bf16[64,1536]{1,0:T(8,128)(2,1)S(1)} %get-tuple-element.142), channel_id=1, source_target_pairs={{64,0},{128,64},{192,128},{256,192},{320,256},{384,320},{448,384},... | collective-permute-start | bytes 589832 | tf_op jit(solution)/shard_map/ppermute | solution.py:415
  86.7 16.1 %collective-permute-start.14 = (bf16[64,1536]{1,0:T(8,128)(2,1)S(1)}, bf16[64,1536]{1,0:T(8,128)(2,1)S(1)}, u32[]{:S(2)}, u32[]{:S(2)}) collective-permute-start(bf16[64,1536]{1,0:T(8,128)(2,1)S(1)} %get-tuple-element.141), channel_id=1, source_target_pairs={{64,0},{128,64},{192,128},{256,192},{320,256},{384,320},{448,384},... | collective-permute-start | bytes 589832 | tf_op jit(solution)/shard_map/ppermute | solution.py:415
  93.7 13.9 %collective-permute-start.17 = (bf16[64,1536]{1,0:T(8,128)(2,1)S(1)}, bf16[64,1536]{1,0:T(8,128)(2,1)S(1)}, u32[]{:S(2)}, u32[]{:S(2)}) collective-permute-start(bf16[64,1536]{1,0:T(8,128)(2,1)S(1)} %get-tuple-element.148), channel_id=1, source_target_pairs={{64,0},{128,64},{192,128},{256,192},{320,256},{384,320},{448,384},... | collective-permute-start | bytes 589832 | tf_op jit(solution)/shard_map/ppermute | solution.py:415
  103.3 12.4 %collective-permute-start.16 = (bf16[64,1536]{1,0:T(8,128)(2,1)S(1)}, bf16[64,1536]{1,0:T(8,128)(2,1)S(1)}, u32[]{:S(2)}, u32[]{:S(2)}) collective-permute-start(bf16[64,1536]{1,0:T(8,128)(2,1)S(1)} %get-tuple-element.147), channel_id=1, source_target_pairs={{64,0},{128,64},{192,128},{256,192},{320,256},{384,320},{448,384},... | collective-permute-start | bytes 589832 | tf_op jit(solution)/shard_map/ppermute | solution.py:415
  108.9 12.9 %collective-permute-start.19 = (bf16[64,1536]{1,0:T(8,128)(2,1)}, bf16[64,1536]{1,0:T(8,128)(2,1)}, u32[]{:S(2)}, u32[]{:S(2)}) collective-permute-start(bf16[64,1536]{1,0:T(8,128)(2,1)} %get-tuple-element.154), channel_id=1, source_target_pairs={{64,0},{128,64},{192,128},{256,192},{320,256},{384,320},{448,384},... | collective-permute-start | bytes 589832 | tf_op jit(solution)/shard_map/ppermute | solution.py:415
  117.0 10.6 %collective-permute-start.18 = (bf16[64,1536]{1,0:T(8,128)(2,1)}, bf16[64,1536]{1,0:T(8,128)(2,1)}, u32[]{:S(2)}, u32[]{:S(2)}) collective-permute-start(bf16[64,1536]{1,0:T(8,128)(2,1)} %get-tuple-element.153), channel_id=1, source_target_pairs={{64,0},{128,64},{192,128},{256,192},{320,256},{384,320},{448,384},... | collective-permute-start | bytes 589832 | tf_op jit(solution)/shard_map/ppermute | solution.py:415
  120.5 18.7 %collective-permute-start.26 = (bf16[32,1536]{1,0:T(8,128)(2,1)}, bf16[32,1536]{1,0:T(8,128)(2,1)}, u32[]{:S(2)}, u32[]{:S(2)}) collective-permute-start(bf16[32,1536]{1,0:T(8,128)(2,1)} %get-tuple-element.182), channel_id=1, source_target_pairs={{192,448},{193,449},{194,450},{195,451},{196,452},{197,453},{198,4... | collective-permute-start | bytes 294920 | tf_op jit(solution)/shard_map/ppermute | solution.py:361
  121.8 1.1 copy-start.3
  122.9 1.1 copy-start.7
  124.0 1.0 copy-start.11
  125.1 0.9 copy-start.15
  129.5 22.1 %collective-permute-start.20 = (bf16[64,1536]{1,0:T(8,128)(2,1)}, bf16[64,1536]{1,0:T(8,128)(2,1)}, u32[]{:S(2)}, u32[]{:S(2)}) collective-permute-start(bf16[64,1536]{1,0:T(8,128)(2,1)} %get-tuple-element.159), channel_id=1, source_target_pairs={{64,0},{128,64},{192,128},{256,192},{320,256},{384,320},{448,384},... | collective-permute-start | bytes 589832 | tf_op jit(solution)/shard_map/ppermute | solution.py:415
  137.0 9.4 %collective-permute-start.21 = (bf16[64,1536]{1,0:T(8,128)(2,1)}, bf16[64,1536]{1,0:T(8,128)(2,1)}, u32[]{:S(2)}, u32[]{:S(2)}) collective-permute-start(bf16[64,1536]{1,0:T(8,128)(2,1)} %get-tuple-element.160), channel_id=1, source_target_pairs={{64,0},{128,64},{192,128},{256,192},{320,256},{384,320},{448,384},... | collective-permute-start | bytes 589832 | tf_op jit(solution)/shard_map/ppermute | solution.py:415
  140.7 21.5 %collective-permute-start.27 = (bf16[32,1536]{1,0:T(8,128)(2,1)}, bf16[32,1536]{1,0:T(8,128)(2,1)}, u32[]{:S(2)}, u32[]{:S(2)}) collective-permute-start(bf16[32,1536]{1,0:T(8,128)(2,1)} %broadcast_select_fusion), channel_id=1, source_target_pairs={{192,64},{448,320},{193,65},{449,321},{194,66},{450,322},{195,67},... | collective-permute-start | bytes 294920 | tf_op jit(solution)/shard_map/ppermute | solution.py:364
  146.4 1.1 copy-start.4
  147.5 1.1 copy-start.8
  148.7 1.0 copy-start.12
  149.7 0.9 copy-start.16
  151.6 14.6 %copy-start.5 = (bf16[1536,256]{1,0:T(8,128)(2,1)S(1)}, bf16[1536,256]{1,0:T(8,128)(2,1)}, u32[]{:S(2)}) copy-start(bf16[1536,256]{1,0:T(8,128)(2,1)} %copy-done.2) | copy-start | bytes 2359300
  151.6 14.6 %copy-start.9 = (bf16[256,1536]{1,0:T(8,128)(2,1)S(1)}, bf16[256,1536]{1,0:T(8,128)(2,1)}, u32[]{:S(2)}) copy-start(bf16[256,1536]{1,0:T(8,128)(2,1)} %copy-done.6) | copy-start | bytes 2359300
  151.7 14.6 %copy-start.13 = (f32[512,256]{1,0:T(8,128)S(1)}, f32[512,256]{1,0:T(8,128)}, u32[]{:S(2)}) copy-start(f32[512,256]{1,0:T(8,128)} %copy-done.10) | copy-start | bytes 1572868
  151.7 14.6 %copy-start.17 = (f32[512,128]{1,0:T(8,128)S(1)}, f32[512,128]{1,0:T(8,128)}, u32[]{:S(2)}) copy-start(f32[512,128]{1,0:T(8,128)} %copy-done.14) | copy-start | bytes 786436
  152.8 14.0 %collective-permute-start.22 = (bf16[64,1536]{1,0:T(8,128)(2,1)S(1)}, bf16[64,1536]{1,0:T(8,128)(2,1)S(1)}, u32[]{:S(2)}, u32[]{:S(2)}) collective-permute-start(bf16[64,1536]{1,0:T(8,128)(2,1)S(1)} %get-tuple-element.165), channel_id=1, source_target_pairs={{64,0},{128,64},{192,128},{256,192},{320,256},{384,320},{448,384},... | collective-permute-start | bytes 589832 | tf_op jit(solution)/shard_map/ppermute | solution.py:415
  156.4 9.8 %collective-permute-start.23 = (bf16[64,1536]{1,0:T(8,128)(2,1)S(1)}, bf16[64,1536]{1,0:T(8,128)(2,1)S(1)}, u32[]{:S(2)}, u32[]{:S(2)}) collective-permute-start(bf16[64,1536]{1,0:T(8,128)(2,1)S(1)} %get-tuple-element.166), channel_id=1, source_target_pairs={{64,0},{128,64},{192,128},{256,192},{320,256},{384,320},{448,384},... | collective-permute-start | bytes 589832 | tf_op jit(solution)/shard_map/ppermute | solution.py:415
  163.2 13.3 %collective-permute-start.28 = (bf16[32,1536]{1,0:T(8,128)(2,1)S(1)}, bf16[32,1536]{1,0:T(8,128)(2,1)S(1)}, u32[]{:S(2)}, u32[]{:S(2)}) collective-permute-start(bf16[32,1536]{1,0:T(8,128)(2,1)S(1)} %broadcast_select_fusion.1), channel_id=1, source_target_pairs={{64,0},{192,128},{320,256},{448,384},{65,1},{193,129},{321,257},{4... | collective-permute-start | bytes 294920 | tf_op jit(solution)/shard_map/ppermute | solution.py:367
  167.4 16.5 %collective-permute-start.24 = (bf16[64,1536]{1,0:T(8,128)(2,1)S(1)}, bf16[64,1536]{1,0:T(8,128)(2,1)S(1)}, u32[]{:S(2)}, u32[]{:S(2)}) collective-permute-start(bf16[64,1536]{1,0:T(8,128)(2,1)S(1)} %get-tuple-element.171), channel_id=1, source_target_pairs={{64,0},{128,64},{192,128},{256,192},{320,256},{384,320},{448,384},... | collective-permute-start | bytes 589832 | tf_op jit(solution)/shard_map/ppermute | solution.py:415
  173.6 9.1 %collective-permute-start.25 = (bf16[64,1536]{1,0:T(8,128)(2,1)S(1)}, bf16[64,1536]{1,0:T(8,128)(2,1)S(1)}, u32[]{:S(2)}, u32[]{:S(2)}) collective-permute-start(bf16[64,1536]{1,0:T(8,128)(2,1)S(1)} %get-tuple-element.172), channel_id=1, source_target_pairs={{64,0},{128,64},{192,128},{256,192},{320,256},{384,320},{448,384},... | collective-permute-start | bytes 589832 | tf_op jit(solution)/shard_map/ppermute | solution.py:415
  184.0 1.4 copy-start.22
  184.0 1.4 copy-start.28
  187.5 4.3 %collective-permute-start.30 = (bf16[16,64,256]{2,1,0:T(8,128)(2,1)S(1)}, bf16[16,64,256]{2,1,0:T(8,128)(2,1)S(1)}, u32[]{:S(2)}, u32[]{:S(2)}) collective-permute-start(bf16[16,64,256]{2,1,0:T(8,128)(2,1)S(1)} %get-tuple-element.192), channel_id=1, source_target_pairs={{0,1},{1,0},{2,3},{3,2},{4,5},{5,4},{6,7},{7,6},{8,9},{9,8},{10,11... | collective-permute-start | bytes 1572872 | tf_op jit(solution)/shard_map/ppermute | solution.py:261
  189.4 5.2 %collective-permute-start.29 = (bf16[16,64,256]{2,1,0:T(8,128)(2,1)S(1)}, bf16[16,64,256]{2,1,0:T(8,128)(2,1)S(1)}, u32[]{:S(2)}, u32[]{:S(2)}) collective-permute-start(bf16[16,64,256]{2,1,0:T(8,128)(2,1)S(1)} %get-tuple-element.190), channel_id=1, source_target_pairs={{0,1},{1,0},{2,3},{3,2},{4,5},{5,4},{6,7},{7,6},{8,9},{9,8},{10,11... | collective-permute-start | bytes 1572872 | tf_op jit(solution)/shard_map/ppermute | solution.py:261
  192.0 15.7 %collective-permute-start.31 = (bf16[16,64,256]{2,1,0:T(8,128)(2,1)S(1)}, bf16[16,64,256]{2,1,0:T(8,128)(2,1)S(1)}, u32[]{:S(2)}, u32[]{:S(2)}) collective-permute-start(bf16[16,64,256]{2,1,0:T(8,128)(2,1)S(1)} %add_convert_fusion.1), channel_id=1, source_target_pairs={{0,32},{32,0},{1,33},{33,1},{2,34},{34,2},{3,35},{35,3},{4,36},{36... | collective-permute-start | bytes 1572872 | tf_op jit(solution)/shard_map/ppermute | solution.py:261
  208.8 43.4 %all-to-all-start = ((bf16[16,64,256]{2,1,0:T(8,128)(2,1)}), bf16[16,64,256]{2,1,0:T(8,128)(2,1)S(1)}, u32[]{:S(2)}, u32[]{:S(2)}) async-start(bf16[16,64,256]{2,1,0:T(8,128)(2,1)} %add_convert_fusion), calls=%async_computation | async-start | bytes 1048576 | tf_op jit(solution)/shard_map/all_to_all | solution.py:444

commit v2 on v1

--- a/solution.py
+++ b/solution.py
@@ -18,6 +18,7 @@
 BF16 = jnp.bfloat16
 VM = pl.BlockSpec(memory_space=pltpu.VMEM)
 SM = pl.BlockSpec(memory_space=pltpu.SMEM)
+HB = pl.BlockSpec(memory_space=pltpu.MemorySpace.HBM)
 
 
 def silu_slope(pre_act):
@@ -25,7 +26,7 @@
     return sigma * (1.0 + pre_act * (1.0 - sigma))
 
 
-def call(kernel, out_shape, in_specs, args, flops, moved, aliases=None, scratch=(), limit=24):
+def call(kernel, out_shape, in_specs, args, flops, moved, aliases=None, scratch=(), limit=16):
     return pl.pallas_call(
         kernel,
         out_shape=out_shape,
@@ -38,27 +39,38 @@
     )(*args)
 
 
-def prepare_kernel(
-    lens_ref, core_ref, _labels, x_ref, gain_ref, wd_ref, wu_ref, first_ref, low_ref, xn_ref, h_ref, a_ref, q_ref, pooled_ref, wut_ref, wdt_ref, mine_ref, second_ref, _g, _da
-):
+def half_kernel(core_ref, first_ref, mine_ref, sem):
+    half = mine_ref.shape[1]
+    columns = pl.ds(pl.multiple_of(core_ref[0] * half, 128), half)
+    copy = pltpu.make_async_copy(first_ref.at[:, columns], mine_ref, sem)
+    copy.start()
+    copy.wait()
+
+
+def prepare_kernel(lens_ref, *refs):
+    sources, refs = refs[:6], refs[6:]
+    x_ref, top_ref, gain_ref, second_ref, xn_ref, h_ref, a_ref, q_ref, pooled_ref, wut_ref, wdt_ref, _, _ = refs[:13]
+    wd_ref, wu_ref, sems = refs[13:]
+    x_hbm, top_hbm, gain_hbm, second_hbm, wd_hbm, wu_hbm = sources
     micros, seq_len = 4, 128
+    pairs = [(wd_hbm, wd_ref), (gain_hbm, gain_ref), (wu_hbm, wu_ref), (second_hbm, second_ref), (top_hbm, top_ref)]
+    for m in range(micros):
+        rows = slice(m * seq_len, (m + 1) * seq_len)
+        pairs.append((x_hbm.at[rows], x_ref.at[rows]))
+    copies = [pltpu.make_async_copy(source, target, sems.at[i]) for i, (source, target) in enumerate(pairs)]
+    for i in (0, 1, 5, 6, 7, 8, 2, 3, 4):
+        copies[i].start()
+    copies[0].wait()
+    copies[1].wait()
     gain = gain_ref[0:1, :]
-    half = first_ref.shape[1] // 2
-    for c in range(2):
-
-        @pl.when(core_ref[0] == c)
-        def _():
-            mine_ref[...] = first_ref[:, c * half : (c + 1) * half]
-
-    second_ref[...] = low_ref[...]
-    wut_ref[...] = wu_ref[...].T
     wdt_ref[...] = wd_ref[...].T
     pooled_ref[...] = jnp.zeros_like(pooled_ref)
     positions = lax.broadcasted_iota(jnp.int32, (seq_len, 1), 0)
     for m in range(micros):
+        copies[5 + m].wait()
         rows = pl.ds(m * seq_len, seq_len)
         values = x_ref[rows, :].astype(F32)
-        count = lens_ref[m, 0]
+        count = lens_ref[m]
         total = jnp.sum(jnp.where(positions < count, values, 0.0), axis=0, keepdims=True)
         pooled_ref[m : m + 1, :] = total / count.astype(F32)
         q = lax.rsqrt(jnp.mean(values * values, axis=-1, keepdims=True) + EPSILON)
@@ -68,6 +80,10 @@
         a_ref[rows, :] = a
         h_ref[rows, :] = (a * jax.nn.sigmoid(a)).astype(BF16)
         q_ref[rows, :] = jnp.broadcast_to(q, (seq_len, 128))
+    copies[2].wait()
+    wut_ref[...] = wu_ref[...].T
+    copies[3].wait()
+    copies[4].wait()
 
 
 def step_kernel(step, chunks, has_top, has_in, has_rev, *refs):
@@ -105,7 +121,7 @@
             micro = lax.div(place, per)
             first = lax.rem(place, per) * CHUNK
             positions = lax.broadcasted_iota(jnp.int32, (CHUNK, 1), 0) + first
-            extra = jnp.where(positions < lens_ref[micro, 0], rev_ref[pl.ds(micro, 1), :], 0.0)
+            extra = jnp.where(positions < lens_ref[micro], rev_ref[pl.ds(micro, 1), :], 0.0)
             g_ref[rows, :] = (in_ref[...].astype(F32) + extra).astype(BF16)
 
     @pl.when(live)
@@ -127,7 +143,7 @@
     rows = lax.broadcasted_iota(jnp.int32, shape, 0)
     column = jnp.ones(shape, jnp.int32)
     for m in range(4):
-        column = jnp.where(rows == m, ref[m, 0], column)
+        column = jnp.where(rows == m, ref[m], column)
     return column
 
 
@@ -136,7 +152,7 @@
 ):
     half = own_ref.shape[1]
     channels = 2 * half
-    languages = second_ref.shape[1]
+    languages = second_ref.shape[0]
 
     @pl.when(sec_ref[0] == SECTIONS // 2 - 1)
     def _():
@@ -152,15 +168,15 @@
         pre = jnp.concatenate([low, high], axis=1)
         hidden = (pre * jax.nn.sigmoid(pre)).astype(BF16)
         second = second_ref[...]
-        logits = jnp.dot(hidden, second, preferred_element_type=F32)
+        dims = (((1,), (1,)), ((), ()))
+        logits = lax.dot_general(hidden, second, dims, preferred_element_type=F32)
         exponent = jnp.exp(logits)
         probs = exponent / jnp.sum(exponent, axis=-1, keepdims=True)
         lanes = lax.broadcasted_iota(jnp.int32, logits.shape, 1)
         onehot = jnp.where(lanes == per_row(labels_ref, logits.shape), 1.0, 0.0)
         valid = lax.broadcasted_iota(jnp.int32, logits.shape, 0) < 4
         grad_logits = jnp.where(valid, probs - onehot, 0.0).astype(BF16)
-        dims = (((1,), (1,)), ((), ()))
-        grad_hidden = lax.dot_general(grad_logits, second, dims, preferred_element_type=F32)
+        grad_hidden = jnp.dot(grad_logits, second, preferred_element_type=F32)
         grad_pre = (grad_hidden * silu_slope(pre)).astype(BF16)
         hold[...] = jnp.zeros_like(hold)
         hold[0:8, :] = normed.astype(F32)
@@ -179,10 +195,12 @@
         rev_ref[...] = -REVERSAL * grad_pooled / per_row(lens_ref, (8, 1)).astype(F32)
 
 
-def unpack_kernel(sec_ref, band_rows, n_dp, lines_ref, nb_ref, gp_ref, hid_ref, gl_ref):
+def critic_sums_kernel(band_rows, parts, sec_ref, yl_ref, core_ref, lines_ref, kept_ref, sent_ref, crit):
+    n_yl, n_z, n_c = parts
+    n_dp = n_yl * n_z * n_c
     features = lines_ref.shape[1]
     channels = features // 2
-    padded = gp_ref.shape[1] // n_dp
+    padded = crit.shape[0] // n_dp
     share = channels // n_dp
 
     def grow(block):
@@ -196,7 +214,7 @@
     lines = lines_ref[...].astype(F32)
     base = sec_ref[0] * band_rows
     band = pick((features, 256), lambda i, j: (i == j + base) & (j < band_rows))
-    nb_ref[...] = jnp.dot(grow(lines[0:8]), band, preferred_element_type=F32).astype(BF16)
+    nb = jnp.dot(grow(lines[0:8]), band, preferred_element_type=F32).astype(BF16)
     wide = (channels, n_dp * padded)
     columns = lax.broadcasted_iota(jnp.int32, (1, wide[1]), 1)
     slot = lax.div(columns, padded)
@@ -204,14 +222,60 @@
     source = jnp.where(inside < share, slot * share + inside, -1)
     spread = jnp.where(lax.broadcasted_iota(jnp.int32, wide, 0) == source, 1.0, 0.0).astype(BF16)
     both = grow(lines[8:16])
-    gp_ref[...] = jnp.dot(both[:, :channels], spread, preferred_element_type=F32).astype(BF16)
-    hid_ref[...] = jnp.dot(both[:, channels:], spread, preferred_element_type=F32).astype(BF16)
-    shift = pick((128, 128), lambda i, j: j == i + 64)
-    gl_ref[...] = jnp.dot(grow(lines[16:24, :128]), shift, preferred_element_type=F32).astype(BF16)
-
-
-def finish_kernel(parts, place_ref, xn_ref, g_ref, h_ref, da_ref, nb_ref, gl_ref, gp_ref, hid_ref, *refs):
-    outs, (down, up, crit) = refs[:-3], refs[-3:]
+    gp = jnp.dot(both[:, :channels], spread, preferred_element_type=F32).astype(BF16)
+    hid = jnp.dot(both[:, channels:], spread, preferred_element_type=F32).astype(BF16)
+    shift = pick((128, 256), lambda i, j: j == i + 192)
+    gl = jnp.dot(grow(lines[16:24, :128]), shift, preferred_element_type=F32).astype(BF16)
+    dims = (((0,), (0,)), ((), ()))
+    crit[...] = lax.dot_general(gp, nb, dims, preferred_element_type=F32)
+    crit[...] += lax.dot_general(hid, gl, dims, preferred_element_type=F32)
+
+    def pack(z, _):
+        for dy, dc, dest in places(parts, yl_ref, core_ref, z):
+            piece = crit[pl.ds(pl.multiple_of(dest * padded, 16), padded), :].astype(BF16)
+            (sent_ref if dc else kept_ref)[dy, z] = piece
+        return 0
+
+    lax.fori_loop(0, n_z, pack, 0)
+
+
+def places(parts, yl_ref, core_ref, z):
+    n_yl, n_z, n_c = parts
+    found = []
+    for dy in range(n_yl):
+        for dc in range(n_c):
+            yl = yl_ref[0] if dy == 0 else n_yl - 1 - yl_ref[0]
+            c = core_ref[0] if dc == 0 else n_c - 1 - core_ref[0]
+            found.append((dy, dc, (yl * n_z + z) * n_c + c))
+    return found
+
+
+def plus(left, right):
+    return (left.astype(F32) + right.astype(F32)).astype(BF16)
+
+
+def split_kernel(kept_ref, got_ref, own_ref, other_ref):
+    own_ref[...] = plus(kept_ref[0], got_ref[0])
+    if kept_ref.shape[0] > 1:
+        other_ref[...] = plus(kept_ref[1], got_ref[1])
+
+
+def add_kernel(left_ref, right_ref, out_ref):
+    out_ref[...] = plus(left_ref[...], right_ref[...])
+
+
+def pick_kernel(flag_ref, moved_ref, held_ref, out_ref):
+    @pl.when(flag_ref[0] != 0)
+    def _():
+        out_ref[...] = moved_ref[...]
+
+    @pl.when(flag_ref[0] == 0)
+    def _():
+        out_ref[...] = held_ref[...]
+
+
+def finish_kernel(parts, yl_ref, core_ref, xn_ref, g_ref, h_ref, da_ref, *refs):
+    outs, (down, up) = refs[:-2], refs[-2:]
     n_yl, n_z, n_c = parts
     features = xn_ref.shape[1]
     dims = (((0,), (0,)), ((), ()))
@@ -220,24 +284,13 @@
         cols = pl.ds(k * width, width)
         down[cols, :] = lax.dot_general(xn_ref[:, cols], da_ref[...], dims, preferred_element_type=F32)
         up[cols, :] = lax.dot_general(g_ref[:, cols], h_ref[...], dims, preferred_element_type=F32)
-    crit[:, :128] = lax.dot_general(gp_ref[...], nb_ref[:, :128], dims, preferred_element_type=F32)
-    crit[:, 128:] = lax.dot_general(
-        gp_ref[...], nb_ref[:, 128:], dims, preferred_element_type=F32
-    ) + lax.dot_general(hid_ref[...], gl_ref[...], dims, preferred_element_type=F32)
     span = features // (n_yl * n_z * n_c)
-    cspan = crit.shape[0] // (n_yl * n_z * n_c)
-    my_yl, my_c = place_ref[0], place_ref[1]
 
     def pack(z, _):
-        for dy in range(n_yl):
-            for dc in range(n_c):
-                yl = my_yl if dy == 0 else n_yl - 1 - my_yl
-                c = my_c if dc == 0 else n_c - 1 - my_c
-                dest = (yl * n_z + z) * n_c + c
-                wide = pl.ds(pl.multiple_of(dest * span, 8), span)
-                thin = pl.ds(pl.multiple_of(dest * cspan, 8), cspan)
-                piece = jnp.concatenate([down[wide, :], up[wide, :], crit[thin, :]], axis=0)
-                outs[dc * n_yl + dy][z] = piece.astype(BF16)
+        for dy, dc, dest in places(parts, yl_ref, core_ref, z):
+            rows = pl.ds(pl.multiple_of(dest * span, 8), span)
+            piece = jnp.concatenate([down[rows, :], up[rows, :]], axis=0)
+            outs[dc * n_yl + dy][z] = piece.astype(BF16)
         return 0
 
     lax.fori_loop(0, n_z, pack, 0)
@@ -284,9 +337,25 @@
     half = channels // 2
     sds = jax.ShapeDtypeStruct
 
-    xn, h, a, q, pooled, wut, wdt, mine, second, grads, inner = call(
+    lens = seq_lengths.reshape(micros)
+    mine = call(
+        half_kernel,
+        sds((critic_first.shape[0], half), BF16),
+        [SM, HB],
+        (core_s, critic_first),
+        0,
+        1 << 19,
+        scratch=[pltpu.SemaphoreType.DMA], limit=16,
+    )
+    even = lax.ppermute(mine, SEC, [(i, i + 1) for i in range(0, SECTIONS, 2)])
+    languages = critic_second.shape[1]
+    x, top, gain_v, second, xn, h, a, q, pooled, wut, wdt, grads, inner = call(
         prepare_kernel,
         (
+            sds((rows, features), BF16),
+            sds((rows, features), BF16),
+            sds((1, features), F32),
+            sds((languages, channels), BF16),
             sds((rows, features), BF16),
             sds((rows, rank), BF16),
             sds((rows, rank), F32),
@@ -294,20 +363,19 @@
             sds((8, features), F32),
             sds((features, rank), BF16),
             sds((rank, features), BF16),
-            sds((critic_first.shape[0], half), BF16),
-            sds(critic_second.shape, BF16),
             sds((rows, features), BF16),
             sds((rows, rank), BF16),
         ),
-        [SM] * 3 + [VM] * 6,
-        (seq_lengths, core_s, lang_labels, x, gain, wd, w_up[0], critic_first, critic_second),
+        [SM] + [HB] * 6,
+        (lens, x, top, gain, critic_second.T, wd, w_up[0]),
         2 * rows * features * rank,
         8 << 20,
-        limit=10,
+        scratch=[pltpu.VMEM((features, rank), BF16), pltpu.VMEM((rank, features), BF16), pltpu.SemaphoreType.DMA((9,))], limit=16,
     )
 
     three = SECTIONS // 2 - 1
     held = {}
+    yl_s = lax.axis_index("yl").reshape(1).astype(jnp.int32)
     band_rows = critic_first.shape[0]
     share = channels // n_dp
     padded = -(-share // 16) * 16
@@ -320,19 +388,17 @@
             (after(sec_s, token), *pieces),
             0,
             2 << 20,
-            limit=4,
         )
 
     def side_work(step, token):
         if step == 0:
-            held["even"] = lax.ppermute(after(mine, token), SEC, [(i, i + 1) for i in range(0, SECTIONS, 2)])
+            held["pair"] = join(token, even, mine)
+            held["far"] = [lax.ppermute(held["pair"], SEC, [(i, three)]) for i in (7, 5, 1)]
         elif step == 1:
             held["pooled"] = lax.ppermute(after(pooled, token), SEC, [(4, three)])
-        elif step == 2:
-            held["pair"] = join(token, held["even"], mine)
-            held["far"] = [lax.ppermute(held["pair"], SEC, [(i, three)]) for i in (1, 5, 7)]
-        elif step == 5:
-            held["own"] = join(token, held["far"][0], held["pair"], *held["far"][1:])
+        elif step == 4:
+            far = held["far"]
+            held["own"] = join(token, far[2], held["pair"], far[1], far[0])
             pairs = [(three * 2, three * 2 + 1), (three * 2 + 1, three * 2)]
             held["other"] = lax.ppermute(held["own"], SEC + ("c",), pairs)
         elif step == 7:
@@ -343,8 +409,8 @@
                 (
                     after(sec_s, token),
                     core_s,
-                    lang_labels,
-                    seq_lengths,
+                    lang_labels.reshape(micros),
+                    lens,
                     held["pooled"],
                     held["own"],
                     held["other"],
@@ -353,34 +419,47 @@
                 1 << 27,
                 4 << 20,
                 scratch=[pltpu.VMEM((32, features), F32)],
-                limit=8,
             )
-        elif step in (9, 12, 15):
+        elif step in (8, 10, 12):
             lines = after(held["lines"], token)
-            if step == 9:
-                moved = lax.ppermute(lines, SEC, [(3, 7)])
-                gets = sec == 7
-            elif step == 12:
-                moved = lax.ppermute(lines, SEC, [(3, 1), (7, 5)])
-                gets = (sec == 1) | (sec == 5)
+            if step == 8:
+                route, gets = [(3, 7)], sec == 7
+            elif step == 10:
+                route, gets = [(3, 1), (7, 5)], (sec == 1) | (sec == 5)
             else:
-                moved = lax.ppermute(lines, SEC, [(i + 1, i) for i in range(0, SECTIONS, 2)])
-                gets = sec % 2 == 0
-            held["lines"] = jnp.where(gets, moved, lines)
-        elif step == 18:
-            held["critic"] = call(
-                lambda sec_ref, *refs: unpack_kernel(sec_ref, band_rows, n_dp, *refs),
-                (
-                    sds((16, 256), BF16),
-                    sds((16, n_dp * padded), BF16),
-                    sds((16, n_dp * padded), BF16),
-                    sds((16, 128), BF16),
-                ),
-                [SM, VM],
-                (after(sec_s, token), held["lines"]),
+                route, gets = [(i + 1, i) for i in range(0, SECTIONS, 2)], sec % 2 == 0
+            moved = lax.ppermute(lines, SEC, route)
+            held["moved"] = (gets.astype(jnp.int32).reshape(1), moved)
+        elif step == 14:
+            kept, sent = call(
+                functools.partial(critic_sums_kernel, band_rows, parts),
+                (sds((n_yl, n_z, padded, rank), BF16),) * 2,
+                [SM, SM, SM, VM],
+                (after(sec_s, token), yl_s, core_s, held["lines"]),
                 1 << 26,
                 1 << 20,
-                limit=12,
+                scratch=[pltpu.VMEM((n_dp * padded, rank), F32)],
+            )
+            held["kept"] = kept
+            held["got"] = swap(sent, "c", n_c)
+        elif step == 16:
+            one = sds((n_z, padded, rank), BF16)
+            own, other = call(split_kernel, (one, one), [VM, VM], (after(held["kept"], token), held["got"]), 0, 1 << 20)
+            held["own_sum"] = own
+            if n_yl == 2:
+                held["other_sum"] = swap(other, "yl", n_yl)
+        elif step == 19 and n_yl == 2:
+            args = (after(held["own_sum"], token), held["other_sum"])
+            held["own_sum"] = call(add_kernel, sds(args[0].shape, BF16), [VM, VM], args, 0, 1 << 20)
+        if step in (9, 11, 13):
+            flag, moved = held.pop("moved")
+            held["lines"] = call(
+                pick_kernel,
+                sds(held["lines"].shape, BF16),
+                [SM, VM, VM],
+                (after(flag, token), moved, held["lines"]),
+                0,
+                1 << 18,
             )
 
     steps = DELAY * (SECTIONS - 1) + chunks
@@ -391,7 +470,7 @@
         has_in = step >= DELAY
         first_rev = DELAY * (SECTIONS - 1 - three)
         has_rev = first_rev <= step < first_rev + chunks
-        args = [sec_s, seq_lengths, x, a, q, gain, wut, wdt]
+        args = [sec_s, lens, x, a, q, gain_v, wut, wdt]
         specs = [SM, SM] + [VM] * 6
         if has_top:
             args.append(top)
@@ -409,43 +488,40 @@
             4 * CHUNK * features * rank,
             3 << 20,
             aliases={len(args) - 2: 1, len(args) - 1: 2},
-            limit=6,
         )
         if step < steps - DELAY:
             received[step] = lax.ppermute(outgoing, SEC, route)
         side_work(step, outgoing)
 
-    band, gp, hid, gl = held["critic"]
     span = features // n_dp
-    piece = sds((n_z, 2 * span + padded, rank), BF16)
-    place = jnp.stack([lax.axis_index("yl"), core]).astype(jnp.int32)
+    piece = sds((n_z, 2 * span, rank), BF16)
     packed = call(
         functools.partial(finish_kernel, parts),
         (piece,) * (n_yl * n_c),
-        [SM] + [VM] * 8,
-        (place, xn, grads, h, inner, band, gl, gp, hid),
+        [SM, SM] + [VM] * 4,
+        (yl_s, core_s, xn, grads, h, inner),
         4 * rows * features * rank,
         8 << 20,
-        scratch=[pltpu.VMEM((features, rank), F32)] * 2 + [pltpu.VMEM((n_dp * padded, rank), F32)],
-        limit=16,
+        scratch=[pltpu.VMEM((features, rank), F32)] * 2,
     )
-
-    def add(left, right):
-        return (left.astype(F32) + right.astype(F32)).astype(BF16)
 
     kept, sent = packed[:n_yl], packed[n_yl:]
     halves = [None] * n_yl
     for i in reversed(range(n_yl)):
-        halves[i] = add(kept[i], swap(sent[i], "c", n_c))
+        halves[i] = plus(kept[i], swap(sent[i], "c", n_c))
     summed = halves[0]
+    crit = after(held["own_sum"], summed)
+    if n_z > 1:
+        crit = lax.all_to_all(crit, "z", 0, 0, tiled=True)
     if n_yl == 2:
-        summed = add(summed, swap(halves[1], "yl", n_yl))
+        moved = swap(halves[1], "yl", n_yl)
+        summed = plus(summed, after(moved, crit))
     if n_z > 1:
         summed = lax.all_to_all(summed, "z", 0, 0, tiled=True)
     total = jnp.sum(summed.astype(F32), axis=0)
     down = total[:span]
-    up = total[span : 2 * span].T
-    crit = total[2 * span : 2 * span + share]
+    up = total[span:].T
+    crit = jnp.sum(crit.astype(F32), axis=0)[:share]
     dp_place = lax.axis_index(("yl", "z", "c"))
     wd_own = lax.dynamic_slice_in_dim(wd, dp_place * span, span, 0).astype(F32)
     gain_own = lax.dynamic_slice_in_dim(gain[0], dp_place * span, span, 0)

time: 257 us -> 266 us (1.035)
  the two profiles are of different devices: /device:TPU:6 before, /device:TPU:4 now
where the time goes in v2:
time: 266 us; the launch traced here: 264 us
  starting transfers between devices  144 us (54%)
  waiting for transfers between devices  57.3 us (22%)
  Pallas kernels  37.3 us (14%)
  local copies, waits for them, and re-layouts  19.5 us (7%)
  other arithmetic  3.85 us (1%)
    ppermute x20, starting transfers between devices, whole(): received[step] = lax.ppermute(outgoing, SEC, route)  93.7 us
    pallas_call x34, Pallas kernels, call(): pl.pallas_call(kernel, out_shape=out_shape, in_specs=in_specs, out_specs=...  37.3 us
    all_to_all x1, waiting for transfers between devices, whole(): summed = lax.all_to_all(summed, 'z', 0, 0, tiled=True)  20.4 us
    unnamed x56, local copies, waits for them, and re-layouts  18.2 us
    all_to_all x1, starting transfers between devices, whole(): crit = lax.all_to_all(crit, 'z', 0, 0, tiled=True)  15.2 us
    ppermute x5, waiting for transfers between devices, swap(): return lax.ppermute(block, axis, [(i, size - 1 - i) for i in range(size)])  14.9 us
    ppermute x5, starting transfers between devices, swap(): return lax.ppermute(block, axis, [(i, size - 1 - i) for i in range(size)])  11.4 us
    ppermute x20, waiting for transfers between devices, whole(): received[step] = lax.ppermute(outgoing, SEC, route)  11.2 us
  transfers between devices with their start and end apart: 36, of which 12 were waited for; matrix products, arithmetic and copies ran while one was open for 1% of the time, Pallas kernels for 14%

profile of v2, /device:TPU:4, one launch (start us, length us, event | category | flops | bytes accessed | tf_op | source)
XLA Modules:
  0.0 263.8 jit_solution(14665516945930265401)
XLA Ops:
  2.3 5.8 %collective-permute-start.8 = (bf16[192,384]{1,0:T(8,128)(2,1)}, bf16[192,384]{1,0:T(8,128)(2,1)}, u32[]{:S(2)}, u32[]{:S(2)}) collective-permute-start(bf16[192,384]{1,0:T(8,128)(2,1)} %shard_map.137.refs_1_), channel_id=1, source_target_pairs={{0,64},{128,192},{256,320},{384,448},{1,65},{129,193},{257,321},{3... | collective-permute-start | bytes 442376 | tf_op jit(solution)/shard_map/ppermute | solution.py:350
  8.1 1.4 copy-done.14
  9.5 1.4 copy-done.15
  15.3 4.5 %shard_map.128 = (bf16[512,1536]{1,0:T(8,128)(2,1)S(1)}, bf16[512,1536]{1,0:T(8,128)(2,1)S(1)}, f32[1,1536]{1,0:T(1,128)S(1)}, bf16[29,768]{1,0:T(8,128)(2,1)S(1...) custom-call(s32[4]{0:T(128)S(1)} %bitcast.30, ...), custom_call_target="tpu_custom_call" | custom-call | flops 402653184 | bytes 8388608 | tf_op jit(solution)/shard_map/pallas_call | solution.py:30
  21.0 1.9 collective-permute-start.1
  26.6 7.3 %collective-permute-start = (bf16[64,1536]{1,0:T(8,128)(2,1)S(1)}, bf16[64,1536]{1,0:T(8,128)(2,1)S(1)}, u32[]{:S(2)}, u32[]{:S(2)}) collective-permute-start(bf16[64,1536]{1,0:T(8,128)(2,1)S(1)} %get-tuple-element.119), channel_id=1, source_target_pairs={{64,0},{128,64},{192,128},{256,192},{320,256},{384,320},{448,384},... | collective-permute-start | bytes 589832 | tf_op jit(solution)/shard_map/ppermute | solution.py:493
  34.4 1.9 collective-permute-start.3
  36.4 2.8 %collective-permute-done.refs_9_ = bf16[64,1536]{1,0:T(8,128)(2,1)S(1)} collective-permute-done((bf16[64,1536]{1,0:T(8,128)(2,1)S(1)}, bf16[64,1536]{1,0:T(8,128)(2,1)S(1)}, u32[]{:S(2)}, u32[]{:S(2)}) %collective-permute-start) | collective-permute-done | bytes 196640 | tf_op jit(solution)/shard_map/ppermute | solution.py:493
  39.7 3.9 %collective-permute-done.3.refs_9_ = bf16[64,1536]{1,0:T(8,128)(2,1)S(1)} collective-permute-done((bf16[64,1536]{1,0:T(8,128)(2,1)S(1)}, bf16[64,1536]{1,0:T(8,128)(2,1)S(1)}, u32[]{:S(2)}, u32[]{:S(2)}) %collective-permute-start.3) | collective-permute-done | bytes 196640 | tf_op jit(solution)/shard_map/ppermute | solution.py:493
  45.0 6.1 %collective-permute-start.2 = (bf16[64,1536]{1,0:T(8,128)(2,1)S(1)}, bf16[64,1536]{1,0:T(8,128)(2,1)S(1)}, u32[]{:S(2)}, u32[]{:S(2)}) collective-permute-start(bf16[64,1536]{1,0:T(8,128)(2,1)S(1)} %get-tuple-element.125), channel_id=1, source_target_pairs={{64,0},{128,64},{192,128},{256,192},{320,256},{384,320},{448,384},... | collective-permute-start | bytes 589832 | tf_op jit(solution)/shard_map/ppermute | solution.py:493
  51.1 3.2 %collective-permute-start.5 = (bf16[64,1536]{1,0:T(8,128)(2,1)S(1)}, bf16[64,1536]{1,0:T(8,128)(2,1)S(1)}, u32[]{:S(2)}, u32[]{:S(2)}) collective-permute-start(bf16[64,1536]{1,0:T(8,128)(2,1)S(1)} %get-tuple-element.132), channel_id=1, source_target_pairs={{64,0},{128,64},{192,128},{256,192},{320,256},{384,320},{448,384},... | collective-permute-start | bytes 589832 | tf_op jit(solution)/shard_map/ppermute | solution.py:493
  54.3 2.0 collective-permute-done.2.refs_9_
  56.9 6.8 %collective-permute-start.4 = (bf16[64,1536]{1,0:T(8,128)(2,1)S(1)}, bf16[64,1536]{1,0:T(8,128)(2,1)S(1)}, u32[]{:S(2)}, u32[]{:S(2)}) collective-permute-start(bf16[64,1536]{1,0:T(8,128)(2,1)S(1)} %get-tuple-element.131), channel_id=1, source_target_pairs={{64,0},{128,64},{192,128},{256,192},{320,256},{384,320},{448,384},... | collective-permute-start | bytes 589832 | tf_op jit(solution)/shard_map/ppermute | solution.py:493
  63.7 1.2 shard_map.135
  65.0 2.5 collective-permute-start.13
  67.8 1.2 shard_map.136
  69.1 5.5 %collective-permute-start.6 = (bf16[64,1536]{1,0:T(8,128)(2,1)S(1)}, bf16[64,1536]{1,0:T(8,128)(2,1)S(1)}, u32[]{:S(2)}, u32[]{:S(2)}) collective-permute-start(bf16[64,1536]{1,0:T(8,128)(2,1)S(1)} %get-tuple-element.137), channel_id=1, source_target_pairs={{64,0},{128,64},{192,128},{256,192},{320,256},{384,320},{448,384},... | collective-permute-start | bytes 589832 | tf_op jit(solution)/shard_map/ppermute | solution.py:493
  74.6 1.9 collective-permute-start.7
  76.5 1.8 collective-permute-done.7.pooled_ref
  78.8 1.2 shard_map.141
  80.1 8.4 %collective-permute-start.15 = (bf16[64,1536]{1,0:T(8,128)(2,1)S(1)}, bf16[64,1536]{1,0:T(8,128)(2,1)S(1)}, u32[]{:S(2)}, u32[]{:S(2)}) collective-permute-start(bf16[64,1536]{1,0:T(8,128)(2,1)S(1)} %get-tuple-element.151), channel_id=1, source_target_pairs={{64,0},{128,64},{192,128},{256,192},{320,256},{384,320},{448,384},... | collective-permute-start | bytes 589832 | tf_op jit(solution)/shard_map/ppermute | solution.py:493
  88.5 1.2 shard_map.142
  89.8 2.0 collective-permute-start.14
  91.8 1.5 collective-permute-done.15.refs_8_
  93.2 1.2 shard_map.143
  94.5 6.8 %collective-permute-start.17 = (bf16[64,1536]{1,0:T(8,128)(2,1)S(1)}, bf16[64,1536]{1,0:T(8,128)(2,1)S(1)}, u32[]{:S(2)}, u32[]{:S(2)}) collective-permute-start(bf16[64,1536]{1,0:T(8,128)(2,1)S(1)} %get-tuple-element.157), channel_id=1, source_target_pairs={{64,0},{128,64},{192,128},{256,192},{320,256},{384,320},{448,384},... | collective-permute-start | bytes 589832 | tf_op jit(solution)/shard_map/ppermute | solution.py:493
  101.3 1.2 shard_map.144
  102.6 2.0 collective-permute-start.16
  105.1 1.2 shard_map.145
  106.4 6.8 %collective-permute-start.19 = (bf16[64,1536]{1,0:T(8,128)(2,1)S(1)}, bf16[64,1536]{1,0:T(8,128)(2,1)S(1)}, u32[]{:S(2)}, u32[]{:S(2)}) collective-permute-start(bf16[64,1536]{1,0:T(8,128)(2,1)S(1)} %get-tuple-element.163), channel_id=1, source_target_pairs={{64,0},{128,64},{192,128},{256,192},{320,256},{384,320},{448,384},... | collective-permute-start | bytes 589832 | tf_op jit(solution)/shard_map/ppermute | solution.py:493
  113.2 1.2 shard_map.146
  114.5 3.0 %collective-permute-start.18 = (bf16[64,1536]{1,0:T(8,128)(2,1)S(1)}, bf16[64,1536]{1,0:T(8,128)(2,1)S(1)}, u32[]{:S(2)}, u32[]{:S(2)}) collective-permute-start(bf16[64,1536]{1,0:T(8,128)(2,1)S(1)} %get-tuple-element.162), channel_id=1, source_target_pairs={{64,0},{128,64},{192,128},{256,192},{320,256},{384,320},{448,384},... | collective-permute-start | bytes 589832 | tf_op jit(solution)/shard_map/ppermute | solution.py:493
  118.3 6.4 %collective-permute-start.21 = (bf16[64,1536]{1,0:T(8,128)(2,1)S(1)}, bf16[64,1536]{1,0:T(8,128)(2,1)S(1)}, u32[]{:S(2)}, u32[]{:S(2)}) collective-permute-start(bf16[64,1536]{1,0:T(8,128)(2,1)S(1)} %get-tuple-element.169), channel_id=1, source_target_pairs={{64,0},{128,64},{192,128},{256,192},{320,256},{384,320},{448,384},... | collective-permute-start | bytes 589832 | tf_op jit(solution)/shard_map/ppermute | solution.py:493
  125.2 5.1 %collective-permute-start.20 = (bf16[64,1536]{1,0:T(8,128)(2,1)S(1)}, bf16[64,1536]{1,0:T(8,128)(2,1)S(1)}, u32[]{:S(2)}, u32[]{:S(2)}) collective-permute-start(bf16[64,1536]{1,0:T(8,128)(2,1)S(1)} %get-tuple-element.168), channel_id=1, source_target_pairs={{64,0},{128,64},{192,128},{256,192},{320,256},{384,320},{448,384},... | collective-permute-start | bytes 589832 | tf_op jit(solution)/shard_map/ppermute | solution.py:493
  130.4 1.2 shard_map.149
  131.6 4.2 %collective-permute-start.23 = (bf16[64,1536]{1,0:T(8,128)(2,1)}, bf16[64,1536]{1,0:T(8,128)(2,1)}, u32[]{:S(2)}, u32[]{:S(2)}) collective-permute-start(bf16[64,1536]{1,0:T(8,128)(2,1)} %get-tuple-element.175), channel_id=1, source_target_pairs={{64,0},{128,64},{192,128},{256,192},{320,256},{384,320},{448,384},... | collective-permute-start | bytes 589832 | tf_op jit(solution)/shard_map/ppermute | solution.py:493
  135.9 1.2 shard_map.150
  137.1 6.1 %collective-permute-start.22 = (bf16[64,1536]{1,0:T(8,128)(2,1)}, bf16[64,1536]{1,0:T(8,128)(2,1)}, u32[]{:S(2)}, u32[]{:S(2)}) collective-permute-start(bf16[64,1536]{1,0:T(8,128)(2,1)} %get-tuple-element.174), channel_id=1, source_target_pairs={{64,0},{128,64},{192,128},{256,192},{320,256},{384,320},{448,384},... | collective-permute-start | bytes 589832 | tf_op jit(solution)/shard_map/ppermute | solution.py:493
  143.3 1.3 collective-permute-start.29
  146.4 1.3 collective-permute-start.30
  151.9 1.6 shard_map.151
  153.5 5.7 %collective-permute-start.25 = (bf16[64,1536]{1,0:T(8,128)(2,1)}, bf16[64,1536]{1,0:T(8,128)(2,1)}, u32[]{:S(2)}, u32[]{:S(2)}) collective-permute-start(bf16[64,1536]{1,0:T(8,128)(2,1)} %get-tuple-element.181), channel_id=1, source_target_pairs={{64,0},{128,64},{192,128},{256,192},{320,256},{384,320},{448,384},... | collective-permute-start | bytes 589832 | tf_op jit(solution)/shard_map/ppermute | solution.py:493
  159.2 1.6 shard_map.152
  160.9 1.9 collective-permute-start.24
  162.8 1.5 shard_map.157.held_ref
  164.3 1.3 collective-permute-start.31
  165.6 6.9 %collective-permute-done.31.moved_ref = bf16[32,1536]{1,0:T(8,128)(2,1)S(1)} collective-permute-done((bf16[32,1536]{1,0:T(8,128)(2,1)}, bf16[32,1536]{1,0:T(8,128)(2,1)S(1)}, u32[]{:S(2)}, u32[]{:S(2)}) %collective-permute-start.31) | collective-permute-done | bytes 98336 | tf_op jit(solution)/shard_map/ppermute | solution.py:431
  173.5 1.6 shard_map.159
  175.0 1.9 collective-permute-start.32
  181.2 1.6 shard_map.153
  182.9 1.8 shard_map.154
  184.6 1.3 shard_map.155
  186.0 2.4 collective-permute-start.26
  188.4 1.9 collective-permute-start.27
  190.4 2.6 collective-permute-start.33
  193.0 5.2 %collective-permute-done.33.right_ref = bf16[16,16,256]{2,1,0:T(8,128)(2,1)S(1)} collective-permute-done((bf16[16,16,256]{2,1,0:T(8,128)(2,1)S(1)}, bf16[16,16,256]{2,1,0:T(8,128)(2,1)S(1)}, u32[]{:S(2)}, u32[]{:S(2)}) %collective-permute-start.33) | collective-permute-done | bytes 131104 | tf_op jit(solution)/shard_map/ppermute | solution.py:314
  199.0 15.2 %all-to-all-start = ((bf16[16,16,256]{2,1,0:T(8,128)(2,1)}), bf16[16,16,256]{2,1,0:T(8,128)(2,1)S(1)}, u32[]{:S(2)}, u32[]{:S(2)}) async-start(bf16[16,16,256]{2,1,0:T(8,128)(2,1)} %shard_map.161), calls=%async_computation | async-start | bytes 262144 | tf_op jit(solution)/shard_map/all_to_all | solution.py:515
  214.3 2.6 collective-permute-start.28
  216.9 9.7 %collective-permute-done.28 = bf16[16,48,256]{2,1,0:T(8,128)(2,1)S(1)} collective-permute-done((bf16[16,48,256]{2,1,0:T(8,128)(2,1)S(1)}, bf16[16,48,256]{2,1,0:T(8,128)(2,1)S(1)}, u32[]{:S(2)}, u32[]{:S(2)}) %collective-permute-start.28) | collective-permute-done | bytes 393248 | tf_op jit(solution)/shard_map/ppermute | solution.py:314
  226.6 2.1 all-to-all-done
  229.6 9.6 %all-to-all-start.1 = ((bf16[16,48,256]{2,1,0:T(8,128)(2,1)}), bf16[16,48,256]{2,1,0:T(8,128)(2,1)S(1)}, u32[]{:S(2)}, u32[]{:S(2)}) async-start(bf16[16,48,256]{2,1,0:T(8,128)(2,1)} %add_convert_fusion), calls=%async_computation.1 | async-start | bytes 786432 | tf_op jit(solution)/shard_map/all_to_all | solution.py:520
  240.5 20.4 %all-to-all-done.1 = bf16[16,48,256]{2,1,0:T(8,128)(2,1)S(1)} async-done(((bf16[16,48,256]{2,1,0:T(8,128)(2,1)}), bf16[16,48,256]{2,1,0:T(8,128)(2,1)S(1)}, u32[]{:S(2)}, u32[]{:S(2)}) %all-to-all-start.1) | async-done | bytes 393248 | tf_op jit(solution)/shard_map/all_to_all | solution.py:520
  261.0 1.4 fusion
  262.5 1.3 bitcast_divide_fusion
  (107 shorter events, 31.1 us)
Async XLA Ops:
  0.6 1.0 copy-start.18
  2.3 20.6 %collective-permute-start.8 = (bf16[192,384]{1,0:T(8,128)(2,1)}, bf16[192,384]{1,0:T(8,128)(2,1)}, u32[]{:S(2)}, u32[]{:S(2)}) collective-permute-start(bf16[192,384]{1,0:T(8,128)(2,1)} %shard_map.137.refs_1_), channel_id=1, source_target_pairs={{0,64},{128,192},{256,320},{384,448},{1,65},{129,193},{257,321},{3... | collective-permute-start | bytes 442376 | tf_op jit(solution)/shard_map/ppermute | solution.py:350
  8.1 1.4 copy-start.14
  9.5 1.4 copy-start.15
  10.9 1.1 copy-start.16
  12.0 1.1 copy-start.17
  13.2 0.7 copy-start.19
  13.8 0.8 copy-start.25
  14.6 0.7 copy-start.26
  19.8 1.1 copy-start.12
  19.8 1.2 copy-start.21
  19.8 116.1 %copy-start = (bf16[1536,256]{1,0:T(8,128)(2,1)}, bf16[1536,256]{1,0:T(8,128)(2,1)S(1)}, u32[]{:S(2)}) copy-start(bf16[1536,256]{1,0:T(8,128)(2,1)S(1)} %get-tuple-element.112.refs_6_) | copy-start | bytes 2359300
  19.8 116.1 %copy-start.3 = (bf16[256,1536]{1,0:T(8,128)(2,1)}, bf16[256,1536]{1,0:T(8,128)(2,1)S(1)}, u32[]{:S(2)}) copy-start(bf16[256,1536]{1,0:T(8,128)(2,1)S(1)} %get-tuple-element.113.refs_7_) | copy-start | bytes 2359300
  19.8 116.1 %copy-start.6 = (f32[512,256]{1,0:T(8,128)}, f32[512,256]{1,0:T(8,128)S(1)}, u32[]{:S(2)}) copy-start(f32[512,256]{1,0:T(8,128)S(1)} %get-tuple-element.109.refs_3_) | copy-start | bytes 1572868
  19.8 116.1 %copy-start.9 = (f32[512,128]{1,0:T(8,128)}, f32[512,128]{1,0:T(8,128)S(1)}, u32[]{:S(2)}) copy-start(f32[512,128]{1,0:T(8,128)S(1)} %get-tuple-element.110.refs_4_) | copy-start | bytes 786436
  19.8 6.1 %copy-start.20 = (s32[4,1]{0,1:T(1,128)S(1)}, s32[4,1]{0,1:T(1,128)}, u32[]{:S(2)}) copy-start(s32[4,1]{0,1:T(1,128)} %param.11) | copy-start | bytes 52
  21.0 12.8 %collective-permute-start.1 = (bf16[64,1536]{1,0:T(8,128)(2,1)S(1)}, bf16[64,1536]{1,0:T(8,128)(2,1)S(1)}, u32[]{:S(2)}, u32[]{:S(2)}) collective-permute-start(bf16[64,1536]{1,0:T(8,128)(2,1)S(1)} %get-tuple-element.120), channel_id=1, source_target_pairs={{64,0},{128,64},{192,128},{256,192},{320,256},{384,320},{448,384},... | collective-permute-start | bytes 589832 | tf_op jit(solution)/shard_map/ppermute | solution.py:493
  23.9 20.3 %collective-permute-start.11 = (bf16[384,384]{1,0:T(8,128)(2,1)S(1)}, bf16[384,384]{1,0:T(8,128)(2,1)S(1)}, u32[]{:S(2)}, u32[]{:S(2)}) collective-permute-start(bf16[384,384]{1,0:T(8,128)(2,1)S(1)} %shard_map.138.refs_1_), channel_id=1, source_target_pairs={{448,192},{449,193},{450,194},{451,195},{452,196},{453,197},{454,1... | collective-permute-start | bytes 884744 | tf_op jit(solution)/shard_map/ppermute | solution.py:396
  24.6 19.6 %collective-permute-start.10 = (bf16[384,384]{1,0:T(8,128)(2,1)S(1)}, bf16[384,384]{1,0:T(8,128)(2,1)S(1)}, u32[]{:S(2)}, u32[]{:S(2)}) collective-permute-start(bf16[384,384]{1,0:T(8,128)(2,1)S(1)} %shard_map.138.refs_1_), channel_id=1, source_target_pairs={{320,192},{321,193},{322,194},{323,195},{324,196},{325,197},{326,1... | collective-permute-start | bytes 884744 | tf_op jit(solution)/shard_map/ppermute | solution.py:396
  25.3 18.9 %collective-permute-start.9 = (bf16[384,384]{1,0:T(8,128)(2,1)S(1)}, bf16[384,384]{1,0:T(8,128)(2,1)S(1)}, u32[]{:S(2)}, u32[]{:S(2)}) collective-permute-start(bf16[384,384]{1,0:T(8,128)(2,1)S(1)} %shard_map.138.refs_1_), channel_id=1, source_target_pairs={{64,192},{65,193},{66,194},{67,195},{68,196},{69,197},{70,198},{71... | collective-permute-start | bytes 884744 | tf_op jit(solution)/shard_map/ppermute | solution.py:396
  26.6 12.6 %collective-permute-start = (bf16[64,1536]{1,0:T(8,128)(2,1)S(1)}, bf16[64,1536]{1,0:T(8,128)(2,1)S(1)}, u32[]{:S(2)}, u32[]{:S(2)}) collective-permute-start(bf16[64,1536]{1,0:T(8,128)(2,1)S(1)} %get-tuple-element.119), channel_id=1, source_target_pairs={{64,0},{128,64},{192,128},{256,192},{320,256},{384,320},{448,384},... | collective-permute-start | bytes 589832 | tf_op jit(solution)/shard_map/ppermute | solution.py:493
  34.4 9.2 %collective-permute-start.3 = (bf16[64,1536]{1,0:T(8,128)(2,1)S(1)}, bf16[64,1536]{1,0:T(8,128)(2,1)S(1)}, u32[]{:S(2)}, u32[]{:S(2)}) collective-permute-start(bf16[64,1536]{1,0:T(8,128)(2,1)S(1)} %get-tuple-element.126), channel_id=1, source_target_pairs={{64,0},{128,64},{192,128},{256,192},{320,256},{384,320},{448,384},... | collective-permute-start | bytes 589832 | tf_op jit(solution)/shard_map/ppermute | solution.py:493
  44.2 34.0 %collective-permute-start.12 = (bf16[1536,384]{1,0:T(8,128)(2,1)S(1)}, bf16[1536,384]{1,0:T(8,128)(2,1)S(1)}, u32[]{:S(2)}, u32[]{:S(2)}) collective-permute-start(bf16[1536,384]{1,0:T(8,128)(2,1)S(1)} %shard_map.139.own_ref), channel_id=1, source_target_pairs={{192,193},{193,192},{194,195},{195,194},{196,197},{197,196},{198,1... | collective-permute-start | bytes 3538952 | tf_op jit(solution)/shard_map/ppermute | solution.py:403
  45.0 11.4 %collective-permute-start.2 = (bf16[64,1536]{1,0:T(8,128)(2,1)S(1)}, bf16[64,1536]{1,0:T(8,128)(2,1)S(1)}, u32[]{:S(2)}, u32[]{:S(2)}) collective-permute-start(bf16[64,1536]{1,0:T(8,128)(2,1)S(1)} %get-tuple-element.125), channel_id=1, source_target_pairs={{64,0},{128,64},{192,128},{256,192},{320,256},{384,320},{448,384},... | collective-permute-start | bytes 589832 | tf_op jit(solution)/shard_map/ppermute | solution.py:493
  51.1 12.6 %collective-permute-start.5 = (bf16[64,1536]{1,0:T(8,128)(2,1)S(1)}, bf16[64,1536]{1,0:T(8,128)(2,1)S(1)}, u32[]{:S(2)}, u32[]{:S(2)}) collective-permute-start(bf16[64,1536]{1,0:T(8,128)(2,1)S(1)} %get-tuple-element.132), channel_id=1, source_target_pairs={{64,0},{128,64},{192,128},{256,192},{320,256},{384,320},{448,384},... | collective-permute-start | bytes 589832 | tf_op jit(solution)/shard_map/ppermute | solution.py:493
  56.9 10.9 %collective-permute-start.4 = (bf16[64,1536]{1,0:T(8,128)(2,1)S(1)}, bf16[64,1536]{1,0:T(8,128)(2,1)S(1)}, u32[]{:S(2)}, u32[]{:S(2)}) collective-permute-start(bf16[64,1536]{1,0:T(8,128)(2,1)S(1)} %get-tuple-element.131), channel_id=1, source_target_pairs={{64,0},{128,64},{192,128},{256,192},{320,256},{384,320},{448,384},... | collective-permute-start | bytes 589832 | tf_op jit(solution)/shard_map/ppermute | solution.py:493
  65.0 13.9 %collective-permute-start.13 = (bf16[64,1536]{1,0:T(8,128)(2,1)S(1)}, bf16[64,1536]{1,0:T(8,128)(2,1)S(1)}, u32[]{:S(2)}, u32[]{:S(2)}) collective-permute-start(bf16[64,1536]{1,0:T(8,128)(2,1)S(1)} %get-tuple-element.145), channel_id=1, source_target_pairs={{64,0},{128,64},{192,128},{256,192},{320,256},{384,320},{448,384},... | collective-permute-start | bytes 589832 | tf_op jit(solution)/shard_map/ppermute | solution.py:493
  67.8 10.5 %copy-start.27 = (s32[4,1]{0,1:T(1,128)S(1)}, s32[4,1]{0,1:T(1,128)}, u32[]{:S(2)}) copy-start(s32[4,1]{0,1:T(1,128)} %param.12) | copy-start | bytes 52
  69.1 19.5 %collective-permute-start.6 = (bf16[64,1536]{1,0:T(8,128)(2,1)S(1)}, bf16[64,1536]{1,0:T(8,128)(2,1)S(1)}, u32[]{:S(2)}, u32[]{:S(2)}) collective-permute-start(bf16[64,1536]{1,0:T(8,128)(2,1)S(1)} %get-tuple-element.137), channel_id=1, source_target_pairs={{64,0},{128,64},{192,128},{256,192},{320,256},{384,320},{448,384},... | collective-permute-start | bytes 589832 | tf_op jit(solution)/shard_map/ppermute | solution.py:493
  74.6 3.7 %collective-permute-start.7 = (f32[8,1536]{1,0:T(8,128)S(1)}, f32[8,1536]{1,0:T(8,128)S(1)}, u32[]{:S(2)}, u32[]{:S(2)}) collective-permute-start(f32[8,1536]{1,0:T(8,128)S(1)} %get-tuple-element.140), channel_id=1, source_target_pairs={{256,192},{257,193},{258,194},{259,195},{260,196},{261,197},{262,1... | collective-permute-start | bytes 147464 | tf_op jit(solution)/shard_map/ppermute | solution.py:398
  78.8 64.4 %copy-start.23 = (bf16[32,1536]{1,0:T(8,128)(2,1)}, bf16[32,1536]{1,0:T(8,128)(2,1)S(1)}, u32[]{:S(2)}) copy-start(bf16[32,1536]{1,0:T(8,128)(2,1)S(1)} %get-tuple-element.198.held_ref) | copy-start | bytes 294916
  80.1 13.1 %collective-permute-start.15 = (bf16[64,1536]{1,0:T(8,128)(2,1)S(1)}, bf16[64,1536]{1,0:T(8,128)(2,1)S(1)}, u32[]{:S(2)}, u32[]{:S(2)}) collective-permute-start(bf16[64,1536]{1,0:T(8,128)(2,1)S(1)} %get-tuple-element.151), channel_id=1, source_target_pairs={{64,0},{128,64},{192,128},{256,192},{320,256},{384,320},{448,384},... | collective-permute-start | bytes 589832 | tf_op jit(solution)/shard_map/ppermute | solution.py:493
  89.8 11.5 %collective-permute-start.14 = (bf16[64,1536]{1,0:T(8,128)(2,1)S(1)}, bf16[64,1536]{1,0:T(8,128)(2,1)S(1)}, u32[]{:S(2)}, u32[]{:S(2)}) collective-permute-start(bf16[64,1536]{1,0:T(8,128)(2,1)S(1)} %get-tuple-element.150), channel_id=1, source_target_pairs={{64,0},{128,64},{192,128},{256,192},{320,256},{384,320},{448,384},... | collective-permute-start | bytes 589832 | tf_op jit(solution)/shard_map/ppermute | solution.py:493
  94.5 10.7 %collective-permute-start.17 = (bf16[64,1536]{1,0:T(8,128)(2,1)S(1)}, bf16[64,1536]{1,0:T(8,128)(2,1)S(1)}, u32[]{:S(2)}, u32[]{:S(2)}) collective-permute-start(bf16[64,1536]{1,0:T(8,128)(2,1)S(1)} %get-tuple-element.157), channel_id=1, source_target_pairs={{64,0},{128,64},{192,128},{256,192},{320,256},{384,320},{448,384},... | collective-permute-start | bytes 589832 | tf_op jit(solution)/shard_map/ppermute | solution.py:493
  102.6 10.7 %collective-permute-start.16 = (bf16[64,1536]{1,0:T(8,128)(2,1)S(1)}, bf16[64,1536]{1,0:T(8,128)(2,1)S(1)}, u32[]{:S(2)}, u32[]{:S(2)}) collective-permute-start(bf16[64,1536]{1,0:T(8,128)(2,1)S(1)} %get-tuple-element.156), channel_id=1, source_target_pairs={{64,0},{128,64},{192,128},{256,192},{320,256},{384,320},{448,384},... | collective-permute-start | bytes 589832 | tf_op jit(solution)/shard_map/ppermute | solution.py:493
  106.4 11.1 %collective-permute-start.19 = (bf16[64,1536]{1,0:T(8,128)(2,1)S(1)}, bf16[64,1536]{1,0:T(8,128)(2,1)S(1)}, u32[]{:S(2)}, u32[]{:S(2)}) collective-permute-start(bf16[64,1536]{1,0:T(8,128)(2,1)S(1)} %get-tuple-element.163), channel_id=1, source_target_pairs={{64,0},{128,64},{192,128},{256,192},{320,256},{384,320},{448,384},... | collective-permute-start | bytes 589832 | tf_op jit(solution)/shard_map/ppermute | solution.py:493
  114.5 10.2 %collective-permute-start.18 = (bf16[64,1536]{1,0:T(8,128)(2,1)S(1)}, bf16[64,1536]{1,0:T(8,128)(2,1)S(1)}, u32[]{:S(2)}, u32[]{:S(2)}) collective-permute-start(bf16[64,1536]{1,0:T(8,128)(2,1)S(1)} %get-tuple-element.162), channel_id=1, source_target_pairs={{64,0},{128,64},{192,128},{256,192},{320,256},{384,320},{448,384},... | collective-permute-start | bytes 589832 | tf_op jit(solution)/shard_map/ppermute | solution.py:493
  118.3 12.1 %collective-permute-start.21 = (bf16[64,1536]{1,0:T(8,128)(2,1)S(1)}, bf16[64,1536]{1,0:T(8,128)(2,1)S(1)}, u32[]{:S(2)}, u32[]{:S(2)}) collective-permute-start(bf16[64,1536]{1,0:T(8,128)(2,1)S(1)} %get-tuple-element.169), channel_id=1, source_target_pairs={{64,0},{128,64},{192,128},{256,192},{320,256},{384,320},{448,384},... | collective-permute-start | bytes 589832 | tf_op jit(solution)/shard_map/ppermute | solution.py:493
  125.2 10.6 %collective-permute-start.20 = (bf16[64,1536]{1,0:T(8,128)(2,1)S(1)}, bf16[64,1536]{1,0:T(8,128)(2,1)S(1)}, u32[]{:S(2)}, u32[]{:S(2)}) collective-permute-start(bf16[64,1536]{1,0:T(8,128)(2,1)S(1)} %get-tuple-element.168), channel_id=1, source_target_pairs={{64,0},{128,64},{192,128},{256,192},{320,256},{384,320},{448,384},... | collective-permute-start | bytes 589832 | tf_op jit(solution)/shard_map/ppermute | solution.py:493
  131.6 16.0 %collective-permute-start.23 = (bf16[64,1536]{1,0:T(8,128)(2,1)}, bf16[64,1536]{1,0:T(8,128)(2,1)}, u32[]{:S(2)}, u32[]{:S(2)}) collective-permute-start(bf16[64,1536]{1,0:T(8,128)(2,1)} %get-tuple-element.175), channel_id=1, source_target_pairs={{64,0},{128,64},{192,128},{256,192},{320,256},{384,320},{448,384},... | collective-permute-start | bytes 589832 | tf_op jit(solution)/shard_map/ppermute | solution.py:493
  137.1 22.1 %collective-permute-start.22 = (bf16[64,1536]{1,0:T(8,128)(2,1)}, bf16[64,1536]{1,0:T(8,128)(2,1)}, u32[]{:S(2)}, u32[]{:S(2)}) collective-permute-start(bf16[64,1536]{1,0:T(8,128)(2,1)} %get-tuple-element.174), channel_id=1, source_target_pairs={{64,0},{128,64},{192,128},{256,192},{320,256},{384,320},{448,384},... | collective-permute-start | bytes 589832 | tf_op jit(solution)/shard_map/ppermute | solution.py:493
  143.3 1.3 collective-permute-start.29
  144.6 0.9 copy-start.24
  146.4 16.4 %collective-permute-start.30 = (bf16[32,1536]{1,0:T(8,128)(2,1)S(1)}, bf16[32,1536]{1,0:T(8,128)(2,1)}, u32[]{:S(2)}, u32[]{:S(2)}) collective-permute-start(bf16[32,1536]{1,0:T(8,128)(2,1)S(1)} %shard_map.156.held_ref), channel_id=1, source_target_pairs={{192,64},{448,320},{193,65},{449,321},{194,66},{450,322},{195,67},... | collective-permute-start | bytes 294920 | tf_op jit(solution)/shard_map/ppermute | solution.py:431
  147.7 1.1 copy-start.1
  148.8 1.1 copy-start.4
  149.9 1.0 copy-start.7
  151.0 0.9 copy-start.10
  153.5 23.4 %collective-permute-start.25 = (bf16[64,1536]{1,0:T(8,128)(2,1)}, bf16[64,1536]{1,0:T(8,128)(2,1)}, u32[]{:S(2)}, u32[]{:S(2)}) collective-permute-start(bf16[64,1536]{1,0:T(8,128)(2,1)} %get-tuple-element.181), channel_id=1, source_target_pairs={{64,0},{128,64},{192,128},{256,192},{320,256},{384,320},{448,384},... | collective-permute-start | bytes 589832 | tf_op jit(solution)/shard_map/ppermute | solution.py:493
  160.9 22.0 %collective-permute-start.24 = (bf16[64,1536]{1,0:T(8,128)(2,1)}, bf16[64,1536]{1,0:T(8,128)(2,1)}, u32[]{:S(2)}, u32[]{:S(2)}) collective-permute-start(bf16[64,1536]{1,0:T(8,128)(2,1)} %get-tuple-element.180), channel_id=1, source_target_pairs={{64,0},{128,64},{192,128},{256,192},{320,256},{384,320},{448,384},... | collective-permute-start | bytes 589832 | tf_op jit(solution)/shard_map/ppermute | solution.py:493
  164.3 8.2 %collective-permute-start.31 = (bf16[32,1536]{1,0:T(8,128)(2,1)}, bf16[32,1536]{1,0:T(8,128)(2,1)S(1)}, u32[]{:S(2)}, u32[]{:S(2)}) collective-permute-start(bf16[32,1536]{1,0:T(8,128)(2,1)} %shard_map.157.held_ref), channel_id=1, source_target_pairs={{64,0},{192,128},{320,256},{448,384},{65,1},{193,129},{321,257},{4... | collective-permute-start | bytes 294920 | tf_op jit(solution)/shard_map/ppermute | solution.py:431
  175.0 15.3 %collective-permute-start.32 = (bf16[2,16,16,256]{3,2,1,0:T(8,128)(2,1)S(1)}, bf16[2,16,16,256]{3,2,1,0:T(8,128)(2,1)S(1)}, u32[]{:S(2)}, u32[]{:S(2)}) collective-permute-start(bf16[2,16,16,256]{3,2,1,0:T(8,128)(2,1)S(1)} %get-tuple-element.203), channel_id=1, source_target_pairs={{0,1},{1,0},{2,3},{3,2},{4,5},{5,4},{6,7},{7,6},{8,9},{9,8},{10,11... | collective-permute-start | bytes 786440 | tf_op jit(solution)/shard_map/ppermute | solution.py:314
  177.0 1.1 copy-start.2
  178.1 1.1 copy-start.5
  179.2 1.0 copy-start.8
  180.3 0.9 copy-start.11
  182.9 1.8 copy-start.13
  182.9 1.8 copy-start.22
  186.0 12.9 %collective-permute-start.26 = (bf16[16,48,256]{2,1,0:T(8,128)(2,1)S(1)}, bf16[16,48,256]{2,1,0:T(8,128)(2,1)S(1)}, u32[]{:S(2)}, u32[]{:S(2)}) collective-permute-start(bf16[16,48,256]{2,1,0:T(8,128)(2,1)S(1)} %get-tuple-element.190), channel_id=1, source_target_pairs={{0,1},{1,0},{2,3},{3,2},{4,5},{5,4},{6,7},{7,6},{8,9},{9,8},{10,11... | collective-permute-start | bytes 1179656 | tf_op jit(solution)/shard_map/ppermute | solution.py:314
  188.4 25.8 %collective-permute-start.27 = (bf16[16,48,256]{2,1,0:T(8,128)(2,1)S(1)}, bf16[16,48,256]{2,1,0:T(8,128)(2,1)S(1)}, u32[]{:S(2)}, u32[]{:S(2)}) collective-permute-start(bf16[16,48,256]{2,1,0:T(8,128)(2,1)S(1)} %get-tuple-element.192), channel_id=1, source_target_pairs={{0,1},{1,0},{2,3},{3,2},{4,5},{5,4},{6,7},{7,6},{8,9},{9,8},{10,11... | collective-permute-start | bytes 1179656 | tf_op jit(solution)/shard_map/ppermute | solution.py:314
  190.4 7.8 %collective-permute-start.33 = (bf16[16,16,256]{2,1,0:T(8,128)(2,1)S(1)}, bf16[16,16,256]{2,1,0:T(8,128)(2,1)S(1)}, u32[]{:S(2)}, u32[]{:S(2)}) collective-permute-start(bf16[16,16,256]{2,1,0:T(8,128)(2,1)S(1)} %get-tuple-element.206), channel_id=1, source_target_pairs={{0,32},{32,0},{1,33},{33,1},{2,34},{34,2},{3,35},{35,3},{4,36},{36... | collective-permute-start | bytes 393224 | tf_op jit(solution)/shard_map/ppermute | solution.py:314
  199.0 29.7 %all-to-all-start = ((bf16[16,16,256]{2,1,0:T(8,128)(2,1)}), bf16[16,16,256]{2,1,0:T(8,128)(2,1)S(1)}, u32[]{:S(2)}, u32[]{:S(2)}) async-start(bf16[16,16,256]{2,1,0:T(8,128)(2,1)} %shard_map.161), calls=%async_computation | async-start | bytes 262144 | tf_op jit(solution)/shard_map/all_to_all | solution.py:515
  214.3 12.3 %collective-permute-start.28 = (bf16[16,48,256]{2,1,0:T(8,128)(2,1)S(1)}, bf16[16,48,256]{2,1,0:T(8,128)(2,1)S(1)}, u32[]{:S(2)}, u32[]{:S(2)}) collective-permute-start(bf16[16,48,256]{2,1,0:T(8,128)(2,1)S(1)} %add_convert_fusion.1), channel_id=1, source_target_pairs={{0,32},{32,0},{1,33},{33,1},{2,34},{34,2},{3,35},{35,3},{4,36},{36... | collective-permute-start | bytes 1179656 | tf_op jit(solution)/shard_map/ppermute | solution.py:314
  229.6 31.4 %all-to-all-start.1 = ((bf16[16,48,256]{2,1,0:T(8,128)(2,1)}), bf16[16,48,256]{2,1,0:T(8,128)(2,1)S(1)}, u32[]{:S(2)}, u32[]{:S(2)}) async-start(bf16[16,48,256]{2,1,0:T(8,128)(2,1)} %add_convert_fusion), calls=%async_computation.1 | async-start | bytes 786432 | tf_op jit(solution)/shard_map/all_to_all | solution.py:520

commit v3 on v2

--- a/solution.py
+++ b/solution.py
@@ -12,13 +12,13 @@
 REVERSAL = 0.5
 SECTIONS = 8
 CHUNK = 64
+STAY = [2, 3, 4, 6, 7]
 DELAY = 2
 SEC = ("x", "yh")
 F32 = jnp.float32
 BF16 = jnp.bfloat16
 VM = pl.BlockSpec(memory_space=pltpu.VMEM)
 SM = pl.BlockSpec(memory_space=pltpu.SMEM)
-HB = pl.BlockSpec(memory_space=pltpu.MemorySpace.HBM)
 
 
 def silu_slope(pre_act):
@@ -39,35 +39,24 @@
     )(*args)
 
 
-def half_kernel(core_ref, first_ref, mine_ref, sem):
+def half_kernel(core_ref, first_ref, mine_ref):
     half = mine_ref.shape[1]
-    columns = pl.ds(pl.multiple_of(core_ref[0] * half, 128), half)
-    copy = pltpu.make_async_copy(first_ref.at[:, columns], mine_ref, sem)
-    copy.start()
-    copy.wait()
-
-
-def prepare_kernel(lens_ref, *refs):
-    sources, refs = refs[:6], refs[6:]
-    x_ref, top_ref, gain_ref, second_ref, xn_ref, h_ref, a_ref, q_ref, pooled_ref, wut_ref, wdt_ref, _, _ = refs[:13]
-    wd_ref, wu_ref, sems = refs[13:]
-    x_hbm, top_hbm, gain_hbm, second_hbm, wd_hbm, wu_hbm = sources
+    for c in range(2):
+
+        @pl.when(core_ref[0] == c)
+        def _():
+            mine_ref[...] = first_ref[:, c * half : (c + 1) * half]
+
+
+def prepare_kernel(lens_ref, _yl, x_ref, gain_ref, wd_ref, wu_ref, *refs):
+    xn_ref, h_ref, a_ref, q_ref, pooled_ref, wut_ref, wdt_ref, _, _ = refs
     micros, seq_len = 4, 128
-    pairs = [(wd_hbm, wd_ref), (gain_hbm, gain_ref), (wu_hbm, wu_ref), (second_hbm, second_ref), (top_hbm, top_ref)]
-    for m in range(micros):
-        rows = slice(m * seq_len, (m + 1) * seq_len)
-        pairs.append((x_hbm.at[rows], x_ref.at[rows]))
-    copies = [pltpu.make_async_copy(source, target, sems.at[i]) for i, (source, target) in enumerate(pairs)]
-    for i in (0, 1, 5, 6, 7, 8, 2, 3, 4):
-        copies[i].start()
-    copies[0].wait()
-    copies[1].wait()
     gain = gain_ref[0:1, :]
+    wut_ref[...] = wu_ref[...].T
     wdt_ref[...] = wd_ref[...].T
     pooled_ref[...] = jnp.zeros_like(pooled_ref)
     positions = lax.broadcasted_iota(jnp.int32, (seq_len, 1), 0)
     for m in range(micros):
-        copies[5 + m].wait()
         rows = pl.ds(m * seq_len, seq_len)
         values = x_ref[rows, :].astype(F32)
         count = lens_ref[m]
@@ -80,10 +69,6 @@
         a_ref[rows, :] = a
         h_ref[rows, :] = (a * jax.nn.sigmoid(a)).astype(BF16)
         q_ref[rows, :] = jnp.broadcast_to(q, (seq_len, 128))
-    copies[2].wait()
-    wut_ref[...] = wu_ref[...].T
-    copies[3].wait()
-    copies[4].wait()
 
 
 def step_kernel(step, chunks, has_top, has_in, has_rev, *refs):
@@ -93,7 +78,7 @@
     top_ref = refs.pop(0) if has_top else None
     in_ref = refs.pop(0) if has_in else None
     rev_ref = refs.pop(0) if has_rev else None
-    _, _, out_ref, g_ref, da_ref = refs
+    out_ref, g_ref, da_ref = refs[2:5]
     features = x_ref.shape[1]
     sec = sec_ref[0]
     place = step - DELAY * (SECTIONS - 1 - sec)
@@ -260,16 +245,22 @@
         other_ref[...] = plus(kept_ref[1], got_ref[1])
 
 
+def copy_kernel(source_ref, out_ref):
+    out_ref[...] = source_ref[...]
+
+
 def add_kernel(left_ref, right_ref, out_ref):
     out_ref[...] = plus(left_ref[...], right_ref[...])
 
 
-def pick_kernel(flag_ref, moved_ref, held_ref, out_ref):
-    @pl.when(flag_ref[0] != 0)
+def pick_kernel(targets, sec_ref, moved_ref, held_ref, out_ref):
+    gets = functools.reduce(jnp.logical_or, [sec_ref[0] == target for target in targets])
+
+    @pl.when(gets)
     def _():
         out_ref[...] = moved_ref[...]
 
-    @pl.when(flag_ref[0] == 0)
+    @pl.when(jnp.logical_not(gets))
     def _():
         out_ref[...] = held_ref[...]
 
@@ -333,6 +324,7 @@
     wd = w_down[0]
     sec_s = sec.reshape(1).astype(jnp.int32)
     core_s = core.reshape(1).astype(jnp.int32)
+    yl_s = lax.axis_index("yl").reshape(1).astype(jnp.int32)
     channels = critic_first.shape[1]
     half = channels // 2
     sds = jax.ShapeDtypeStruct
@@ -341,21 +333,16 @@
     mine = call(
         half_kernel,
         sds((critic_first.shape[0], half), BF16),
-        [SM, HB],
+        [SM, VM],
         (core_s, critic_first),
         0,
         1 << 19,
-        scratch=[pltpu.SemaphoreType.DMA], limit=16,
     )
     even = lax.ppermute(mine, SEC, [(i, i + 1) for i in range(0, SECTIONS, 2)])
-    languages = critic_second.shape[1]
-    x, top, gain_v, second, xn, h, a, q, pooled, wut, wdt, grads, inner = call(
+    second = critic_second.T
+    xn, h, a, q, pooled, wut, wdt, grads, inner = call(
         prepare_kernel,
         (
-            sds((rows, features), BF16),
-            sds((rows, features), BF16),
-            sds((1, features), F32),
-            sds((languages, channels), BF16),
             sds((rows, features), BF16),
             sds((rows, rank), BF16),
             sds((rows, rank), F32),
@@ -366,16 +353,14 @@
             sds((rows, features), BF16),
             sds((rows, rank), BF16),
         ),
-        [SM] + [HB] * 6,
-        (lens, x, top, gain, critic_second.T, wd, w_up[0]),
+        [SM, SM] + [VM] * 4,
+        (lens, yl_s, x, gain, wd, w_up[0]),
         2 * rows * features * rank,
         8 << 20,
-        scratch=[pltpu.VMEM((features, rank), BF16), pltpu.VMEM((rank, features), BF16), pltpu.SemaphoreType.DMA((9,))], limit=16,
     )
 
     three = SECTIONS // 2 - 1
     held = {}
-    yl_s = lax.axis_index("yl").reshape(1).astype(jnp.int32)
     band_rows = critic_first.shape[0]
     share = channels // n_dp
     padded = -(-share // 16) * 16
@@ -423,13 +408,13 @@
         elif step in (8, 10, 12):
             lines = after(held["lines"], token)
             if step == 8:
-                route, gets = [(3, 7)], sec == 7
+                route = [(3, 7)]
             elif step == 10:
-                route, gets = [(3, 1), (7, 5)], (sec == 1) | (sec == 5)
+                route = [(3, 1), (7, 5)]
             else:
-                route, gets = [(i + 1, i) for i in range(0, SECTIONS, 2)], sec % 2 == 0
+                route = [(i + 1, i) for i in range(0, SECTIONS, 2)]
             moved = lax.ppermute(lines, SEC, route)
-            held["moved"] = (gets.astype(jnp.int32).reshape(1), moved)
+            held["moved"] = ([target for _, target in route], moved)
         elif step == 14:
             kept, sent = call(
                 functools.partial(critic_sums_kernel, band_rows, parts),
@@ -444,7 +429,9 @@
             held["got"] = swap(sent, "c", n_c)
         elif step == 16:
             one = sds((n_z, padded, rank), BF16)
-            own, other = call(split_kernel, (one, one), [VM, VM], (after(held["kept"], token), held["got"]), 0, 1 << 20)
+            own, other = call(
+                split_kernel, (one, one), [VM, VM], (after(held["kept"], token), held["got"]), 0, 1 << 20
+            )
             held["own_sum"] = own
             if n_yl == 2:
                 held["other_sum"] = swap(other, "yl", n_yl)
@@ -452,25 +439,25 @@
             args = (after(held["own_sum"], token), held["other_sum"])
             held["own_sum"] = call(add_kernel, sds(args[0].shape, BF16), [VM, VM], args, 0, 1 << 20)
         if step in (9, 11, 13):
-            flag, moved = held.pop("moved")
+            targets, moved = held.pop("moved")
             held["lines"] = call(
-                pick_kernel,
+                functools.partial(pick_kernel, targets),
                 sds(held["lines"].shape, BF16),
                 [SM, VM, VM],
-                (after(flag, token), moved, held["lines"]),
+                (after(sec_s, token), moved, held["lines"]),
                 0,
                 1 << 18,
             )
 
     steps = DELAY * (SECTIONS - 1) + chunks
     received = {}
-    route = [(i, i - 1) for i in range(1, SECTIONS)]
+    relay_route = [(i, i - 1) for i in range(1, SECTIONS)]
     for step in range(steps):
         has_top = step < chunks
         has_in = step >= DELAY
         first_rev = DELAY * (SECTIONS - 1 - three)
         has_rev = first_rev <= step < first_rev + chunks
-        args = [sec_s, lens, x, a, q, gain_v, wut, wdt]
+        args = [sec_s, lens, x, a, q, gain, wut, wdt]
         specs = [SM, SM] + [VM] * 6
         if has_top:
             args.append(top)
@@ -480,17 +467,19 @@
             args.append(held["rev"])
         args += [grads, inner]
         specs += [VM] * (len(args) - len(specs))
-        outgoing, grads, inner = call(
+        passed = [len(args) - 2, len(args) - 1] + STAY
+        outgoing, grads, inner, *stay = call(
             functools.partial(step_kernel, step, chunks, has_top, has_in, has_rev),
-            (sds((CHUNK, features), BF16), sds((rows, features), BF16), sds((rows, rank), BF16)),
+            (sds((CHUNK, features), BF16),) + tuple(sds(args[i].shape, args[i].dtype) for i in passed),
             specs,
             tuple(args),
             4 * CHUNK * features * rank,
             3 << 20,
-            aliases={len(args) - 2: 1, len(args) - 1: 2},
+            aliases={i: k + 1 for k, i in enumerate(passed)},
         )
+        x, a, q, wut, wdt = stay
         if step < steps - DELAY:
-            received[step] = lax.ppermute(outgoing, SEC, route)
+            received[step] = lax.ppermute(outgoing, SEC, relay_route)
         side_work(step, outgoing)
 
     span = features // n_dp
@@ -510,11 +499,13 @@
     for i in reversed(range(n_yl)):
         halves[i] = plus(kept[i], swap(sent[i], "c", n_c))
     summed = halves[0]
-    crit = after(held["own_sum"], summed)
+    crit = held["own_sum"]
+    if n_yl == 2:
+        moved = swap(halves[1], "yl", n_yl)
+        crit = call(copy_kernel, sds(crit.shape, BF16), [VM], (after(crit, halves[1]),), 0, 1 << 18)
     if n_z > 1:
         crit = lax.all_to_all(crit, "z", 0, 0, tiled=True)
     if n_yl == 2:
-        moved = swap(halves[1], "yl", n_yl)
         summed = plus(summed, after(moved, crit))
     if n_z > 1:
         summed = lax.all_to_all(summed, "z", 0, 0, tiled=True)

time: 266 us -> 234 us (0.88)
  the two profiles are of different devices: /device:TPU:4 before, /device:TPU:68 now
where the time goes in v3:
time: 234 us; the launch traced here: 232 us
  starting transfers between devices  146 us (62%)
  waiting for transfers between devices  53 us (23%)
  Pallas kernels  25.7 us (11%)
  local copies, waits for them, and re-layouts  3.8 us (2%)
  other arithmetic  2.41 us (1%)
    ppermute x20, starting transfers between devices, whole(): received[step] = lax.ppermute(outgoing, SEC, relay_route)  96.6 us
    pallas_call x35, Pallas kernels, call(): pl.pallas_call(kernel, out_shape=out_shape, in_specs=in_specs, out_specs=...  25.7 us
    all_to_all x1, waiting for transfers between devices, whole(): summed = lax.all_to_all(summed, 'z', 0, 0, tiled=True)  20.6 us
    all_to_all x1, starting transfers between devices, whole(): crit = lax.all_to_all(crit, 'z', 0, 0, tiled=True)  14.8 us
    ppermute x5, waiting for transfers between devices, swap(): return lax.ppermute(block, axis, [(i, size - 1 - i) for i in range(size)])  11.7 us
    ppermute x5, starting transfers between devices, swap(): return lax.ppermute(block, axis, [(i, size - 1 - i) for i in range(size)])  11.4 us
    ppermute x20, waiting for transfers between devices, whole(): received[step] = lax.ppermute(outgoing, SEC, relay_route)  11.1 us
    all_to_all x1, starting transfers between devices, whole(): summed = lax.all_to_all(summed, 'z', 0, 0, tiled=True)  10.9 us
  transfers between devices with their start and end apart: 36, of which 12 were waited for; matrix products, arithmetic and copies ran while one was open for 1% of the time, Pallas kernels for 11%

profile of v3, /device:TPU:68, one launch (start us, length us, event | category | flops | bytes accessed | tf_op | source)
XLA Modules:
  0.0 232.5 jit_solution(9882359558180762576)
XLA Ops:
  0.7 1.5 copy.323
  2.2 1.0 copy-done.4
  3.2 5.1 %collective-permute-start.8 = (bf16[192,384]{1,0:T(8,128)(2,1)S(1)}, bf16[192,384]{1,0:T(8,128)(2,1)S(1)}, u32[]{:S(2)}, u32[]{:S(2)}) collective-permute-start(bf16[192,384]{1,0:T(8,128)(2,1)S(1)} %shard_map.137.refs_1_), channel_id=1, source_target_pairs={{0,64},{128,192},{256,320},{384,448},{1,65},{129,193},{257,321},{3... | collective-permute-start | bytes 442376 | tf_op jit(solution)/shard_map/ppermute | solution.py:341
  8.4 1.9 shard_map.128
  10.9 1.9 collective-permute-start
  12.8 0.7 collective-permute-start.11
  13.5 0.7 collective-permute-start.10
  14.2 0.7 collective-permute-start.9
  15.5 7.3 %collective-permute-start.1 = (bf16[64,1536]{1,0:T(8,128)(2,1)S(1)}, bf16[64,1536]{1,0:T(8,128)(2,1)S(1)}, u32[]{:S(2)}, u32[]{:S(2)}) collective-permute-start(bf16[64,1536]{1,0:T(8,128)(2,1)S(1)} %get-tuple-element.235), channel_id=1, source_target_pairs={{64,0},{128,64},{192,128},{256,192},{320,256},{384,320},{448,384},... | collective-permute-start | bytes 589832 | tf_op jit(solution)/shard_map/ppermute | solution.py:482
  23.3 1.9 collective-permute-start.2
  25.3 2.7 %collective-permute-done.1.refs_9_ = bf16[64,1536]{1,0:T(8,128)(2,1)S(1)} collective-permute-done((bf16[64,1536]{1,0:T(8,128)(2,1)S(1)}, bf16[64,1536]{1,0:T(8,128)(2,1)S(1)}, u32[]{:S(2)}, u32[]{:S(2)}) %collective-permute-start.1) | collective-permute-done | bytes 196640 | tf_op jit(solution)/shard_map/ppermute | solution.py:482
  28.6 4.0 %collective-permute-done.2.refs_9_ = bf16[64,1536]{1,0:T(8,128)(2,1)S(1)} collective-permute-done((bf16[64,1536]{1,0:T(8,128)(2,1)S(1)}, bf16[64,1536]{1,0:T(8,128)(2,1)S(1)}, u32[]{:S(2)}, u32[]{:S(2)}) %collective-permute-start.2) | collective-permute-done | bytes 196640 | tf_op jit(solution)/shard_map/ppermute | solution.py:482
  33.2 0.7 collective-permute-start.12
  33.9 6.1 %collective-permute-start.3 = (bf16[64,1536]{1,0:T(8,128)(2,1)S(1)}, bf16[64,1536]{1,0:T(8,128)(2,1)S(1)}, u32[]{:S(2)}, u32[]{:S(2)}) collective-permute-start(bf16[64,1536]{1,0:T(8,128)(2,1)S(1)} %get-tuple-element.251), channel_id=1, source_target_pairs={{64,0},{128,64},{192,128},{256,192},{320,256},{384,320},{448,384},... | collective-permute-start | bytes 589832 | tf_op jit(solution)/shard_map/ppermute | solution.py:482
  40.0 3.2 %collective-permute-start.4 = (bf16[64,1536]{1,0:T(8,128)(2,1)S(1)}, bf16[64,1536]{1,0:T(8,128)(2,1)S(1)}, u32[]{:S(2)}, u32[]{:S(2)}) collective-permute-start(bf16[64,1536]{1,0:T(8,128)(2,1)S(1)} %get-tuple-element.259), channel_id=1, source_target_pairs={{64,0},{128,64},{192,128},{256,192},{320,256},{384,320},{448,384},... | collective-permute-start | bytes 589832 | tf_op jit(solution)/shard_map/ppermute | solution.py:482
  43.2 2.0 collective-permute-done.3.refs_9_
  45.8 6.8 %collective-permute-start.5 = (bf16[64,1536]{1,0:T(8,128)(2,1)S(1)}, bf16[64,1536]{1,0:T(8,128)(2,1)S(1)}, u32[]{:S(2)}, u32[]{:S(2)}) collective-permute-start(bf16[64,1536]{1,0:T(8,128)(2,1)S(1)} %get-tuple-element.267), channel_id=1, source_target_pairs={{64,0},{128,64},{192,128},{256,192},{320,256},{384,320},{448,384},... | collective-permute-start | bytes 589832 | tf_op jit(solution)/shard_map/ppermute | solution.py:482
  52.6 1.2 shard_map.135
  53.9 2.5 %collective-permute-start.6 = (bf16[64,1536]{1,0:T(8,128)(2,1)S(1)}, bf16[64,1536]{1,0:T(8,128)(2,1)S(1)}, u32[]{:S(2)}, u32[]{:S(2)}) collective-permute-start(bf16[64,1536]{1,0:T(8,128)(2,1)S(1)} %get-tuple-element.275), channel_id=1, source_target_pairs={{64,0},{128,64},{192,128},{256,192},{320,256},{384,320},{448,384},... | collective-permute-start | bytes 589832 | tf_op jit(solution)/shard_map/ppermute | solution.py:482
  56.7 1.2 shard_map.136
  58.0 5.5 %collective-permute-start.13 = (bf16[64,1536]{1,0:T(8,128)(2,1)S(1)}, bf16[64,1536]{1,0:T(8,128)(2,1)S(1)}, u32[]{:S(2)}, u32[]{:S(2)}) collective-permute-start(bf16[64,1536]{1,0:T(8,128)(2,1)S(1)} %get-tuple-element.276), channel_id=1, source_target_pairs={{64,0},{128,64},{192,128},{256,192},{320,256},{384,320},{448,384},... | collective-permute-start | bytes 589832 | tf_op jit(solution)/shard_map/ppermute | solution.py:482
  63.5 1.9 collective-permute-start.7
  65.4 1.8 collective-permute-done.7.pooled_ref
  67.8 1.2 shard_map.141
  69.0 8.4 %collective-permute-start.14 = (bf16[64,1536]{1,0:T(8,128)(2,1)S(1)}, bf16[64,1536]{1,0:T(8,128)(2,1)S(1)}, u32[]{:S(2)}, u32[]{:S(2)}) collective-permute-start(bf16[64,1536]{1,0:T(8,128)(2,1)S(1)} %get-tuple-element.297), channel_id=1, source_target_pairs={{64,0},{128,64},{192,128},{256,192},{320,256},{384,320},{448,384},... | collective-permute-start | bytes 589832 | tf_op jit(solution)/shard_map/ppermute | solution.py:482
  77.5 1.2 shard_map.142
  78.7 2.0 collective-permute-start.15
  80.7 1.5 collective-permute-done.14.refs_8_
  82.2 1.2 shard_map.143
  83.4 6.8 %collective-permute-start.16 = (bf16[64,1536]{1,0:T(8,128)(2,1)S(1)}, bf16[64,1536]{1,0:T(8,128)(2,1)S(1)}, u32[]{:S(2)}, u32[]{:S(2)}) collective-permute-start(bf16[64,1536]{1,0:T(8,128)(2,1)S(1)} %get-tuple-element.313), channel_id=1, source_target_pairs={{64,0},{128,64},{192,128},{256,192},{320,256},{384,320},{448,384},... | collective-permute-start | bytes 589832 | tf_op jit(solution)/shard_map/ppermute | solution.py:482
  90.3 1.2 shard_map.144
  91.5 2.0 collective-permute-start.17
  94.1 1.2 shard_map.145
  95.3 6.8 %collective-permute-start.18 = (bf16[64,1536]{1,0:T(8,128)(2,1)S(1)}, bf16[64,1536]{1,0:T(8,128)(2,1)S(1)}, u32[]{:S(2)}, u32[]{:S(2)}) collective-permute-start(bf16[64,1536]{1,0:T(8,128)(2,1)S(1)} %get-tuple-element.329), channel_id=1, source_target_pairs={{64,0},{128,64},{192,128},{256,192},{320,256},{384,320},{448,384},... | collective-permute-start | bytes 589832 | tf_op jit(solution)/shard_map/ppermute | solution.py:482
  102.2 1.2 shard_map.146
  103.4 3.0 %collective-permute-start.19 = (bf16[64,1536]{1,0:T(8,128)(2,1)S(1)}, bf16[64,1536]{1,0:T(8,128)(2,1)S(1)}, u32[]{:S(2)}, u32[]{:S(2)}) collective-permute-start(bf16[64,1536]{1,0:T(8,128)(2,1)S(1)} %get-tuple-element.337), channel_id=1, source_target_pairs={{64,0},{128,64},{192,128},{256,192},{320,256},{384,320},{448,384},... | collective-permute-start | bytes 589832 | tf_op jit(solution)/shard_map/ppermute | solution.py:482
  107.1 6.3 %collective-permute-start.20 = (bf16[64,1536]{1,0:T(8,128)(2,1)S(1)}, bf16[64,1536]{1,0:T(8,128)(2,1)S(1)}, u32[]{:S(2)}, u32[]{:S(2)}) collective-permute-start(bf16[64,1536]{1,0:T(8,128)(2,1)S(1)} %get-tuple-element.345), channel_id=1, source_target_pairs={{64,0},{128,64},{192,128},{256,192},{320,256},{384,320},{448,384},... | collective-permute-start | bytes 589832 | tf_op jit(solution)/shard_map/ppermute | solution.py:482
  114.0 5.0 %collective-permute-start.21 = (bf16[64,1536]{1,0:T(8,128)(2,1)S(1)}, bf16[64,1536]{1,0:T(8,128)(2,1)S(1)}, u32[]{:S(2)}, u32[]{:S(2)}) collective-permute-start(bf16[64,1536]{1,0:T(8,128)(2,1)S(1)} %get-tuple-element.353), channel_id=1, source_target_pairs={{64,0},{128,64},{192,128},{256,192},{320,256},{384,320},{448,384},... | collective-permute-start | bytes 589832 | tf_op jit(solution)/shard_map/ppermute | solution.py:482
  119.1 0.8 shard_map.149
  119.8 4.3 %collective-permute-start.22 = (bf16[64,1536]{1,0:T(8,128)(2,1)S(1)}, bf16[64,1536]{1,0:T(8,128)(2,1)S(1)}, u32[]{:S(2)}, u32[]{:S(2)}) collective-permute-start(bf16[64,1536]{1,0:T(8,128)(2,1)S(1)} %get-tuple-element.361), channel_id=1, source_target_pairs={{64,0},{128,64},{192,128},{256,192},{320,256},{384,320},{448,384},... | collective-permute-start | bytes 589832 | tf_op jit(solution)/shard_map/ppermute | solution.py:482
  124.7 6.6 %collective-permute-start.23 = (bf16[64,1536]{1,0:T(8,128)(2,1)S(1)}, bf16[64,1536]{1,0:T(8,128)(2,1)S(1)}, u32[]{:S(2)}, u32[]{:S(2)}) collective-permute-start(bf16[64,1536]{1,0:T(8,128)(2,1)S(1)} %get-tuple-element.369), channel_id=1, source_target_pairs={{64,0},{128,64},{192,128},{256,192},{320,256},{384,320},{448,384},... | collective-permute-start | bytes 589832 | tf_op jit(solution)/shard_map/ppermute | solution.py:482
  131.3 0.7 collective-permute-start.29
  133.3 5.3 %collective-permute-start.24 = (bf16[64,1536]{1,0:T(8,128)(2,1)S(1)}, bf16[64,1536]{1,0:T(8,128)(2,1)S(1)}, u32[]{:S(2)}, u32[]{:S(2)}) collective-permute-start(bf16[64,1536]{1,0:T(8,128)(2,1)S(1)} %get-tuple-element.377), channel_id=1, source_target_pairs={{64,0},{128,64},{192,128},{256,192},{320,256},{384,320},{448,384},... | collective-permute-start | bytes 589832 | tf_op jit(solution)/shard_map/ppermute | solution.py:482
  139.2 4.7 %collective-permute-start.25 = (bf16[64,1536]{1,0:T(8,128)(2,1)S(1)}, bf16[64,1536]{1,0:T(8,128)(2,1)S(1)}, u32[]{:S(2)}, u32[]{:S(2)}) collective-permute-start(bf16[64,1536]{1,0:T(8,128)(2,1)S(1)} %get-tuple-element.385), channel_id=1, source_target_pairs={{64,0},{128,64},{192,128},{256,192},{320,256},{384,320},{448,384},... | collective-permute-start | bytes 589832 | tf_op jit(solution)/shard_map/ppermute | solution.py:482
  144.0 1.3 collective-permute-start.31
  145.3 6.7 %collective-permute-done.31.moved_ref = bf16[32,1536]{1,0:T(8,128)(2,1)S(1)} collective-permute-done((bf16[32,1536]{1,0:T(8,128)(2,1)S(1)}, bf16[32,1536]{1,0:T(8,128)(2,1)S(1)}, u32[]{:S(2)}, u32[]{:S(2)}) %collective-permute-start.31) | collective-permute-done | bytes 98336 | tf_op jit(solution)/shard_map/ppermute | solution.py:416
  152.0 1.6 shard_map.159
  153.6 1.9 collective-permute-start.32
  155.5 1.3 shard_map.153
  156.8 1.2 shard_map.154
  158.0 1.3 shard_map.155
  159.4 2.4 %collective-permute-start.27 = (bf16[16,48,256]{2,1,0:T(8,128)(2,1)S(1)}, bf16[16,48,256]{2,1,0:T(8,128)(2,1)S(1)}, u32[]{:S(2)}, u32[]{:S(2)}) collective-permute-start(bf16[16,48,256]{2,1,0:T(8,128)(2,1)S(1)} %get-tuple-element.394), channel_id=1, source_target_pairs={{0,1},{1,0},{2,3},{3,2},{4,5},{5,4},{6,7},{7,6},{8,9},{9,8},{10,11... | collective-permute-start | bytes 1179656 | tf_op jit(solution)/shard_map/ppermute | solution.py:305
  161.9 2.6 %collective-permute-start.33 = (bf16[16,16,256]{2,1,0:T(8,128)(2,1)S(1)}, bf16[16,16,256]{2,1,0:T(8,128)(2,1)S(1)}, u32[]{:S(2)}, u32[]{:S(2)}) collective-permute-start(bf16[16,16,256]{2,1,0:T(8,128)(2,1)S(1)} %get-tuple-element.408), channel_id=1, source_target_pairs={{0,32},{32,0},{1,33},{33,1},{2,34},{34,2},{3,35},{35,3},{4,36},{36... | collective-permute-start | bytes 393224 | tf_op jit(solution)/shard_map/ppermute | solution.py:305
  164.5 4.7 %collective-permute-done.33.right_ref = bf16[16,16,256]{2,1,0:T(8,128)(2,1)S(1)} collective-permute-done((bf16[16,16,256]{2,1,0:T(8,128)(2,1)S(1)}, bf16[16,16,256]{2,1,0:T(8,128)(2,1)S(1)}, u32[]{:S(2)}, u32[]{:S(2)}) %collective-permute-start.33) | collective-permute-done | bytes 131104 | tf_op jit(solution)/shard_map/ppermute | solution.py:305
  170.0 14.8 %all-to-all-start = ((bf16[16,16,256]{2,1,0:T(8,128)(2,1)}), bf16[16,16,256]{2,1,0:T(8,128)(2,1)S(1)}, u32[]{:S(2)}, u32[]{:S(2)}) async-start(bf16[16,16,256]{2,1,0:T(8,128)(2,1)} %shard_map.162), calls=%async_computation | async-start | bytes 262144 | tf_op jit(solution)/shard_map/all_to_all | solution.py:507
  184.7 2.6 %collective-permute-start.28 = (bf16[16,48,256]{2,1,0:T(8,128)(2,1)S(1)}, bf16[16,48,256]{2,1,0:T(8,128)(2,1)S(1)}, u32[]{:S(2)}, u32[]{:S(2)}) collective-permute-start(bf16[16,48,256]{2,1,0:T(8,128)(2,1)S(1)} %add_convert_fusion.1), channel_id=1, source_target_pairs={{0,32},{32,0},{1,33},{33,1},{2,34},{34,2},{3,35},{35,3},{4,36},{36... | collective-permute-start | bytes 1179656 | tf_op jit(solution)/shard_map/ppermute | solution.py:305
  187.3 1.9 collective-permute-start.26
  189.2 7.0 %collective-permute-done.28 = bf16[16,48,256]{2,1,0:T(8,128)(2,1)S(1)} collective-permute-done((bf16[16,48,256]{2,1,0:T(8,128)(2,1)S(1)}, bf16[16,48,256]{2,1,0:T(8,128)(2,1)S(1)}, u32[]{:S(2)}, u32[]{:S(2)}) %collective-permute-start.28) | collective-permute-done | bytes 393248 | tf_op jit(solution)/shard_map/ppermute | solution.py:305
  196.2 1.1 all-to-all-done
  197.3 0.9 add_convert_fusion
  198.2 10.9 %all-to-all-start.1 = ((bf16[16,48,256]{2,1,0:T(8,128)(2,1)}), bf16[16,48,256]{2,1,0:T(8,128)(2,1)S(1)}, u32[]{:S(2)}, u32[]{:S(2)}) async-start(bf16[16,48,256]{2,1,0:T(8,128)(2,1)} %add_convert_fusion), calls=%async_computation.1 | async-start | bytes 786432 | tf_op jit(solution)/shard_map/all_to_all | solution.py:511
  209.2 0.7 slice.22
  210.5 20.6 %all-to-all-done.1 = bf16[16,48,256]{2,1,0:T(8,128)(2,1)S(1)} async-done(((bf16[16,48,256]{2,1,0:T(8,128)(2,1)}), bf16[16,48,256]{2,1,0:T(8,128)(2,1)S(1)}, u32[]{:S(2)}, u32[]{:S(2)}) %all-to-all-start.1) | async-done | bytes 393248 | tf_op jit(solution)/shard_map/all_to_all | solution.py:511
  231.1 0.7 fusion
  (68 shorter events, 10.8 us)
Async XLA Ops:
  0.6 7.7 %copy-start.5 = (s32[4,1]{0,1:T(1,128)S(1)}, s32[4,1]{0,1:T(1,128)}, u32[]{:S(2)}) copy-start(s32[4,1]{0,1:T(1,128)} %param.11) | copy-start | bytes 52
  0.6 7.7 %copy-start.1 = (f32[1,1536]{1,0:T(1,128)S(1)}, f32[1,1536]{1,0:T(1,128)}, u32[]{:S(2)}) copy-start(f32[1,1536]{1,0:T(1,128)} %refs_5_.43) | copy-start | bytes 18436
  0.7 7.7 %copy-start.2 = (bf16[1,1536,256]{2,1,0:T(8,128)(2,1)S(1)}, bf16[1,1536,256]{2,1,0:T(8,128)(2,1)}, u32[]{:S(2)}) copy-start(bf16[1,1536,256]{2,1,0:T(8,128)(2,1)} %param.14) | copy-start | bytes 2359300
  0.7 7.7 %copy-start.3 = (bf16[1,256,1536]{2,1,0:T(8,128)(2,1)S(1)}, bf16[1,256,1536]{2,1,0:T(8,128)(2,1)}, u32[]{:S(2)}) copy-start(bf16[1,256,1536]{2,1,0:T(8,128)(2,1)} %param.15) | copy-start | bytes 2359300
  2.2 1.0 copy-start.4
  3.2 9.6 %collective-permute-start.8 = (bf16[192,384]{1,0:T(8,128)(2,1)S(1)}, bf16[192,384]{1,0:T(8,128)(2,1)S(1)}, u32[]{:S(2)}, u32[]{:S(2)}) collective-permute-start(bf16[192,384]{1,0:T(8,128)(2,1)S(1)} %shard_map.137.refs_1_), channel_id=1, source_target_pairs={{0,64},{128,192},{256,320},{384,448},{1,65},{129,193},{257,321},{3... | collective-permute-start | bytes 442376 | tf_op jit(solution)/shard_map/ppermute | solution.py:341
  8.4 2.0 copy-start
  10.9 11.9 %collective-permute-start = (bf16[64,1536]{1,0:T(8,128)(2,1)S(1)}, bf16[64,1536]{1,0:T(8,128)(2,1)S(1)}, u32[]{:S(2)}, u32[]{:S(2)}) collective-permute-start(bf16[64,1536]{1,0:T(8,128)(2,1)S(1)} %get-tuple-element.227), channel_id=1, source_target_pairs={{64,0},{128,64},{192,128},{256,192},{320,256},{384,320},{448,384},... | collective-permute-start | bytes 589832 | tf_op jit(solution)/shard_map/ppermute | solution.py:482
  12.8 20.3 %collective-permute-start.11 = (bf16[384,384]{1,0:T(8,128)(2,1)S(1)}, bf16[384,384]{1,0:T(8,128)(2,1)S(1)}, u32[]{:S(2)}, u32[]{:S(2)}) collective-permute-start(bf16[384,384]{1,0:T(8,128)(2,1)S(1)} %shard_map.138.refs_1_), channel_id=1, source_target_pairs={{448,192},{449,193},{450,194},{451,195},{452,196},{453,197},{454,1... | collective-permute-start | bytes 884744 | tf_op jit(solution)/shard_map/ppermute | solution.py:381
  13.5 19.6 %collective-permute-start.10 = (bf16[384,384]{1,0:T(8,128)(2,1)S(1)}, bf16[384,384]{1,0:T(8,128)(2,1)S(1)}, u32[]{:S(2)}, u32[]{:S(2)}) collective-permute-start(bf16[384,384]{1,0:T(8,128)(2,1)S(1)} %shard_map.138.refs_1_), channel_id=1, source_target_pairs={{320,192},{321,193},{322,194},{323,195},{324,196},{325,197},{326,1... | collective-permute-start | bytes 884744 | tf_op jit(solution)/shard_map/ppermute | solution.py:381
  14.2 18.9 %collective-permute-start.9 = (bf16[384,384]{1,0:T(8,128)(2,1)S(1)}, bf16[384,384]{1,0:T(8,128)(2,1)S(1)}, u32[]{:S(2)}, u32[]{:S(2)}) collective-permute-start(bf16[384,384]{1,0:T(8,128)(2,1)S(1)} %shard_map.138.refs_1_), channel_id=1, source_target_pairs={{64,192},{65,193},{66,194},{67,195},{68,196},{69,197},{70,198},{71... | collective-permute-start | bytes 884744 | tf_op jit(solution)/shard_map/ppermute | solution.py:381
  15.5 12.5 %collective-permute-start.1 = (bf16[64,1536]{1,0:T(8,128)(2,1)S(1)}, bf16[64,1536]{1,0:T(8,128)(2,1)S(1)}, u32[]{:S(2)}, u32[]{:S(2)}) collective-permute-start(bf16[64,1536]{1,0:T(8,128)(2,1)S(1)} %get-tuple-element.235), channel_id=1, source_target_pairs={{64,0},{128,64},{192,128},{256,192},{320,256},{384,320},{448,384},... | collective-permute-start | bytes 589832 | tf_op jit(solution)/shard_map/ppermute | solution.py:482
  23.3 9.2 %collective-permute-start.2 = (bf16[64,1536]{1,0:T(8,128)(2,1)S(1)}, bf16[64,1536]{1,0:T(8,128)(2,1)S(1)}, u32[]{:S(2)}, u32[]{:S(2)}) collective-permute-start(bf16[64,1536]{1,0:T(8,128)(2,1)S(1)} %get-tuple-element.243), channel_id=1, source_target_pairs={{64,0},{128,64},{192,128},{256,192},{320,256},{384,320},{448,384},... | collective-permute-start | bytes 589832 | tf_op jit(solution)/shard_map/ppermute | solution.py:482
  33.2 34.0 %collective-permute-start.12 = (bf16[1536,384]{1,0:T(8,128)(2,1)S(1)}, bf16[1536,384]{1,0:T(8,128)(2,1)S(1)}, u32[]{:S(2)}, u32[]{:S(2)}) collective-permute-start(bf16[1536,384]{1,0:T(8,128)(2,1)S(1)} %shard_map.139.own_ref), channel_id=1, source_target_pairs={{192,193},{193,192},{194,195},{195,194},{196,197},{197,196},{198,1... | collective-permute-start | bytes 3538952 | tf_op jit(solution)/shard_map/ppermute | solution.py:388
  33.9 11.3 %collective-permute-start.3 = (bf16[64,1536]{1,0:T(8,128)(2,1)S(1)}, bf16[64,1536]{1,0:T(8,128)(2,1)S(1)}, u32[]{:S(2)}, u32[]{:S(2)}) collective-permute-start(bf16[64,1536]{1,0:T(8,128)(2,1)S(1)} %get-tuple-element.251), channel_id=1, source_target_pairs={{64,0},{128,64},{192,128},{256,192},{320,256},{384,320},{448,384},... | collective-permute-start | bytes 589832 | tf_op jit(solution)/shard_map/ppermute | solution.py:482
  40.0 12.7 %collective-permute-start.4 = (bf16[64,1536]{1,0:T(8,128)(2,1)S(1)}, bf16[64,1536]{1,0:T(8,128)(2,1)S(1)}, u32[]{:S(2)}, u32[]{:S(2)}) collective-permute-start(bf16[64,1536]{1,0:T(8,128)(2,1)S(1)} %get-tuple-element.259), channel_id=1, source_target_pairs={{64,0},{128,64},{192,128},{256,192},{320,256},{384,320},{448,384},... | collective-permute-start | bytes 589832 | tf_op jit(solution)/shard_map/ppermute | solution.py:482
  45.8 10.9 %collective-permute-start.5 = (bf16[64,1536]{1,0:T(8,128)(2,1)S(1)}, bf16[64,1536]{1,0:T(8,128)(2,1)S(1)}, u32[]{:S(2)}, u32[]{:S(2)}) collective-permute-start(bf16[64,1536]{1,0:T(8,128)(2,1)S(1)} %get-tuple-element.267), channel_id=1, source_target_pairs={{64,0},{128,64},{192,128},{256,192},{320,256},{384,320},{448,384},... | collective-permute-start | bytes 589832 | tf_op jit(solution)/shard_map/ppermute | solution.py:482
  53.9 13.8 %collective-permute-start.6 = (bf16[64,1536]{1,0:T(8,128)(2,1)S(1)}, bf16[64,1536]{1,0:T(8,128)(2,1)S(1)}, u32[]{:S(2)}, u32[]{:S(2)}) collective-permute-start(bf16[64,1536]{1,0:T(8,128)(2,1)S(1)} %get-tuple-element.275), channel_id=1, source_target_pairs={{64,0},{128,64},{192,128},{256,192},{320,256},{384,320},{448,384},... | collective-permute-start | bytes 589832 | tf_op jit(solution)/shard_map/ppermute | solution.py:482
  56.7 10.5 %copy-start.6 = (bf16[768,29]{0,1:T(8,128)(2,1)S(1)}, bf16[768,29]{0,1:T(8,128)(2,1)}, u32[]{:S(2)}) copy-start(bf16[768,29]{0,1:T(8,128)(2,1)} %param.17) | copy-start | bytes 133636
  56.7 10.5 %copy-start.7 = (s32[4,1]{0,1:T(1,128)S(1)}, s32[4,1]{0,1:T(1,128)}, u32[]{:S(2)}) copy-start(s32[4,1]{0,1:T(1,128)} %param.12) | copy-start | bytes 52
  58.0 19.5 %collective-permute-start.13 = (bf16[64,1536]{1,0:T(8,128)(2,1)S(1)}, bf16[64,1536]{1,0:T(8,128)(2,1)S(1)}, u32[]{:S(2)}, u32[]{:S(2)}) collective-permute-start(bf16[64,1536]{1,0:T(8,128)(2,1)S(1)} %get-tuple-element.276), channel_id=1, source_target_pairs={{64,0},{128,64},{192,128},{256,192},{320,256},{384,320},{448,384},... | collective-permute-start | bytes 589832 | tf_op jit(solution)/shard_map/ppermute | solution.py:482
  63.5 3.7 %collective-permute-start.7 = (f32[8,1536]{1,0:T(8,128)S(1)}, f32[8,1536]{1,0:T(8,128)S(1)}, u32[]{:S(2)}, u32[]{:S(2)}) collective-permute-start(f32[8,1536]{1,0:T(8,128)S(1)} %get-tuple-element.279), channel_id=1, source_target_pairs={{256,192},{257,193},{258,194},{259,195},{260,196},{261,197},{262,1... | collective-permute-start | bytes 147464 | tf_op jit(solution)/shard_map/ppermute | solution.py:383
  69.0 13.2 %collective-permute-start.14 = (bf16[64,1536]{1,0:T(8,128)(2,1)S(1)}, bf16[64,1536]{1,0:T(8,128)(2,1)S(1)}, u32[]{:S(2)}, u32[]{:S(2)}) collective-permute-start(bf16[64,1536]{1,0:T(8,128)(2,1)S(1)} %get-tuple-element.297), channel_id=1, source_target_pairs={{64,0},{128,64},{192,128},{256,192},{320,256},{384,320},{448,384},... | collective-permute-start | bytes 589832 | tf_op jit(solution)/shard_map/ppermute | solution.py:482
  78.7 11.5 %collective-permute-start.15 = (bf16[64,1536]{1,0:T(8,128)(2,1)S(1)}, bf16[64,1536]{1,0:T(8,128)(2,1)S(1)}, u32[]{:S(2)}, u32[]{:S(2)}) collective-permute-start(bf16[64,1536]{1,0:T(8,128)(2,1)S(1)} %get-tuple-element.305), channel_id=1, source_target_pairs={{64,0},{128,64},{192,128},{256,192},{320,256},{384,320},{448,384},... | collective-permute-start | bytes 589832 | tf_op jit(solution)/shard_map/ppermute | solution.py:482
  83.4 10.7 %collective-permute-start.16 = (bf16[64,1536]{1,0:T(8,128)(2,1)S(1)}, bf16[64,1536]{1,0:T(8,128)(2,1)S(1)}, u32[]{:S(2)}, u32[]{:S(2)}) collective-permute-start(bf16[64,1536]{1,0:T(8,128)(2,1)S(1)} %get-tuple-element.313), channel_id=1, source_target_pairs={{64,0},{128,64},{192,128},{256,192},{320,256},{384,320},{448,384},... | collective-permute-start | bytes 589832 | tf_op jit(solution)/shard_map/ppermute | solution.py:482
  91.5 10.7 %collective-permute-start.17 = (bf16[64,1536]{1,0:T(8,128)(2,1)S(1)}, bf16[64,1536]{1,0:T(8,128)(2,1)S(1)}, u32[]{:S(2)}, u32[]{:S(2)}) collective-permute-start(bf16[64,1536]{1,0:T(8,128)(2,1)S(1)} %get-tuple-element.321), channel_id=1, source_target_pairs={{64,0},{128,64},{192,128},{256,192},{320,256},{384,320},{448,384},... | collective-permute-start | bytes 589832 | tf_op jit(solution)/shard_map/ppermute | solution.py:482
  95.3 11.1 %collective-permute-start.18 = (bf16[64,1536]{1,0:T(8,128)(2,1)S(1)}, bf16[64,1536]{1,0:T(8,128)(2,1)S(1)}, u32[]{:S(2)}, u32[]{:S(2)}) collective-permute-start(bf16[64,1536]{1,0:T(8,128)(2,1)S(1)} %get-tuple-element.329), channel_id=1, source_target_pairs={{64,0},{128,64},{192,128},{256,192},{320,256},{384,320},{448,384},... | collective-permute-start | bytes 589832 | tf_op jit(solution)/shard_map/ppermute | solution.py:482
  103.4 10.0 %collective-permute-start.19 = (bf16[64,1536]{1,0:T(8,128)(2,1)S(1)}, bf16[64,1536]{1,0:T(8,128)(2,1)S(1)}, u32[]{:S(2)}, u32[]{:S(2)}) collective-permute-start(bf16[64,1536]{1,0:T(8,128)(2,1)S(1)} %get-tuple-element.337), channel_id=1, source_target_pairs={{64,0},{128,64},{192,128},{256,192},{320,256},{384,320},{448,384},... | collective-permute-start | bytes 589832 | tf_op jit(solution)/shard_map/ppermute | solution.py:482
  107.1 12.0 %collective-permute-start.20 = (bf16[64,1536]{1,0:T(8,128)(2,1)S(1)}, bf16[64,1536]{1,0:T(8,128)(2,1)S(1)}, u32[]{:S(2)}, u32[]{:S(2)}) collective-permute-start(bf16[64,1536]{1,0:T(8,128)(2,1)S(1)} %get-tuple-element.345), channel_id=1, source_target_pairs={{64,0},{128,64},{192,128},{256,192},{320,256},{384,320},{448,384},... | collective-permute-start | bytes 589832 | tf_op jit(solution)/shard_map/ppermute | solution.py:482
  114.0 10.1 %collective-permute-start.21 = (bf16[64,1536]{1,0:T(8,128)(2,1)S(1)}, bf16[64,1536]{1,0:T(8,128)(2,1)S(1)}, u32[]{:S(2)}, u32[]{:S(2)}) collective-permute-start(bf16[64,1536]{1,0:T(8,128)(2,1)S(1)} %get-tuple-element.353), channel_id=1, source_target_pairs={{64,0},{128,64},{192,128},{256,192},{320,256},{384,320},{448,384},... | collective-permute-start | bytes 589832 | tf_op jit(solution)/shard_map/ppermute | solution.py:482
  119.8 12.9 %collective-permute-start.22 = (bf16[64,1536]{1,0:T(8,128)(2,1)S(1)}, bf16[64,1536]{1,0:T(8,128)(2,1)S(1)}, u32[]{:S(2)}, u32[]{:S(2)}) collective-permute-start(bf16[64,1536]{1,0:T(8,128)(2,1)S(1)} %get-tuple-element.361), channel_id=1, source_target_pairs={{64,0},{128,64},{192,128},{256,192},{320,256},{384,320},{448,384},... | collective-permute-start | bytes 589832 | tf_op jit(solution)/shard_map/ppermute | solution.py:482
  124.7 13.9 %collective-permute-start.23 = (bf16[64,1536]{1,0:T(8,128)(2,1)S(1)}, bf16[64,1536]{1,0:T(8,128)(2,1)S(1)}, u32[]{:S(2)}, u32[]{:S(2)}) collective-permute-start(bf16[64,1536]{1,0:T(8,128)(2,1)S(1)} %get-tuple-element.369), channel_id=1, source_target_pairs={{64,0},{128,64},{192,128},{256,192},{320,256},{384,320},{448,384},... | collective-permute-start | bytes 589832 | tf_op jit(solution)/shard_map/ppermute | solution.py:482
  131.3 0.7 collective-permute-start.29
  132.0 11.9 %collective-permute-start.30 = (bf16[32,1536]{1,0:T(8,128)(2,1)S(1)}, bf16[32,1536]{1,0:T(8,128)(2,1)S(1)}, u32[]{:S(2)}, u32[]{:S(2)}) collective-permute-start(bf16[32,1536]{1,0:T(8,128)(2,1)S(1)} %shard_map.156.held_ref), channel_id=1, source_target_pairs={{192,64},{448,320},{193,65},{449,321},{194,66},{450,322},{195,67},... | collective-permute-start | bytes 294920 | tf_op jit(solution)/shard_map/ppermute | solution.py:416
  133.3 22.2 %collective-permute-start.24 = (bf16[64,1536]{1,0:T(8,128)(2,1)S(1)}, bf16[64,1536]{1,0:T(8,128)(2,1)S(1)}, u32[]{:S(2)}, u32[]{:S(2)}) collective-permute-start(bf16[64,1536]{1,0:T(8,128)(2,1)S(1)} %get-tuple-element.377), channel_id=1, source_target_pairs={{64,0},{128,64},{192,128},{256,192},{320,256},{384,320},{448,384},... | collective-permute-start | bytes 589832 | tf_op jit(solution)/shard_map/ppermute | solution.py:482
  139.2 17.6 %collective-permute-start.25 = (bf16[64,1536]{1,0:T(8,128)(2,1)S(1)}, bf16[64,1536]{1,0:T(8,128)(2,1)S(1)}, u32[]{:S(2)}, u32[]{:S(2)}) collective-permute-start(bf16[64,1536]{1,0:T(8,128)(2,1)S(1)} %get-tuple-element.385), channel_id=1, source_target_pairs={{64,0},{128,64},{192,128},{256,192},{320,256},{384,320},{448,384},... | collective-permute-start | bytes 589832 | tf_op jit(solution)/shard_map/ppermute | solution.py:482
  144.0 8.0 %collective-permute-start.31 = (bf16[32,1536]{1,0:T(8,128)(2,1)S(1)}, bf16[32,1536]{1,0:T(8,128)(2,1)S(1)}, u32[]{:S(2)}, u32[]{:S(2)}) collective-permute-start(bf16[32,1536]{1,0:T(8,128)(2,1)S(1)} %shard_map.157.held_ref), channel_id=1, source_target_pairs={{64,0},{192,128},{320,256},{448,384},{65,1},{193,129},{321,257},{4... | collective-permute-start | bytes 294920 | tf_op jit(solution)/shard_map/ppermute | solution.py:416
  153.6 8.2 %collective-permute-start.32 = (bf16[2,16,16,256]{3,2,1,0:T(8,128)(2,1)S(1)}, bf16[2,16,16,256]{3,2,1,0:T(8,128)(2,1)S(1)}, u32[]{:S(2)}, u32[]{:S(2)}) collective-permute-start(bf16[2,16,16,256]{3,2,1,0:T(8,128)(2,1)S(1)} %get-tuple-element.405), channel_id=1, source_target_pairs={{0,1},{1,0},{2,3},{3,2},{4,5},{5,4},{6,7},{7,6},{8,9},{9,8},{10,11... | collective-permute-start | bytes 786440 | tf_op jit(solution)/shard_map/ppermute | solution.py:305
  159.4 9.8 %collective-permute-start.27 = (bf16[16,48,256]{2,1,0:T(8,128)(2,1)S(1)}, bf16[16,48,256]{2,1,0:T(8,128)(2,1)S(1)}, u32[]{:S(2)}, u32[]{:S(2)}) collective-permute-start(bf16[16,48,256]{2,1,0:T(8,128)(2,1)S(1)} %get-tuple-element.394), channel_id=1, source_target_pairs={{0,1},{1,0},{2,3},{3,2},{4,5},{5,4},{6,7},{7,6},{8,9},{9,8},{10,11... | collective-permute-start | bytes 1179656 | tf_op jit(solution)/shard_map/ppermute | solution.py:305
  161.9 7.3 %collective-permute-start.33 = (bf16[16,16,256]{2,1,0:T(8,128)(2,1)S(1)}, bf16[16,16,256]{2,1,0:T(8,128)(2,1)S(1)}, u32[]{:S(2)}, u32[]{:S(2)}) collective-permute-start(bf16[16,16,256]{2,1,0:T(8,128)(2,1)S(1)} %get-tuple-element.408), channel_id=1, source_target_pairs={{0,32},{32,0},{1,33},{33,1},{2,34},{34,2},{3,35},{35,3},{4,36},{36... | collective-permute-start | bytes 393224 | tf_op jit(solution)/shard_map/ppermute | solution.py:305
  170.0 27.4 %all-to-all-start = ((bf16[16,16,256]{2,1,0:T(8,128)(2,1)}), bf16[16,16,256]{2,1,0:T(8,128)(2,1)S(1)}, u32[]{:S(2)}, u32[]{:S(2)}) async-start(bf16[16,16,256]{2,1,0:T(8,128)(2,1)} %shard_map.162), calls=%async_computation | async-start | bytes 262144 | tf_op jit(solution)/shard_map/all_to_all | solution.py:507
  184.7 11.5 %collective-permute-start.28 = (bf16[16,48,256]{2,1,0:T(8,128)(2,1)S(1)}, bf16[16,48,256]{2,1,0:T(8,128)(2,1)S(1)}, u32[]{:S(2)}, u32[]{:S(2)}) collective-permute-start(bf16[16,48,256]{2,1,0:T(8,128)(2,1)S(1)} %add_convert_fusion.1), channel_id=1, source_target_pairs={{0,32},{32,0},{1,33},{33,1},{2,34},{34,2},{3,35},{35,3},{4,36},{36... | collective-permute-start | bytes 1179656 | tf_op jit(solution)/shard_map/ppermute | solution.py:305
  187.3 10.0 %collective-permute-start.26 = (bf16[16,48,256]{2,1,0:T(8,128)(2,1)S(1)}, bf16[16,48,256]{2,1,0:T(8,128)(2,1)S(1)}, u32[]{:S(2)}, u32[]{:S(2)}) collective-permute-start(bf16[16,48,256]{2,1,0:T(8,128)(2,1)S(1)} %get-tuple-element.392), channel_id=1, source_target_pairs={{0,1},{1,0},{2,3},{3,2},{4,5},{5,4},{6,7},{7,6},{8,9},{9,8},{10,11... | collective-permute-start | bytes 1179656 | tf_op jit(solution)/shard_map/ppermute | solution.py:305
  198.2 32.8 %all-to-all-start.1 = ((bf16[16,48,256]{2,1,0:T(8,128)(2,1)}), bf16[16,48,256]{2,1,0:T(8,128)(2,1)S(1)}, u32[]{:S(2)}, u32[]{:S(2)}) async-start(bf16[16,48,256]{2,1,0:T(8,128)(2,1)} %add_convert_fusion), calls=%async_computation.1 | async-start | bytes 786432 | tf_op jit(solution)/shard_map/all_to_all | solution.py:511

commit v4 on v3

--- a/solution.py
+++ b/solution.py
@@ -245,10 +245,6 @@
         other_ref[...] = plus(kept_ref[1], got_ref[1])
 
 
-def copy_kernel(source_ref, out_ref):
-    out_ref[...] = source_ref[...]
-
-
 def add_kernel(left_ref, right_ref, out_ref):
     out_ref[...] = plus(left_ref[...], right_ref[...])
 
@@ -405,7 +401,17 @@
                 4 << 20,
                 scratch=[pltpu.VMEM((32, features), F32)],
             )
-        elif step in (8, 10, 12):
+        if step in (10, 12, 14) and "moved" in held:
+            targets, moved = held.pop("moved")
+            held["lines"] = call(
+                functools.partial(pick_kernel, targets),
+                sds(held["lines"].shape, BF16),
+                [SM, VM, VM],
+                (after(sec_s, token), moved, held["lines"]),
+                0,
+                1 << 18,
+            )
+        if step in (8, 10, 12):
             lines = after(held["lines"], token)
             if step == 8:
                 route = [(3, 7)]
@@ -429,25 +435,13 @@
             held["got"] = swap(sent, "c", n_c)
         elif step == 16:
             one = sds((n_z, padded, rank), BF16)
-            own, other = call(
-                split_kernel, (one, one), [VM, VM], (after(held["kept"], token), held["got"]), 0, 1 << 20
-            )
+            own, other = call(split_kernel, (one, one), [VM, VM], (after(held["kept"], token), held["got"]), 0, 1 << 20)
             held["own_sum"] = own
             if n_yl == 2:
                 held["other_sum"] = swap(other, "yl", n_yl)
-        elif step == 19 and n_yl == 2:
+        elif step == 18 and n_yl == 2:
             args = (after(held["own_sum"], token), held["other_sum"])
             held["own_sum"] = call(add_kernel, sds(args[0].shape, BF16), [VM, VM], args, 0, 1 << 20)
-        if step in (9, 11, 13):
-            targets, moved = held.pop("moved")
-            held["lines"] = call(
-                functools.partial(pick_kernel, targets),
-                sds(held["lines"].shape, BF16),
-                [SM, VM, VM],
-                (after(sec_s, token), moved, held["lines"]),
-                0,
-                1 << 18,
-            )
 
     steps = DELAY * (SECTIONS - 1) + chunks
     received = {}
@@ -497,16 +491,15 @@
     kept, sent = packed[:n_yl], packed[n_yl:]
     halves = [None] * n_yl
     for i in reversed(range(n_yl)):
-        halves[i] = plus(kept[i], swap(sent[i], "c", n_c))
+        arrived = swap(sent[i], "c", n_c)
+        args = (kept[i], arrived)
+        halves[i] = call(add_kernel, sds(arrived.shape, BF16), [VM, VM], args, 0, 2 << 20)
     summed = halves[0]
-    crit = held["own_sum"]
-    if n_yl == 2:
-        moved = swap(halves[1], "yl", n_yl)
-        crit = call(copy_kernel, sds(crit.shape, BF16), [VM], (after(crit, halves[1]),), 0, 1 << 18)
+    crit = after(held["own_sum"], packed[-1])
     if n_z > 1:
         crit = lax.all_to_all(crit, "z", 0, 0, tiled=True)
     if n_yl == 2:
-        summed = plus(summed, after(moved, crit))
+        summed = plus(summed, swap(halves[1], "yl", n_yl))
     if n_z > 1:
         summed = lax.all_to_all(summed, "z", 0, 0, tiled=True)
     total = jnp.sum(summed.astype(F32), axis=0)

time: 234 us -> 241 us (1.030)
  the two profiles are of different devices: /device:TPU:68 before, /device:TPU:2 now
where the time goes in v4:
time: 241 us; the launch traced here: 240 us
  starting transfers between devices  111 us (46%)
  waiting for transfers between devices  95.4 us (40%)
  Pallas kernels  25.8 us (11%)
  local copies, waits for them, and re-layouts  3.8 us (2%)
    ppermute x20, starting transfers between devices, whole(): received[step] = lax.ppermute(outgoing, SEC, relay_route)  68.7 us
    ppermute x20, waiting for transfers between devices, whole(): received[step] = lax.ppermute(outgoing, SEC, relay_route)  43.7 us
    pallas_call x36, Pallas kernels, call(): pl.pallas_call(kernel, out_shape=out_shape, in_specs=in_specs, out_specs=...  25.8 us
    all_to_all x1, waiting for transfers between devices, whole(): summed = lax.all_to_all(summed, 'z', 0, 0, tiled=True)  20.9 us
    all_to_all x1, starting transfers between devices, whole(): crit = lax.all_to_all(crit, 'z', 0, 0, tiled=True)  15.2 us
    all_to_all x1, waiting for transfers between devices, whole(): crit = lax.all_to_all(crit, 'z', 0, 0, tiled=True)  13.1 us
    ppermute x5, starting transfers between devices, swap(): return lax.ppermute(block, axis, [(i, size - 1 - i) for i in range(size)])  12.1 us
    ppermute x5, waiting for transfers between devices, swap(): return lax.ppermute(block, axis, [(i, size - 1 - i) for i in range(size)])  9.81 us
  transfers between devices with their start and end apart: 36, of which 17 were waited for; matrix products, arithmetic and copies ran while one was open for 1% of the time, Pallas kernels for 11%

profile of v4, /device:TPU:2, one launch (start us, length us, event | category | flops | bytes accessed | tf_op | source)
XLA Modules:
  0.0 239.7 jit_solution(8002371649396524857)
XLA Ops:
  0.7 1.5 copy.323
  2.2 1.0 copy-done.4
  3.2 5.1 %collective-permute-start.8 = (bf16[192,384]{1,0:T(8,128)(2,1)S(1)}, bf16[192,384]{1,0:T(8,128)(2,1)S(1)}, u32[]{:S(2)}, u32[]{:S(2)}) collective-permute-start(bf16[192,384]{1,0:T(8,128)(2,1)S(1)} %shard_map.137.refs_1_), channel_id=1, source_target_pairs={{0,64},{128,192},{256,320},{384,448},{1,65},{129,193},{257,321},{3... | collective-permute-start | bytes 442376 | tf_op jit(solution)/shard_map/ppermute | solution.py:337
  8.4 1.9 shard_map.128
  10.9 1.9 collective-permute-start
  15.5 9.4 %collective-permute-start.1 = (bf16[64,1536]{1,0:T(8,128)(2,1)S(1)}, bf16[64,1536]{1,0:T(8,128)(2,1)S(1)}, u32[]{:S(2)}, u32[]{:S(2)}) collective-permute-start(bf16[64,1536]{1,0:T(8,128)(2,1)S(1)} %get-tuple-element.233), channel_id=1, source_target_pairs={{64,0},{128,64},{192,128},{256,192},{320,256},{384,320},{448,384},... | collective-permute-start | bytes 589832 | tf_op jit(solution)/shard_map/ppermute | solution.py:476
  25.5 1.9 collective-permute-start.2
  27.4 2.4 %collective-permute-done.1.refs_9_ = bf16[64,1536]{1,0:T(8,128)(2,1)S(1)} collective-permute-done((bf16[64,1536]{1,0:T(8,128)(2,1)S(1)}, bf16[64,1536]{1,0:T(8,128)(2,1)S(1)}, u32[]{:S(2)}, u32[]{:S(2)}) %collective-permute-start.1) | collective-permute-done | bytes 196640 | tf_op jit(solution)/shard_map/ppermute | solution.py:476
  30.4 4.1 %collective-permute-done.2.refs_9_ = bf16[64,1536]{1,0:T(8,128)(2,1)S(1)} collective-permute-done((bf16[64,1536]{1,0:T(8,128)(2,1)S(1)}, bf16[64,1536]{1,0:T(8,128)(2,1)S(1)}, u32[]{:S(2)}, u32[]{:S(2)}) %collective-permute-start.2) | collective-permute-done | bytes 196640 | tf_op jit(solution)/shard_map/ppermute | solution.py:476
  35.2 0.7 collective-permute-start.12
  35.9 4.7 %collective-permute-start.3 = (bf16[64,1536]{1,0:T(8,128)(2,1)S(1)}, bf16[64,1536]{1,0:T(8,128)(2,1)S(1)}, u32[]{:S(2)}, u32[]{:S(2)}) collective-permute-start(bf16[64,1536]{1,0:T(8,128)(2,1)S(1)} %get-tuple-element.249), channel_id=1, source_target_pairs={{64,0},{128,64},{192,128},{256,192},{320,256},{384,320},{448,384},... | collective-permute-start | bytes 589832 | tf_op jit(solution)/shard_map/ppermute | solution.py:476
  40.6 1.9 collective-permute-start.4
  42.6 3.8 %collective-permute-done.3.refs_9_ = bf16[64,1536]{1,0:T(8,128)(2,1)S(1)} collective-permute-done((bf16[64,1536]{1,0:T(8,128)(2,1)S(1)}, bf16[64,1536]{1,0:T(8,128)(2,1)S(1)}, u32[]{:S(2)}, u32[]{:S(2)}) %collective-permute-start.3) | collective-permute-done | bytes 196640 | tf_op jit(solution)/shard_map/ppermute | solution.py:476
  46.9 5.9 %collective-permute-start.5 = (bf16[64,1536]{1,0:T(8,128)(2,1)S(1)}, bf16[64,1536]{1,0:T(8,128)(2,1)S(1)}, u32[]{:S(2)}, u32[]{:S(2)}) collective-permute-start(bf16[64,1536]{1,0:T(8,128)(2,1)S(1)} %get-tuple-element.265), channel_id=1, source_target_pairs={{64,0},{128,64},{192,128},{256,192},{320,256},{384,320},{448,384},... | collective-permute-start | bytes 589832 | tf_op jit(solution)/shard_map/ppermute | solution.py:476
  53.5 1.9 collective-permute-start.6
  55.4 1.5 collective-permute-done.5.refs_9_
  57.5 6.7 %collective-permute-start.13 = (bf16[64,1536]{1,0:T(8,128)(2,1)S(1)}, bf16[64,1536]{1,0:T(8,128)(2,1)S(1)}, u32[]{:S(2)}, u32[]{:S(2)}) collective-permute-start(bf16[64,1536]{1,0:T(8,128)(2,1)S(1)} %get-tuple-element.274), channel_id=1, source_target_pairs={{64,0},{128,64},{192,128},{256,192},{320,256},{384,320},{448,384},... | collective-permute-start | bytes 589832 | tf_op jit(solution)/shard_map/ppermute | solution.py:476
  66.1 1.9 collective-permute-start.14
  68.6 6.1 %collective-permute-start.15 = (bf16[64,1536]{1,0:T(8,128)(2,1)S(1)}, bf16[64,1536]{1,0:T(8,128)(2,1)S(1)}, u32[]{:S(2)}, u32[]{:S(2)}) collective-permute-start(bf16[64,1536]{1,0:T(8,128)(2,1)S(1)} %get-tuple-element.303), channel_id=1, source_target_pairs={{64,0},{128,64},{192,128},{256,192},{320,256},{384,320},{448,384},... | collective-permute-start | bytes 589832 | tf_op jit(solution)/shard_map/ppermute | solution.py:476
  74.8 8.2 %collective-permute-done.14.refs_8_ = bf16[64,1536]{1,0:T(8,128)(2,1)S(1)} collective-permute-done((bf16[64,1536]{1,0:T(8,128)(2,1)S(1)}, bf16[64,1536]{1,0:T(8,128)(2,1)S(1)}, u32[]{:S(2)}, u32[]{:S(2)}) %collective-permute-start.14) | collective-permute-done | bytes 196640 | tf_op jit(solution)/shard_map/ppermute | solution.py:476
  82.9 1.2 shard_map.143
  84.2 1.9 collective-permute-start.16
  86.1 1.2 shard_map.144
  87.4 1.9 collective-permute-start.17
  89.3 5.6 %collective-permute-done.16.refs_8_ = bf16[64,1536]{1,0:T(8,128)(2,1)S(1)} collective-permute-done((bf16[64,1536]{1,0:T(8,128)(2,1)S(1)}, bf16[64,1536]{1,0:T(8,128)(2,1)S(1)}, u32[]{:S(2)}, u32[]{:S(2)}) %collective-permute-start.16) | collective-permute-done | bytes 196640 | tf_op jit(solution)/shard_map/ppermute | solution.py:476
  94.9 1.2 shard_map.145
  96.1 2.4 %collective-permute-start.18 = (bf16[64,1536]{1,0:T(8,128)(2,1)S(1)}, bf16[64,1536]{1,0:T(8,128)(2,1)S(1)}, u32[]{:S(2)}, u32[]{:S(2)}) collective-permute-start(bf16[64,1536]{1,0:T(8,128)(2,1)S(1)} %get-tuple-element.327), channel_id=1, source_target_pairs={{64,0},{128,64},{192,128},{256,192},{320,256},{384,320},{448,384},... | collective-permute-start | bytes 589832 | tf_op jit(solution)/shard_map/ppermute | solution.py:476
  98.6 1.2 shard_map.146
  99.8 2.4 collective-permute-start.19
  102.2 3.7 %collective-permute-done.18.refs_8_ = bf16[64,1536]{1,0:T(8,128)(2,1)S(1)} collective-permute-done((bf16[64,1536]{1,0:T(8,128)(2,1)S(1)}, bf16[64,1536]{1,0:T(8,128)(2,1)S(1)}, u32[]{:S(2)}, u32[]{:S(2)}) %collective-permute-start.18) | collective-permute-done | bytes 196640 | tf_op jit(solution)/shard_map/ppermute | solution.py:476
  105.9 1.2 shard_map.147
  107.2 3.0 %collective-permute-start.20 = (bf16[64,1536]{1,0:T(8,128)(2,1)S(1)}, bf16[64,1536]{1,0:T(8,128)(2,1)S(1)}, u32[]{:S(2)}, u32[]{:S(2)}) collective-permute-start(bf16[64,1536]{1,0:T(8,128)(2,1)S(1)} %get-tuple-element.343), channel_id=1, source_target_pairs={{64,0},{128,64},{192,128},{256,192},{320,256},{384,320},{448,384},... | collective-permute-start | bytes 589832 | tf_op jit(solution)/shard_map/ppermute | solution.py:476
  110.1 1.6 collective-permute-done.19.refs_8_
  111.7 1.2 shard_map.148
  113.0 1.9 collective-permute-start.21
  114.9 2.2 collective-permute-done.20.refs_8_
  117.1 1.4 shard_map.149
  118.5 3.0 %collective-permute-start.22 = (bf16[64,1536]{1,0:T(8,128)(2,1)S(1)}, bf16[64,1536]{1,0:T(8,128)(2,1)S(1)}, u32[]{:S(2)}, u32[]{:S(2)}) collective-permute-start(bf16[64,1536]{1,0:T(8,128)(2,1)S(1)} %get-tuple-element.359), channel_id=1, source_target_pairs={{64,0},{128,64},{192,128},{256,192},{320,256},{384,320},{448,384},... | collective-permute-start | bytes 589832 | tf_op jit(solution)/shard_map/ppermute | solution.py:476
  121.5 2.5 %collective-permute-done.21.refs_8_ = bf16[64,1536]{1,0:T(8,128)(2,1)S(1)} collective-permute-done((bf16[64,1536]{1,0:T(8,128)(2,1)S(1)}, bf16[64,1536]{1,0:T(8,128)(2,1)S(1)}, u32[]{:S(2)}, u32[]{:S(2)}) %collective-permute-start.21) | collective-permute-done | bytes 196640 | tf_op jit(solution)/shard_map/ppermute | solution.py:476
  124.0 1.2 shard_map.150
  125.2 2.7 %collective-permute-start.23 = (bf16[64,1536]{1,0:T(8,128)(2,1)S(1)}, bf16[64,1536]{1,0:T(8,128)(2,1)S(1)}, u32[]{:S(2)}, u32[]{:S(2)}) collective-permute-start(bf16[64,1536]{1,0:T(8,128)(2,1)S(1)} %get-tuple-element.367), channel_id=1, source_target_pairs={{64,0},{128,64},{192,128},{256,192},{320,256},{384,320},{448,384},... | collective-permute-start | bytes 589832 | tf_op jit(solution)/shard_map/ppermute | solution.py:476
  128.5 4.2 %collective-permute-start.24 = (bf16[64,1536]{1,0:T(8,128)(2,1)S(1)}, bf16[64,1536]{1,0:T(8,128)(2,1)S(1)}, u32[]{:S(2)}, u32[]{:S(2)}) collective-permute-start(bf16[64,1536]{1,0:T(8,128)(2,1)S(1)} %get-tuple-element.375), channel_id=1, source_target_pairs={{64,0},{128,64},{192,128},{256,192},{320,256},{384,320},{448,384},... | collective-permute-start | bytes 589832 | tf_op jit(solution)/shard_map/ppermute | solution.py:476
  132.7 4.3 %collective-permute-done.23.refs_8_ = bf16[64,1536]{1,0:T(8,128)(2,1)S(1)} collective-permute-done((bf16[64,1536]{1,0:T(8,128)(2,1)S(1)}, bf16[64,1536]{1,0:T(8,128)(2,1)S(1)}, u32[]{:S(2)}, u32[]{:S(2)}) %collective-permute-start.23) | collective-permute-done | bytes 196640 | tf_op jit(solution)/shard_map/ppermute | solution.py:476
  137.6 2.8 %collective-permute-start.25 = (bf16[64,1536]{1,0:T(8,128)(2,1)S(1)}, bf16[64,1536]{1,0:T(8,128)(2,1)S(1)}, u32[]{:S(2)}, u32[]{:S(2)}) collective-permute-start(bf16[64,1536]{1,0:T(8,128)(2,1)S(1)} %get-tuple-element.383), channel_id=1, source_target_pairs={{64,0},{128,64},{192,128},{256,192},{320,256},{384,320},{448,384},... | collective-permute-start | bytes 589832 | tf_op jit(solution)/shard_map/ppermute | solution.py:476
  141.8 1.3 shard_map.153
  143.1 3.8 %collective-permute-done.25.refs_8_ = bf16[64,1536]{1,0:T(8,128)(2,1)S(1)} collective-permute-done((bf16[64,1536]{1,0:T(8,128)(2,1)S(1)}, bf16[64,1536]{1,0:T(8,128)(2,1)S(1)}, u32[]{:S(2)}, u32[]{:S(2)}) %collective-permute-start.25) | collective-permute-done | bytes 196640 | tf_op jit(solution)/shard_map/ppermute | solution.py:476
  146.8 1.2 shard_map.154
  148.1 1.3 shard_map.155
  149.4 1.9 collective-permute-start.27
  151.4 1.3 collective-permute-start.31
  152.7 7.8 %collective-permute-done.31.moved_ref = bf16[32,1536]{1,0:T(8,128)(2,1)S(1)} collective-permute-done((bf16[32,1536]{1,0:T(8,128)(2,1)S(1)}, bf16[32,1536]{1,0:T(8,128)(2,1)S(1)}, u32[]{:S(2)}, u32[]{:S(2)}) %collective-permute-start.31) | collective-permute-done | bytes 98336 | tf_op jit(solution)/shard_map/ppermute | solution.py:422
  160.6 1.6 shard_map.161
  162.1 1.9 collective-permute-start.32
  164.1 2.4 %collective-permute-start.26 = (bf16[16,48,256]{2,1,0:T(8,128)(2,1)S(1)}, bf16[16,48,256]{2,1,0:T(8,128)(2,1)S(1)}, u32[]{:S(2)}, u32[]{:S(2)}) collective-permute-start(bf16[16,48,256]{2,1,0:T(8,128)(2,1)S(1)} %get-tuple-element.390), channel_id=1, source_target_pairs={{0,1},{1,0},{2,3},{3,2},{4,5},{5,4},{6,7},{7,6},{8,9},{9,8},{10,11... | collective-permute-start | bytes 1179656 | tf_op jit(solution)/shard_map/ppermute | solution.py:301
  166.6 2.6 %collective-permute-start.28 = (bf16[16,48,256]{2,1,0:T(8,128)(2,1)S(1)}, bf16[16,48,256]{2,1,0:T(8,128)(2,1)S(1)}, u32[]{:S(2)}, u32[]{:S(2)}) collective-permute-start(bf16[16,48,256]{2,1,0:T(8,128)(2,1)S(1)} %shard_map.157), channel_id=1, source_target_pairs={{0,32},{32,0},{1,33},{33,1},{2,34},{34,2},{3,35},{35,3},{4,36},{36... | collective-permute-start | bytes 1179656 | tf_op jit(solution)/shard_map/ppermute | solution.py:301
  169.3 3.3 %collective-permute-start.33 = (bf16[16,16,256]{2,1,0:T(8,128)(2,1)S(1)}, bf16[16,16,256]{2,1,0:T(8,128)(2,1)S(1)}, u32[]{:S(2)}, u32[]{:S(2)}) collective-permute-start(bf16[16,16,256]{2,1,0:T(8,128)(2,1)S(1)} %get-tuple-element.405), channel_id=1, source_target_pairs={{0,32},{32,0},{1,33},{33,1},{2,34},{34,2},{3,35},{35,3},{4,36},{36... | collective-permute-start | bytes 393224 | tf_op jit(solution)/shard_map/ppermute | solution.py:301
  172.5 9.8 %collective-permute-done.33.right_ref = bf16[16,16,256]{2,1,0:T(8,128)(2,1)S(1)} collective-permute-done((bf16[16,16,256]{2,1,0:T(8,128)(2,1)S(1)}, bf16[16,16,256]{2,1,0:T(8,128)(2,1)S(1)}, u32[]{:S(2)}, u32[]{:S(2)}) %collective-permute-start.33) | collective-permute-done | bytes 131104 | tf_op jit(solution)/shard_map/ppermute | solution.py:301
  182.3 0.7 shard_map.163
  183.0 15.2 %all-to-all-start.1 = ((bf16[16,16,256]{2,1,0:T(8,128)(2,1)}), bf16[16,16,256]{2,1,0:T(8,128)(2,1)S(1)}, u32[]{:S(2)}, u32[]{:S(2)}) async-start(bf16[16,16,256]{2,1,0:T(8,128)(2,1)} %shard_map.163), calls=%async_computation.1 | async-start | bytes 262144 | tf_op jit(solution)/shard_map/all_to_all | solution.py:500
  198.3 0.9 add_convert_fusion
  199.2 13.1 %all-to-all-done.1 = bf16[16,16,256]{2,1,0:T(8,128)(2,1)S(1)} async-done(((bf16[16,16,256]{2,1,0:T(8,128)(2,1)}), bf16[16,16,256]{2,1,0:T(8,128)(2,1)S(1)}, u32[]{:S(2)}, u32[]{:S(2)}) %all-to-all-start.1) | async-done | bytes 131104 | tf_op jit(solution)/shard_map/all_to_all | solution.py:500
  212.3 3.8 %all-to-all-start = ((bf16[16,48,256]{2,1,0:T(8,128)(2,1)}), bf16[16,48,256]{2,1,0:T(8,128)(2,1)S(1)}, u32[]{:S(2)}, u32[]{:S(2)}) async-start(bf16[16,48,256]{2,1,0:T(8,128)(2,1)} %add_convert_fusion), calls=%async_computation | async-start | bytes 786432 | tf_op jit(solution)/shard_map/all_to_all | solution.py:504
  217.4 20.9 %all-to-all-done = bf16[16,48,256]{2,1,0:T(8,128)(2,1)S(1)} async-done(((bf16[16,48,256]{2,1,0:T(8,128)(2,1)}), bf16[16,48,256]{2,1,0:T(8,128)(2,1)S(1)}, u32[]{:S(2)}, u32[]{:S(2)}) %all-to-all-start) | async-done | bytes 393248 | tf_op jit(solution)/shard_map/all_to_all | solution.py:504
  238.4 0.7 fusion
  (68 shorter events, 13.9 us)
Async XLA Ops:
  0.6 7.7 %copy-start.5 = (s32[4,1]{0,1:T(1,128)S(1)}, s32[4,1]{0,1:T(1,128)}, u32[]{:S(2)}) copy-start(s32[4,1]{0,1:T(1,128)} %param.11) | copy-start | bytes 52
  0.6 7.7 %copy-start.1 = (f32[1,1536]{1,0:T(1,128)S(1)}, f32[1,1536]{1,0:T(1,128)}, u32[]{:S(2)}) copy-start(f32[1,1536]{1,0:T(1,128)} %refs_5_.43) | copy-start | bytes 18436
  0.7 7.7 %copy-start.2 = (bf16[1,1536,256]{2,1,0:T(8,128)(2,1)S(1)}, bf16[1,1536,256]{2,1,0:T(8,128)(2,1)}, u32[]{:S(2)}) copy-start(bf16[1,1536,256]{2,1,0:T(8,128)(2,1)} %param.14) | copy-start | bytes 2359300
  0.7 7.7 %copy-start.3 = (bf16[1,256,1536]{2,1,0:T(8,128)(2,1)S(1)}, bf16[1,256,1536]{2,1,0:T(8,128)(2,1)}, u32[]{:S(2)}) copy-start(bf16[1,256,1536]{2,1,0:T(8,128)(2,1)} %param.15) | copy-start | bytes 2359300
  2.2 1.0 copy-start.4
  3.2 9.6 %collective-permute-start.8 = (bf16[192,384]{1,0:T(8,128)(2,1)S(1)}, bf16[192,384]{1,0:T(8,128)(2,1)S(1)}, u32[]{:S(2)}, u32[]{:S(2)}) collective-permute-start(bf16[192,384]{1,0:T(8,128)(2,1)S(1)} %shard_map.137.refs_1_), channel_id=1, source_target_pairs={{0,64},{128,192},{256,320},{384,448},{1,65},{129,193},{257,321},{3... | collective-permute-start | bytes 442376 | tf_op jit(solution)/shard_map/ppermute | solution.py:337
  8.4 2.0 copy-start
  10.9 14.0 %collective-permute-start = (bf16[64,1536]{1,0:T(8,128)(2,1)S(1)}, bf16[64,1536]{1,0:T(8,128)(2,1)S(1)}, u32[]{:S(2)}, u32[]{:S(2)}) collective-permute-start(bf16[64,1536]{1,0:T(8,128)(2,1)S(1)} %get-tuple-element.225), channel_id=1, source_target_pairs={{64,0},{128,64},{192,128},{256,192},{320,256},{384,320},{448,384},... | collective-permute-start | bytes 589832 | tf_op jit(solution)/shard_map/ppermute | solution.py:476
  12.8 22.3 %collective-permute-start.11 = (bf16[384,384]{1,0:T(8,128)(2,1)S(1)}, bf16[384,384]{1,0:T(8,128)(2,1)S(1)}, u32[]{:S(2)}, u32[]{:S(2)}) collective-permute-start(bf16[384,384]{1,0:T(8,128)(2,1)S(1)} %shard_map.138.refs_1_), channel_id=1, source_target_pairs={{448,192},{449,193},{450,194},{451,195},{452,196},{453,197},{454,1... | collective-permute-start | bytes 884744 | tf_op jit(solution)/shard_map/ppermute | solution.py:377
  13.5 21.6 %collective-permute-start.10 = (bf16[384,384]{1,0:T(8,128)(2,1)S(1)}, bf16[384,384]{1,0:T(8,128)(2,1)S(1)}, u32[]{:S(2)}, u32[]{:S(2)}) collective-permute-start(bf16[384,384]{1,0:T(8,128)(2,1)S(1)} %shard_map.138.refs_1_), channel_id=1, source_target_pairs={{320,192},{321,193},{322,194},{323,195},{324,196},{325,197},{326,1... | collective-permute-start | bytes 884744 | tf_op jit(solution)/shard_map/ppermute | solution.py:377
  14.2 20.9 %collective-permute-start.9 = (bf16[384,384]{1,0:T(8,128)(2,1)S(1)}, bf16[384,384]{1,0:T(8,128)(2,1)S(1)}, u32[]{:S(2)}, u32[]{:S(2)}) collective-permute-start(bf16[384,384]{1,0:T(8,128)(2,1)S(1)} %shard_map.138.refs_1_), channel_id=1, source_target_pairs={{64,192},{65,193},{66,194},{67,195},{68,196},{69,197},{70,198},{71... | collective-permute-start | bytes 884744 | tf_op jit(solution)/shard_map/ppermute | solution.py:377
  15.5 14.4 %collective-permute-start.1 = (bf16[64,1536]{1,0:T(8,128)(2,1)S(1)}, bf16[64,1536]{1,0:T(8,128)(2,1)S(1)}, u32[]{:S(2)}, u32[]{:S(2)}) collective-permute-start(bf16[64,1536]{1,0:T(8,128)(2,1)S(1)} %get-tuple-element.233), channel_id=1, source_target_pairs={{64,0},{128,64},{192,128},{256,192},{320,256},{384,320},{448,384},... | collective-permute-start | bytes 589832 | tf_op jit(solution)/shard_map/ppermute | solution.py:476
  25.5 9.1 %collective-permute-start.2 = (bf16[64,1536]{1,0:T(8,128)(2,1)S(1)}, bf16[64,1536]{1,0:T(8,128)(2,1)S(1)}, u32[]{:S(2)}, u32[]{:S(2)}) collective-permute-start(bf16[64,1536]{1,0:T(8,128)(2,1)S(1)} %get-tuple-element.241), channel_id=1, source_target_pairs={{64,0},{128,64},{192,128},{256,192},{320,256},{384,320},{448,384},... | collective-permute-start | bytes 589832 | tf_op jit(solution)/shard_map/ppermute | solution.py:476
  35.2 29.7 %collective-permute-start.12 = (bf16[1536,384]{1,0:T(8,128)(2,1)S(1)}, bf16[1536,384]{1,0:T(8,128)(2,1)S(1)}, u32[]{:S(2)}, u32[]{:S(2)}) collective-permute-start(bf16[1536,384]{1,0:T(8,128)(2,1)S(1)} %shard_map.139.own_ref), channel_id=1, source_target_pairs={{192,193},{193,192},{194,195},{195,194},{196,197},{197,196},{198,1... | collective-permute-start | bytes 3538952 | tf_op jit(solution)/shard_map/ppermute | solution.py:384
  35.9 10.4 %collective-permute-start.3 = (bf16[64,1536]{1,0:T(8,128)(2,1)S(1)}, bf16[64,1536]{1,0:T(8,128)(2,1)S(1)}, u32[]{:S(2)}, u32[]{:S(2)}) collective-permute-start(bf16[64,1536]{1,0:T(8,128)(2,1)S(1)} %get-tuple-element.249), channel_id=1, source_target_pairs={{64,0},{128,64},{192,128},{256,192},{320,256},{384,320},{448,384},... | collective-permute-start | bytes 589832 | tf_op jit(solution)/shard_map/ppermute | solution.py:476
  40.6 12.2 %collective-permute-start.4 = (bf16[64,1536]{1,0:T(8,128)(2,1)S(1)}, bf16[64,1536]{1,0:T(8,128)(2,1)S(1)}, u32[]{:S(2)}, u32[]{:S(2)}) collective-permute-start(bf16[64,1536]{1,0:T(8,128)(2,1)S(1)} %get-tuple-element.257), channel_id=1, source_target_pairs={{64,0},{128,64},{192,128},{256,192},{320,256},{384,320},{448,384},... | collective-permute-start | bytes 589832 | tf_op jit(solution)/shard_map/ppermute | solution.py:476
  46.9 10.0 %collective-permute-start.5 = (bf16[64,1536]{1,0:T(8,128)(2,1)S(1)}, bf16[64,1536]{1,0:T(8,128)(2,1)S(1)}, u32[]{:S(2)}, u32[]{:S(2)}) collective-permute-start(bf16[64,1536]{1,0:T(8,128)(2,1)S(1)} %get-tuple-element.265), channel_id=1, source_target_pairs={{64,0},{128,64},{192,128},{256,192},{320,256},{384,320},{448,384},... | collective-permute-start | bytes 589832 | tf_op jit(solution)/shard_map/ppermute | solution.py:476
  53.5 12.0 %collective-permute-start.6 = (bf16[64,1536]{1,0:T(8,128)(2,1)S(1)}, bf16[64,1536]{1,0:T(8,128)(2,1)S(1)}, u32[]{:S(2)}, u32[]{:S(2)}) collective-permute-start(bf16[64,1536]{1,0:T(8,128)(2,1)S(1)} %get-tuple-element.273), channel_id=1, source_target_pairs={{64,0},{128,64},{192,128},{256,192},{320,256},{384,320},{448,384},... | collective-permute-start | bytes 589832 | tf_op jit(solution)/shard_map/ppermute | solution.py:476
  56.9 8.0 %copy-start.6 = (bf16[768,29]{0,1:T(8,128)(2,1)S(1)}, bf16[768,29]{0,1:T(8,128)(2,1)}, u32[]{:S(2)}) copy-start(bf16[768,29]{0,1:T(8,128)(2,1)} %param.17) | copy-start | bytes 133636
  56.9 8.0 %copy-start.7 = (s32[4,1]{0,1:T(1,128)S(1)}, s32[4,1]{0,1:T(1,128)}, u32[]{:S(2)}) copy-start(s32[4,1]{0,1:T(1,128)} %param.12) | copy-start | bytes 52
  57.5 10.6 %collective-permute-start.13 = (bf16[64,1536]{1,0:T(8,128)(2,1)S(1)}, bf16[64,1536]{1,0:T(8,128)(2,1)S(1)}, u32[]{:S(2)}, u32[]{:S(2)}) collective-permute-start(bf16[64,1536]{1,0:T(8,128)(2,1)S(1)} %get-tuple-element.274), channel_id=1, source_target_pairs={{64,0},{128,64},{192,128},{256,192},{320,256},{384,320},{448,384},... | collective-permute-start | bytes 589832 | tf_op jit(solution)/shard_map/ppermute | solution.py:476
  64.2 0.7 collective-permute-start.7
  66.1 16.8 %collective-permute-start.14 = (bf16[64,1536]{1,0:T(8,128)(2,1)S(1)}, bf16[64,1536]{1,0:T(8,128)(2,1)S(1)}, u32[]{:S(2)}, u32[]{:S(2)}) collective-permute-start(bf16[64,1536]{1,0:T(8,128)(2,1)S(1)} %get-tuple-element.295), channel_id=1, source_target_pairs={{64,0},{128,64},{192,128},{256,192},{320,256},{384,320},{448,384},... | collective-permute-start | bytes 589832 | tf_op jit(solution)/shard_map/ppermute | solution.py:476
  68.6 17.5 %collective-permute-start.15 = (bf16[64,1536]{1,0:T(8,128)(2,1)S(1)}, bf16[64,1536]{1,0:T(8,128)(2,1)S(1)}, u32[]{:S(2)}, u32[]{:S(2)}) collective-permute-start(bf16[64,1536]{1,0:T(8,128)(2,1)S(1)} %get-tuple-element.303), channel_id=1, source_target_pairs={{64,0},{128,64},{192,128},{256,192},{320,256},{384,320},{448,384},... | collective-permute-start | bytes 589832 | tf_op jit(solution)/shard_map/ppermute | solution.py:476
  84.2 10.7 %collective-permute-start.16 = (bf16[64,1536]{1,0:T(8,128)(2,1)S(1)}, bf16[64,1536]{1,0:T(8,128)(2,1)S(1)}, u32[]{:S(2)}, u32[]{:S(2)}) collective-permute-start(bf16[64,1536]{1,0:T(8,128)(2,1)S(1)} %get-tuple-element.311), channel_id=1, source_target_pairs={{64,0},{128,64},{192,128},{256,192},{320,256},{384,320},{448,384},... | collective-permute-start | bytes 589832 | tf_op jit(solution)/shard_map/ppermute | solution.py:476
  87.4 11.2 %collective-permute-start.17 = (bf16[64,1536]{1,0:T(8,128)(2,1)S(1)}, bf16[64,1536]{1,0:T(8,128)(2,1)S(1)}, u32[]{:S(2)}, u32[]{:S(2)}) collective-permute-start(bf16[64,1536]{1,0:T(8,128)(2,1)S(1)} %get-tuple-element.319), channel_id=1, source_target_pairs={{64,0},{128,64},{192,128},{256,192},{320,256},{384,320},{448,384},... | collective-permute-start | bytes 589832 | tf_op jit(solution)/shard_map/ppermute | solution.py:476
  96.1 9.8 %collective-permute-start.18 = (bf16[64,1536]{1,0:T(8,128)(2,1)S(1)}, bf16[64,1536]{1,0:T(8,128)(2,1)S(1)}, u32[]{:S(2)}, u32[]{:S(2)}) collective-permute-start(bf16[64,1536]{1,0:T(8,128)(2,1)S(1)} %get-tuple-element.327), channel_id=1, source_target_pairs={{64,0},{128,64},{192,128},{256,192},{320,256},{384,320},{448,384},... | collective-permute-start | bytes 589832 | tf_op jit(solution)/shard_map/ppermute | solution.py:476
  99.8 11.9 %collective-permute-start.19 = (bf16[64,1536]{1,0:T(8,128)(2,1)S(1)}, bf16[64,1536]{1,0:T(8,128)(2,1)S(1)}, u32[]{:S(2)}, u32[]{:S(2)}) collective-permute-start(bf16[64,1536]{1,0:T(8,128)(2,1)S(1)} %get-tuple-element.335), channel_id=1, source_target_pairs={{64,0},{128,64},{192,128},{256,192},{320,256},{384,320},{448,384},... | collective-permute-start | bytes 589832 | tf_op jit(solution)/shard_map/ppermute | solution.py:476
  107.2 9.9 %collective-permute-start.20 = (bf16[64,1536]{1,0:T(8,128)(2,1)S(1)}, bf16[64,1536]{1,0:T(8,128)(2,1)S(1)}, u32[]{:S(2)}, u32[]{:S(2)}) collective-permute-start(bf16[64,1536]{1,0:T(8,128)(2,1)S(1)} %get-tuple-element.343), channel_id=1, source_target_pairs={{64,0},{128,64},{192,128},{256,192},{320,256},{384,320},{448,384},... | collective-permute-start | bytes 589832 | tf_op jit(solution)/shard_map/ppermute | solution.py:476
  113.0 11.0 %collective-permute-start.21 = (bf16[64,1536]{1,0:T(8,128)(2,1)S(1)}, bf16[64,1536]{1,0:T(8,128)(2,1)S(1)}, u32[]{:S(2)}, u32[]{:S(2)}) collective-permute-start(bf16[64,1536]{1,0:T(8,128)(2,1)S(1)} %get-tuple-element.351), channel_id=1, source_target_pairs={{64,0},{128,64},{192,128},{256,192},{320,256},{384,320},{448,384},... | collective-permute-start | bytes 589832 | tf_op jit(solution)/shard_map/ppermute | solution.py:476
  118.5 9.4 %collective-permute-start.22 = (bf16[64,1536]{1,0:T(8,128)(2,1)S(1)}, bf16[64,1536]{1,0:T(8,128)(2,1)S(1)}, u32[]{:S(2)}, u32[]{:S(2)}) collective-permute-start(bf16[64,1536]{1,0:T(8,128)(2,1)S(1)} %get-tuple-element.359), channel_id=1, source_target_pairs={{64,0},{128,64},{192,128},{256,192},{320,256},{384,320},{448,384},... | collective-permute-start | bytes 589832 | tf_op jit(solution)/shard_map/ppermute | solution.py:476
  125.2 11.8 %collective-permute-start.23 = (bf16[64,1536]{1,0:T(8,128)(2,1)S(1)}, bf16[64,1536]{1,0:T(8,128)(2,1)S(1)}, u32[]{:S(2)}, u32[]{:S(2)}) collective-permute-start(bf16[64,1536]{1,0:T(8,128)(2,1)S(1)} %get-tuple-element.367), channel_id=1, source_target_pairs={{64,0},{128,64},{192,128},{256,192},{320,256},{384,320},{448,384},... | collective-permute-start | bytes 589832 | tf_op jit(solution)/shard_map/ppermute | solution.py:476
  128.5 13.3 %collective-permute-start.24 = (bf16[64,1536]{1,0:T(8,128)(2,1)S(1)}, bf16[64,1536]{1,0:T(8,128)(2,1)S(1)}, u32[]{:S(2)}, u32[]{:S(2)}) collective-permute-start(bf16[64,1536]{1,0:T(8,128)(2,1)S(1)} %get-tuple-element.375), channel_id=1, source_target_pairs={{64,0},{128,64},{192,128},{256,192},{320,256},{384,320},{448,384},... | collective-permute-start | bytes 589832 | tf_op jit(solution)/shard_map/ppermute | solution.py:476
  137.6 9.3 %collective-permute-start.25 = (bf16[64,1536]{1,0:T(8,128)(2,1)S(1)}, bf16[64,1536]{1,0:T(8,128)(2,1)S(1)}, u32[]{:S(2)}, u32[]{:S(2)}) collective-permute-start(bf16[64,1536]{1,0:T(8,128)(2,1)S(1)} %get-tuple-element.383), channel_id=1, source_target_pairs={{64,0},{128,64},{192,128},{256,192},{320,256},{384,320},{448,384},... | collective-permute-start | bytes 589832 | tf_op jit(solution)/shard_map/ppermute | solution.py:476
  140.4 0.7 collective-permute-start.29
  141.1 10.2 %collective-permute-start.30 = (bf16[32,1536]{1,0:T(8,128)(2,1)S(1)}, bf16[32,1536]{1,0:T(8,128)(2,1)S(1)}, u32[]{:S(2)}, u32[]{:S(2)}) collective-permute-start(bf16[32,1536]{1,0:T(8,128)(2,1)S(1)} %shard_map.158.held_ref), channel_id=1, source_target_pairs={{192,64},{448,320},{193,65},{449,321},{194,66},{450,322},{195,67},... | collective-permute-start | bytes 294920 | tf_op jit(solution)/shard_map/ppermute | solution.py:422
  149.4 17.0 %collective-permute-start.27 = (bf16[16,48,256]{2,1,0:T(8,128)(2,1)S(1)}, bf16[16,48,256]{2,1,0:T(8,128)(2,1)S(1)}, u32[]{:S(2)}, u32[]{:S(2)}) collective-permute-start(bf16[16,48,256]{2,1,0:T(8,128)(2,1)S(1)} %get-tuple-element.392), channel_id=1, source_target_pairs={{0,1},{1,0},{2,3},{3,2},{4,5},{5,4},{6,7},{7,6},{8,9},{9,8},{10,11... | collective-permute-start | bytes 1179656 | tf_op jit(solution)/shard_map/ppermute | solution.py:301
  151.4 9.1 %collective-permute-start.31 = (bf16[32,1536]{1,0:T(8,128)(2,1)S(1)}, bf16[32,1536]{1,0:T(8,128)(2,1)S(1)}, u32[]{:S(2)}, u32[]{:S(2)}) collective-permute-start(bf16[32,1536]{1,0:T(8,128)(2,1)S(1)} %shard_map.159.held_ref), channel_id=1, source_target_pairs={{64,0},{192,128},{320,256},{448,384},{65,1},{193,129},{321,257},{4... | collective-permute-start | bytes 294920 | tf_op jit(solution)/shard_map/ppermute | solution.py:422
  162.1 7.0 %collective-permute-start.32 = (bf16[2,16,16,256]{3,2,1,0:T(8,128)(2,1)S(1)}, bf16[2,16,16,256]{3,2,1,0:T(8,128)(2,1)S(1)}, u32[]{:S(2)}, u32[]{:S(2)}) collective-permute-start(bf16[2,16,16,256]{3,2,1,0:T(8,128)(2,1)S(1)} %get-tuple-element.402), channel_id=1, source_target_pairs={{0,1},{1,0},{2,3},{3,2},{4,5},{5,4},{6,7},{7,6},{8,9},{9,8},{10,11... | collective-permute-start | bytes 786440 | tf_op jit(solution)/shard_map/ppermute | solution.py:301
  164.1 34.1 %collective-permute-start.26 = (bf16[16,48,256]{2,1,0:T(8,128)(2,1)S(1)}, bf16[16,48,256]{2,1,0:T(8,128)(2,1)S(1)}, u32[]{:S(2)}, u32[]{:S(2)}) collective-permute-start(bf16[16,48,256]{2,1,0:T(8,128)(2,1)S(1)} %get-tuple-element.390), channel_id=1, source_target_pairs={{0,1},{1,0},{2,3},{3,2},{4,5},{5,4},{6,7},{7,6},{8,9},{9,8},{10,11... | collective-permute-start | bytes 1179656 | tf_op jit(solution)/shard_map/ppermute | solution.py:301
  166.6 31.7 %collective-permute-start.28 = (bf16[16,48,256]{2,1,0:T(8,128)(2,1)S(1)}, bf16[16,48,256]{2,1,0:T(8,128)(2,1)S(1)}, u32[]{:S(2)}, u32[]{:S(2)}) collective-permute-start(bf16[16,48,256]{2,1,0:T(8,128)(2,1)S(1)} %shard_map.157), channel_id=1, source_target_pairs={{0,32},{32,0},{1,33},{33,1},{2,34},{34,2},{3,35},{35,3},{4,36},{36... | collective-permute-start | bytes 1179656 | tf_op jit(solution)/shard_map/ppermute | solution.py:301
  169.3 13.1 %collective-permute-start.33 = (bf16[16,16,256]{2,1,0:T(8,128)(2,1)S(1)}, bf16[16,16,256]{2,1,0:T(8,128)(2,1)S(1)}, u32[]{:S(2)}, u32[]{:S(2)}) collective-permute-start(bf16[16,16,256]{2,1,0:T(8,128)(2,1)S(1)} %get-tuple-element.405), channel_id=1, source_target_pairs={{0,32},{32,0},{1,33},{33,1},{2,34},{34,2},{3,35},{35,3},{4,36},{36... | collective-permute-start | bytes 393224 | tf_op jit(solution)/shard_map/ppermute | solution.py:301
  183.0 29.3 %all-to-all-start.1 = ((bf16[16,16,256]{2,1,0:T(8,128)(2,1)}), bf16[16,16,256]{2,1,0:T(8,128)(2,1)S(1)}, u32[]{:S(2)}, u32[]{:S(2)}) async-start(bf16[16,16,256]{2,1,0:T(8,128)(2,1)} %shard_map.163), calls=%async_computation.1 | async-start | bytes 262144 | tf_op jit(solution)/shard_map/all_to_all | solution.py:500
  212.3 26.1 %all-to-all-start = ((bf16[16,48,256]{2,1,0:T(8,128)(2,1)}), bf16[16,48,256]{2,1,0:T(8,128)(2,1)S(1)}, u32[]{:S(2)}, u32[]{:S(2)}) async-start(bf16[16,48,256]{2,1,0:T(8,128)(2,1)} %add_convert_fusion), calls=%async_computation | async-start | bytes 786432 | tf_op jit(solution)/shard_map/all_to_all | solution.py:504

commit v5 on v4

--- a/solution.py
+++ b/solution.py
@@ -1,4 +1,5 @@
 import functools
+import math
 
 import jax
 import jax.numpy as jnp
@@ -48,7 +49,7 @@
             mine_ref[...] = first_ref[:, c * half : (c + 1) * half]
 
 
-def prepare_kernel(lens_ref, _yl, x_ref, gain_ref, wd_ref, wu_ref, *refs):
+def prepare_kernel(lens_ref, _sec, _yl, _zl, x_ref, gain_ref, wd_ref, wu_ref, *refs):
     xn_ref, h_ref, a_ref, q_ref, pooled_ref, wut_ref, wdt_ref, _, _ = refs
     micros, seq_len = 4, 128
     gain = gain_ref[0:1, :]
@@ -180,9 +181,9 @@
         rev_ref[...] = -REVERSAL * grad_pooled / per_row(lens_ref, (8, 1)).astype(F32)
 
 
-def critic_sums_kernel(band_rows, parts, sec_ref, yl_ref, core_ref, lines_ref, kept_ref, sent_ref, crit):
-    n_yl, n_z, n_c = parts
-    n_dp = n_yl * n_z * n_c
+def critic_sums_kernel(band_rows, parts, sec_ref, yl_ref, z_ref, core_ref, lines_ref, kept_ref, sent_ref, crit):
+    n_dp = math.prod(parts)
+    n_z = parts[1]
     features = lines_ref.shape[1]
     channels = features // 2
     padded = crit.shape[0] // n_dp
@@ -215,13 +216,10 @@
     crit[...] = lax.dot_general(gp, nb, dims, preferred_element_type=F32)
     crit[...] += lax.dot_general(hid, gl, dims, preferred_element_type=F32)
 
-    def pack(z, _):
-        for dy, dc, dest in places(parts, yl_ref, core_ref, z):
+    for i in range(n_z):
+        for dy, dc, dest in places(parts, yl_ref, core_ref, jnp.bitwise_xor(z_ref[0], mirrored(i, n_z))):
             piece = crit[pl.ds(pl.multiple_of(dest * padded, 16), padded), :].astype(BF16)
-            (sent_ref if dc else kept_ref)[dy, z] = piece
-        return 0
-
-    lax.fori_loop(0, n_z, pack, 0)
+            (sent_ref if dc else kept_ref)[dy, i] = piece
 
 
 def places(parts, yl_ref, core_ref, z):
@@ -235,6 +233,10 @@
     return found
 
 
+def mirrored(i, n):
+    return sum(((i >> b) & 1) * (n >> (b + 1)) for b in range(n.bit_length() - 1))
+
+
 def plus(left, right):
     return (left.astype(F32) + right.astype(F32)).astype(BF16)
 
@@ -245,6 +247,13 @@
         other_ref[...] = plus(kept_ref[1], got_ref[1])
 
 
+def fold_kernel(left_ref, right_ref, low_ref, high_ref):
+    total = plus(left_ref[...], right_ref[...])
+    half = low_ref.shape[0]
+    low_ref[...] = total[:half]
+    high_ref[...] = total[half:]
+
+
 def add_kernel(left_ref, right_ref, out_ref):
     out_ref[...] = plus(left_ref[...], right_ref[...])
 
@@ -263,7 +272,7 @@
 
 def finish_kernel(parts, yl_ref, core_ref, xn_ref, g_ref, h_ref, da_ref, *refs):
     outs, (down, up) = refs[:-2], refs[-2:]
-    n_yl, n_z, n_c = parts
+    n_yl, n_z, _ = parts
     features = xn_ref.shape[1]
     dims = (((0,), (0,)), ((), ()))
     width = 256
@@ -271,7 +280,7 @@
         cols = pl.ds(k * width, width)
         down[cols, :] = lax.dot_general(xn_ref[:, cols], da_ref[...], dims, preferred_element_type=F32)
         up[cols, :] = lax.dot_general(g_ref[:, cols], h_ref[...], dims, preferred_element_type=F32)
-    span = features // (n_yl * n_z * n_c)
+    span = features // math.prod(parts)
 
     def pack(z, _):
         for dy, dc, dest in places(parts, yl_ref, core_ref, z):
@@ -321,6 +330,7 @@
     sec_s = sec.reshape(1).astype(jnp.int32)
     core_s = core.reshape(1).astype(jnp.int32)
     yl_s = lax.axis_index("yl").reshape(1).astype(jnp.int32)
+    z_s = lax.axis_index("z").reshape(1).astype(jnp.int32)
     channels = critic_first.shape[1]
     half = channels // 2
     sds = jax.ShapeDtypeStruct
@@ -349,8 +359,8 @@
             sds((rows, features), BF16),
             sds((rows, rank), BF16),
         ),
-        [SM, SM] + [VM] * 4,
-        (lens, yl_s, x, gain, wd, w_up[0]),
+        [SM] * 4 + [VM] * 4,
+        (lens, sec_s, yl_s, z_s, x, gain, wd, w_up[0]),
         2 * rows * features * rank,
         8 << 20,
     )
@@ -377,7 +387,7 @@
             held["far"] = [lax.ppermute(held["pair"], SEC, [(i, three)]) for i in (7, 5, 1)]
         elif step == 1:
             held["pooled"] = lax.ppermute(after(pooled, token), SEC, [(4, three)])
-        elif step == 4:
+        elif step == 5:
             far = held["far"]
             held["own"] = join(token, far[2], held["pair"], far[1], far[0])
             pairs = [(three * 2, three * 2 + 1), (three * 2 + 1, three * 2)]
@@ -425,8 +435,8 @@
             kept, sent = call(
                 functools.partial(critic_sums_kernel, band_rows, parts),
                 (sds((n_yl, n_z, padded, rank), BF16),) * 2,
-                [SM, SM, SM, VM],
-                (after(sec_s, token), yl_s, core_s, held["lines"]),
+                [SM, SM, SM, SM, VM],
+                (after(sec_s, token), yl_s, z_s, core_s, held["lines"]),
                 1 << 26,
                 1 << 20,
                 scratch=[pltpu.VMEM((n_dp * padded, rank), F32)],
@@ -440,8 +450,16 @@
             if n_yl == 2:
                 held["other_sum"] = swap(other, "yl", n_yl)
         elif step == 18 and n_yl == 2:
-            args = (after(held["own_sum"], token), held["other_sum"])
-            held["own_sum"] = call(add_kernel, sds(args[0].shape, BF16), [VM, VM], args, 0, 1 << 20)
+            fold(after(held["own_sum"], token), held["other_sum"], 1)
+
+    def fold(left, right, bit):
+        size = left.shape[0]
+        if size == 1:
+            held["own_sum"] = call(add_kernel, sds(left.shape, BF16), [VM, VM], (left, right), 0, 1 << 18)
+            return
+        one = sds((size // 2,) + left.shape[1:], BF16)
+        held["own_sum"], high = call(fold_kernel, (one, one), [VM, VM], (left, right), 0, 1 << 20)
+        held["other_sum"] = lax.ppermute(high, "z", [(i, i ^ bit) for i in range(n_z)])
 
     steps = DELAY * (SECTIONS - 1) + chunks
     received = {}
@@ -481,7 +499,7 @@
     packed = call(
         functools.partial(finish_kernel, parts),
         (piece,) * (n_yl * n_c),
-        [SM, SM] + [VM] * 4,
+        [SM] * 2 + [VM] * 4,
         (yl_s, core_s, xn, grads, h, inner),
         4 * rows * features * rank,
         8 << 20,
@@ -495,17 +513,19 @@
         args = (kept[i], arrived)
         halves[i] = call(add_kernel, sds(arrived.shape, BF16), [VM, VM], args, 0, 2 << 20)
     summed = halves[0]
-    crit = after(held["own_sum"], packed[-1])
-    if n_z > 1:
-        crit = lax.all_to_all(crit, "z", 0, 0, tiled=True)
     if n_yl == 2:
-        summed = plus(summed, swap(halves[1], "yl", n_yl))
+        arrived = swap(halves[1], "yl", n_yl)
+        bit = 2
+        while bit <= n_z:
+            fold(held["own_sum"], held["other_sum"], bit)
+            bit *= 2
+        summed = call(add_kernel, sds(arrived.shape, BF16), [VM, VM], (summed, arrived), 0, 2 << 20)
     if n_z > 1:
         summed = lax.all_to_all(summed, "z", 0, 0, tiled=True)
     total = jnp.sum(summed.astype(F32), axis=0)
     down = total[:span]
     up = total[span:].T
-    crit = jnp.sum(crit.astype(F32), axis=0)[:share]
+    crit = held["own_sum"][0, :share].astype(F32)
     dp_place = lax.axis_index(("yl", "z", "c"))
     wd_own = lax.dynamic_slice_in_dim(wd, dp_place * span, span, 0).astype(F32)
     gain_own = lax.dynamic_slice_in_dim(gain[0], dp_place * span, span, 0)
@@ -517,7 +537,7 @@
 
 def solution(mesh):
     n_dp = mesh.shape["dp"]
-    parts = (2, n_dp // 4, 2) if n_dp >= 8 else (1, n_dp // 2, 2)
+    parts = (2, n_dp // 4, 2) if n_dp >= 4 else (1, n_dp // 2, 2)
     fine = Mesh(mesh.devices.reshape((SECTIONS // 2, 2) + parts), SEC + ("yl", "z", "c"))
     dp = ("yl", "z", "c")
     return jax.shard_map(

time: 241 us -> 254 us (1.054)
  the two profiles are of different devices: /device:TPU:2 before, /device:TPU:4 now
where the time goes in v5:
time: 254 us; the launch traced here: 253 us
  starting transfers between devices  165 us (65%)
  waiting for transfers between devices  55.1 us (22%)
  Pallas kernels  25.9 us (10%)
  local copies, waits for them, and re-layouts  3.8 us (1%)
    ppermute x20, starting transfers between devices, whole(): received[step] = lax.ppermute(outgoing, SEC, relay_route)  93 us
    ppermute x4, starting transfers between devices, fold(): lax.ppermute(high, 'z', [(i, i ^ bit) for i in range(n_z)])  29.9 us
    pallas_call x41, Pallas kernels, call(): pl.pallas_call(kernel, out_shape=out_shape, in_specs=in_specs, out_specs=...  25.9 us
    all_to_all x1, starting transfers between devices, whole(): summed = lax.all_to_all(summed, 'z', 0, 0, tiled=True)  16.1 us
    ppermute x20, waiting for transfers between devices, whole(): received[step] = lax.ppermute(outgoing, SEC, relay_route)  15.9 us
    ppermute x5, waiting for transfers between devices, swap(): return lax.ppermute(block, axis, [(i, size - 1 - i) for i in range(size)])  15.6 us
    ppermute x3, waiting for transfers between devices, side_work(): moved = lax.ppermute(lines, SEC, route)  14.2 us
    ppermute x5, starting transfers between devices, swap(): return lax.ppermute(block, axis, [(i, size - 1 - i) for i in range(size)])  12.4 us
  transfers between devices with their start and end apart: 39, of which 18 were waited for; matrix products, arithmetic and copies ran while one was open for 1% of the time, Pallas kernels for 9%

profile of v5, /device:TPU:4, one launch (start us, length us, event | category | flops | bytes accessed | tf_op | source)
XLA Modules:
  0.0 252.6 jit_solution(13439524522810396752)
XLA Ops:
  0.7 1.5 copy.323
  2.2 1.0 copy-done.4
  3.2 5.1 %collective-permute-start.8 = (bf16[192,384]{1,0:T(8,128)(2,1)S(1)}, bf16[192,384]{1,0:T(8,128)(2,1)S(1)}, u32[]{:S(2)}, u32[]{:S(2)}) collective-permute-start(bf16[192,384]{1,0:T(8,128)(2,1)S(1)} %shard_map.137.refs_1_), channel_id=1, source_target_pairs={{0,64},{128,192},{256,320},{384,448},{1,65},{129,193},{257,321},{3... | collective-permute-start | bytes 442376 | tf_op jit(solution)/shard_map/ppermute | solution.py:347
  8.4 1.9 shard_map.128
  10.9 1.9 collective-permute-start
  13.4 5.4 %collective-permute-start.1 = (bf16[64,1536]{1,0:T(8,128)(2,1)S(1)}, bf16[64,1536]{1,0:T(8,128)(2,1)S(1)}, u32[]{:S(2)}, u32[]{:S(2)}) collective-permute-start(bf16[64,1536]{1,0:T(8,128)(2,1)S(1)} %get-tuple-element.240), channel_id=1, source_target_pairs={{64,0},{128,64},{192,128},{256,192},{320,256},{384,320},{448,384},... | collective-permute-start | bytes 589832 | tf_op jit(solution)/shard_map/ppermute | solution.py:494
  20.9 1.2 collective-permute-done.refs_9_
  22.6 2.6 %collective-permute-start.2 = (bf16[64,1536]{1,0:T(8,128)(2,1)S(1)}, bf16[64,1536]{1,0:T(8,128)(2,1)S(1)}, u32[]{:S(2)}, u32[]{:S(2)}) collective-permute-start(bf16[64,1536]{1,0:T(8,128)(2,1)S(1)} %get-tuple-element.248), channel_id=1, source_target_pairs={{64,0},{128,64},{192,128},{256,192},{320,256},{384,320},{448,384},... | collective-permute-start | bytes 589832 | tf_op jit(solution)/shard_map/ppermute | solution.py:494
  25.9 5.1 %collective-permute-start.3 = (bf16[64,1536]{1,0:T(8,128)(2,1)S(1)}, bf16[64,1536]{1,0:T(8,128)(2,1)S(1)}, u32[]{:S(2)}, u32[]{:S(2)}) collective-permute-start(bf16[64,1536]{1,0:T(8,128)(2,1)S(1)} %get-tuple-element.256), channel_id=1, source_target_pairs={{64,0},{128,64},{192,128},{256,192},{320,256},{384,320},{448,384},... | collective-permute-start | bytes 589832 | tf_op jit(solution)/shard_map/ppermute | solution.py:494
  31.0 1.6 collective-permute-done.2.refs_9_
  33.1 2.8 %collective-permute-done.3.refs_9_ = bf16[64,1536]{1,0:T(8,128)(2,1)S(1)} collective-permute-done((bf16[64,1536]{1,0:T(8,128)(2,1)S(1)}, bf16[64,1536]{1,0:T(8,128)(2,1)S(1)}, u32[]{:S(2)}, u32[]{:S(2)}) %collective-permute-start.3) | collective-permute-done | bytes 196640 | tf_op jit(solution)/shard_map/ppermute | solution.py:494
  37.3 6.3 %collective-permute-start.4 = (bf16[64,1536]{1,0:T(8,128)(2,1)S(1)}, bf16[64,1536]{1,0:T(8,128)(2,1)S(1)}, u32[]{:S(2)}, u32[]{:S(2)}) collective-permute-start(bf16[64,1536]{1,0:T(8,128)(2,1)S(1)} %get-tuple-element.264), channel_id=1, source_target_pairs={{64,0},{128,64},{192,128},{256,192},{320,256},{384,320},{448,384},... | collective-permute-start | bytes 589832 | tf_op jit(solution)/shard_map/ppermute | solution.py:494
  43.6 2.2 collective-permute-start.5
  45.8 3.1 %collective-permute-done.4.refs_9_ = bf16[64,1536]{1,0:T(8,128)(2,1)S(1)} collective-permute-done((bf16[64,1536]{1,0:T(8,128)(2,1)S(1)}, bf16[64,1536]{1,0:T(8,128)(2,1)S(1)}, u32[]{:S(2)}, u32[]{:S(2)}) %collective-permute-start.4) | collective-permute-done | bytes 196640 | tf_op jit(solution)/shard_map/ppermute | solution.py:494
  48.9 1.2 shard_map.135
  50.1 6.1 %collective-permute-start.6 = (bf16[64,1536]{1,0:T(8,128)(2,1)S(1)}, bf16[64,1536]{1,0:T(8,128)(2,1)S(1)}, u32[]{:S(2)}, u32[]{:S(2)}) collective-permute-start(bf16[64,1536]{1,0:T(8,128)(2,1)S(1)} %get-tuple-element.280), channel_id=1, source_target_pairs={{64,0},{128,64},{192,128},{256,192},{320,256},{384,320},{448,384},... | collective-permute-start | bytes 589832 | tf_op jit(solution)/shard_map/ppermute | solution.py:494
  56.3 1.3 shard_map.136
  57.5 2.4 collective-permute-start.13
  60.0 3.0 %collective-permute-start.7 = (f32[8,1536]{1,0:T(8,128)S(1)}, f32[8,1536]{1,0:T(8,128)S(1)}, u32[]{:S(2)}, u32[]{:S(2)}) collective-permute-start(f32[8,1536]{1,0:T(8,128)S(1)} %get-tuple-element.284), channel_id=1, source_target_pairs={{256,192},{257,193},{258,194},{259,195},{260,196},{261,197},{262,1... | collective-permute-start | bytes 147464 | tf_op jit(solution)/shard_map/ppermute | solution.py:389
  63.0 2.0 collective-permute-done.7.pooled_ref
  65.5 1.2 shard_map.141
  66.8 8.4 %collective-permute-start.14 = (bf16[64,1536]{1,0:T(8,128)(2,1)S(1)}, bf16[64,1536]{1,0:T(8,128)(2,1)S(1)}, u32[]{:S(2)}, u32[]{:S(2)}) collective-permute-start(bf16[64,1536]{1,0:T(8,128)(2,1)S(1)} %get-tuple-element.302), channel_id=1, source_target_pairs={{64,0},{128,64},{192,128},{256,192},{320,256},{384,320},{448,384},... | collective-permute-start | bytes 589832 | tf_op jit(solution)/shard_map/ppermute | solution.py:494
  75.3 1.2 shard_map.142
  76.5 2.0 collective-permute-start.15
  78.5 1.0 collective-permute-done.14.refs_8_
  79.5 1.2 shard_map.143
  80.7 6.8 %collective-permute-start.16 = (bf16[64,1536]{1,0:T(8,128)(2,1)S(1)}, bf16[64,1536]{1,0:T(8,128)(2,1)S(1)}, u32[]{:S(2)}, u32[]{:S(2)}) collective-permute-start(bf16[64,1536]{1,0:T(8,128)(2,1)S(1)} %get-tuple-element.318), channel_id=1, source_target_pairs={{64,0},{128,64},{192,128},{256,192},{320,256},{384,320},{448,384},... | collective-permute-start | bytes 589832 | tf_op jit(solution)/shard_map/ppermute | solution.py:494
  87.6 1.2 shard_map.144
  88.8 2.0 collective-permute-start.17
  90.8 0.9 collective-permute-done.16.refs_8_
  91.7 1.2 shard_map.145
  92.9 6.8 %collective-permute-start.18 = (bf16[64,1536]{1,0:T(8,128)(2,1)S(1)}, bf16[64,1536]{1,0:T(8,128)(2,1)S(1)}, u32[]{:S(2)}, u32[]{:S(2)}) collective-permute-start(bf16[64,1536]{1,0:T(8,128)(2,1)S(1)} %get-tuple-element.334), channel_id=1, source_target_pairs={{64,0},{128,64},{192,128},{256,192},{320,256},{384,320},{448,384},... | collective-permute-start | bytes 589832 | tf_op jit(solution)/shard_map/ppermute | solution.py:494
  99.8 1.2 shard_map.146
  101.0 2.6 %collective-permute-start.19 = (bf16[64,1536]{1,0:T(8,128)(2,1)S(1)}, bf16[64,1536]{1,0:T(8,128)(2,1)S(1)}, u32[]{:S(2)}, u32[]{:S(2)}) collective-permute-start(bf16[64,1536]{1,0:T(8,128)(2,1)S(1)} %get-tuple-element.342), channel_id=1, source_target_pairs={{64,0},{128,64},{192,128},{256,192},{320,256},{384,320},{448,384},... | collective-permute-start | bytes 589832 | tf_op jit(solution)/shard_map/ppermute | solution.py:494
  104.3 7.5 %collective-permute-start.20 = (bf16[64,1536]{1,0:T(8,128)(2,1)S(1)}, bf16[64,1536]{1,0:T(8,128)(2,1)S(1)}, u32[]{:S(2)}, u32[]{:S(2)}) collective-permute-start(bf16[64,1536]{1,0:T(8,128)(2,1)S(1)} %get-tuple-element.350), channel_id=1, source_target_pairs={{64,0},{128,64},{192,128},{256,192},{320,256},{384,320},{448,384},... | collective-permute-start | bytes 589832 | tf_op jit(solution)/shard_map/ppermute | solution.py:494
  112.5 4.5 %collective-permute-start.21 = (bf16[64,1536]{1,0:T(8,128)(2,1)S(1)}, bf16[64,1536]{1,0:T(8,128)(2,1)S(1)}, u32[]{:S(2)}, u32[]{:S(2)}) collective-permute-start(bf16[64,1536]{1,0:T(8,128)(2,1)S(1)} %get-tuple-element.358), channel_id=1, source_target_pairs={{64,0},{128,64},{192,128},{256,192},{320,256},{384,320},{448,384},... | collective-permute-start | bytes 589832 | tf_op jit(solution)/shard_map/ppermute | solution.py:494
  117.8 6.1 %collective-permute-start.22 = (bf16[64,1536]{1,0:T(8,128)(2,1)S(1)}, bf16[64,1536]{1,0:T(8,128)(2,1)S(1)}, u32[]{:S(2)}, u32[]{:S(2)}) collective-permute-start(bf16[64,1536]{1,0:T(8,128)(2,1)S(1)} %get-tuple-element.366), channel_id=1, source_target_pairs={{64,0},{128,64},{192,128},{256,192},{320,256},{384,320},{448,384},... | collective-permute-start | bytes 589832 | tf_op jit(solution)/shard_map/ppermute | solution.py:494
  124.5 4.2 %collective-permute-start.23 = (bf16[64,1536]{1,0:T(8,128)(2,1)S(1)}, bf16[64,1536]{1,0:T(8,128)(2,1)S(1)}, u32[]{:S(2)}, u32[]{:S(2)}) collective-permute-start(bf16[64,1536]{1,0:T(8,128)(2,1)S(1)} %get-tuple-element.374), channel_id=1, source_target_pairs={{64,0},{128,64},{192,128},{256,192},{320,256},{384,320},{448,384},... | collective-permute-start | bytes 589832 | tf_op jit(solution)/shard_map/ppermute | solution.py:494
  129.8 6.8 %collective-permute-start.24 = (bf16[64,1536]{1,0:T(8,128)(2,1)S(1)}, bf16[64,1536]{1,0:T(8,128)(2,1)S(1)}, u32[]{:S(2)}, u32[]{:S(2)}) collective-permute-start(bf16[64,1536]{1,0:T(8,128)(2,1)S(1)} %get-tuple-element.382), channel_id=1, source_target_pairs={{64,0},{128,64},{192,128},{256,192},{320,256},{384,320},{448,384},... | collective-permute-start | bytes 589832 | tf_op jit(solution)/shard_map/ppermute | solution.py:494
  137.1 3.1 %collective-permute-start.25 = (bf16[64,1536]{1,0:T(8,128)(2,1)S(1)}, bf16[64,1536]{1,0:T(8,128)(2,1)S(1)}, u32[]{:S(2)}, u32[]{:S(2)}) collective-permute-start(bf16[64,1536]{1,0:T(8,128)(2,1)S(1)} %get-tuple-element.390), channel_id=1, source_target_pairs={{64,0},{128,64},{192,128},{256,192},{320,256},{384,320},{448,384},... | collective-permute-start | bytes 589832 | tf_op jit(solution)/shard_map/ppermute | solution.py:494
  140.2 1.3 shard_map.153
  141.5 4.7 %collective-permute-done.25.refs_8_ = bf16[64,1536]{1,0:T(8,128)(2,1)S(1)} collective-permute-done((bf16[64,1536]{1,0:T(8,128)(2,1)S(1)}, bf16[64,1536]{1,0:T(8,128)(2,1)S(1)}, u32[]{:S(2)}, u32[]{:S(2)}) %collective-permute-start.25) | collective-permute-done | bytes 196640 | tf_op jit(solution)/shard_map/ppermute | solution.py:494
  146.2 1.2 shard_map.154
  147.5 1.3 shard_map.155
  148.8 1.9 collective-permute-start.27
  150.7 2.4 collective-permute-start.26
  153.3 3.5 %collective-permute-start.28 = (bf16[16,48,256]{2,1,0:T(8,128)(2,1)S(1)}, bf16[16,48,256]{2,1,0:T(8,128)(2,1)S(1)}, u32[]{:S(2)}, u32[]{:S(2)}) collective-permute-start(bf16[16,48,256]{2,1,0:T(8,128)(2,1)S(1)} %shard_map.157), channel_id=1, source_target_pairs={{0,32},{32,0},{1,33},{33,1},{2,34},{34,2},{3,35},{35,3},{4,36},{36... | collective-permute-start | bytes 1179656 | tf_op jit(solution)/shard_map/ppermute | solution.py:310
  156.9 9.3 %collective-permute-done.28.right_ref = bf16[16,48,256]{2,1,0:T(8,128)(2,1)S(1)} collective-permute-done((bf16[16,48,256]{2,1,0:T(8,128)(2,1)S(1)}, bf16[16,48,256]{2,1,0:T(8,128)(2,1)S(1)}, u32[]{:S(2)}, u32[]{:S(2)}) %collective-permute-start.28) | collective-permute-done | bytes 393248 | tf_op jit(solution)/shard_map/ppermute | solution.py:310
  167.0 16.1 %all-to-all-start = ((bf16[16,48,256]{2,1,0:T(8,128)(2,1)}), bf16[16,48,256]{2,1,0:T(8,128)(2,1)S(1)}, u32[]{:S(2)}, u32[]{:S(2)}) async-start(bf16[16,48,256]{2,1,0:T(8,128)(2,1)} %shard_map.158), calls=%async_computation | async-start | bytes 786432 | tf_op jit(solution)/shard_map/all_to_all | solution.py:524
  184.6 1.3 collective-permute-start.31
  185.9 14.2 %collective-permute-done.31.moved_ref = bf16[32,1536]{1,0:T(8,128)(2,1)S(1)} collective-permute-done((bf16[32,1536]{1,0:T(8,128)(2,1)S(1)}, bf16[32,1536]{1,0:T(8,128)(2,1)S(1)}, u32[]{:S(2)}, u32[]{:S(2)}) %collective-permute-start.31) | collective-permute-done | bytes 98336 | tf_op jit(solution)/shard_map/ppermute | solution.py:432
  200.0 1.4 shard_map.162
  201.4 1.9 collective-permute-start.32
  203.4 1.5 collective-permute-done.32.got_ref
  204.9 2.6 %collective-permute-start.33 = (bf16[16,16,256]{2,1,0:T(8,128)(2,1)S(1)}, bf16[16,16,256]{2,1,0:T(8,128)(2,1)S(1)}, u32[]{:S(2)}, u32[]{:S(2)}) collective-permute-start(bf16[16,16,256]{2,1,0:T(8,128)(2,1)S(1)} %get-tuple-element.412), channel_id=1, source_target_pairs={{0,32},{32,0},{1,33},{33,1},{2,34},{34,2},{3,35},{35,3},{4,36},{36... | collective-permute-start | bytes 393224 | tf_op jit(solution)/shard_map/ppermute | solution.py:310
  207.6 4.8 %collective-permute-done.33.right_ref = bf16[16,16,256]{2,1,0:T(8,128)(2,1)S(1)} collective-permute-done((bf16[16,16,256]{2,1,0:T(8,128)(2,1)S(1)}, bf16[16,16,256]{2,1,0:T(8,128)(2,1)S(1)}, u32[]{:S(2)}, u32[]{:S(2)}) %collective-permute-start.33) | collective-permute-done | bytes 131104 | tf_op jit(solution)/shard_map/ppermute | solution.py:310
  212.4 4.1 %collective-permute-start.34 = (bf16[8,16,256]{2,1,0:T(8,128)(2,1)S(1)}, bf16[8,16,256]{2,1,0:T(8,128)(2,1)S(1)}, u32[]{:S(2)}, u32[]{:S(2)}) collective-permute-start(bf16[8,16,256]{2,1,0:T(8,128)(2,1)S(1)} %get-tuple-element.414), channel_id=1, source_target_pairs={{0,2},{2,0},{4,6},{6,4},{8,10},{10,8},{12,14},{14,12},{16,18},{18,... | collective-permute-start | bytes 196616 | tf_op jit(solution)/shard_map/ppermute | solution.py:462
  216.5 2.2 collective-permute-done.34.right_ref
  218.7 4.8 %collective-permute-start.35 = (bf16[4,16,256]{2,1,0:T(8,128)(2,1)S(1)}, bf16[4,16,256]{2,1,0:T(8,128)(2,1)S(1)}, u32[]{:S(2)}, u32[]{:S(2)}) collective-permute-start(bf16[4,16,256]{2,1,0:T(8,128)(2,1)S(1)} %get-tuple-element.416), channel_id=1, source_target_pairs={{0,4},{2,6},{4,0},{6,2},{8,12},{10,14},{12,8},{14,10},{16,20},{18,... | collective-permute-start | bytes 98312 | tf_op jit(solution)/shard_map/ppermute | solution.py:462
  223.6 1.9 collective-permute-done.35.right_ref
  225.4 7.8 %collective-permute-start.36 = (bf16[2,16,256]{2,1,0:T(8,128)(2,1)S(1)}, bf16[2,16,256]{2,1,0:T(8,128)(2,1)S(1)}, u32[]{:S(2)}, u32[]{:S(2)}) collective-permute-start(bf16[2,16,256]{2,1,0:T(8,128)(2,1)S(1)} %get-tuple-element.418), channel_id=1, source_target_pairs={{0,8},{2,10},{4,12},{6,14},{8,0},{10,2},{12,4},{14,6},{16,24},{18,... | collective-permute-start | bytes 49160 | tf_op jit(solution)/shard_map/ppermute | solution.py:462
  233.3 1.7 collective-permute-done.36.right_ref
  235.0 13.2 %collective-permute-start.37 = (bf16[1,16,256]{2,1,0:T(8,128)(2,1)S(1)}, bf16[1,16,256]{2,1,0:T(8,128)(2,1)S(1)}, u32[]{:S(2)}, u32[]{:S(2)}) collective-permute-start(bf16[1,16,256]{2,1,0:T(8,128)(2,1)S(1)} %get-tuple-element.420), channel_id=1, source_target_pairs={{0,16},{2,18},{4,20},{6,22},{8,24},{10,26},{12,28},{14,30},{16,0},... | collective-permute-start | bytes 24584 | tf_op jit(solution)/shard_map/ppermute | solution.py:462
  248.2 1.7 collective-permute-done.37.right_ref
  (78 shorter events, 16.3 us)
Async XLA Ops:
  0.6 7.7 %copy-start.5 = (s32[4,1]{0,1:T(1,128)S(1)}, s32[4,1]{0,1:T(1,128)}, u32[]{:S(2)}) copy-start(s32[4,1]{0,1:T(1,128)} %param.11) | copy-start | bytes 52
  0.6 7.7 %copy-start.1 = (f32[1,1536]{1,0:T(1,128)S(1)}, f32[1,1536]{1,0:T(1,128)}, u32[]{:S(2)}) copy-start(f32[1,1536]{1,0:T(1,128)} %refs_5_.43) | copy-start | bytes 18436
  0.7 7.7 %copy-start.2 = (bf16[1,1536,256]{2,1,0:T(8,128)(2,1)S(1)}, bf16[1,1536,256]{2,1,0:T(8,128)(2,1)}, u32[]{:S(2)}) copy-start(bf16[1,1536,256]{2,1,0:T(8,128)(2,1)} %param.14) | copy-start | bytes 2359300
  0.7 7.7 %copy-start.3 = (bf16[1,256,1536]{2,1,0:T(8,128)(2,1)S(1)}, bf16[1,256,1536]{2,1,0:T(8,128)(2,1)}, u32[]{:S(2)}) copy-start(bf16[1,256,1536]{2,1,0:T(8,128)(2,1)} %param.15) | copy-start | bytes 2359300
  2.2 1.0 copy-start.4
  3.2 15.6 %collective-permute-start.8 = (bf16[192,384]{1,0:T(8,128)(2,1)S(1)}, bf16[192,384]{1,0:T(8,128)(2,1)S(1)}, u32[]{:S(2)}, u32[]{:S(2)}) collective-permute-start(bf16[192,384]{1,0:T(8,128)(2,1)S(1)} %shard_map.137.refs_1_), channel_id=1, source_target_pairs={{0,64},{128,192},{256,320},{384,448},{1,65},{129,193},{257,321},{3... | collective-permute-start | bytes 442376 | tf_op jit(solution)/shard_map/ppermute | solution.py:347
  8.4 2.0 copy-start
  10.9 11.2 %collective-permute-start = (bf16[64,1536]{1,0:T(8,128)(2,1)S(1)}, bf16[64,1536]{1,0:T(8,128)(2,1)S(1)}, u32[]{:S(2)}, u32[]{:S(2)}) collective-permute-start(bf16[64,1536]{1,0:T(8,128)(2,1)S(1)} %get-tuple-element.232), channel_id=1, source_target_pairs={{64,0},{128,64},{192,128},{256,192},{320,256},{384,320},{448,384},... | collective-permute-start | bytes 589832 | tf_op jit(solution)/shard_map/ppermute | solution.py:494
  13.4 11.9 %collective-permute-start.1 = (bf16[64,1536]{1,0:T(8,128)(2,1)S(1)}, bf16[64,1536]{1,0:T(8,128)(2,1)S(1)}, u32[]{:S(2)}, u32[]{:S(2)}) collective-permute-start(bf16[64,1536]{1,0:T(8,128)(2,1)S(1)} %get-tuple-element.240), channel_id=1, source_target_pairs={{64,0},{128,64},{192,128},{256,192},{320,256},{384,320},{448,384},... | collective-permute-start | bytes 589832 | tf_op jit(solution)/shard_map/ppermute | solution.py:494
  18.8 17.7 %collective-permute-start.11 = (bf16[384,384]{1,0:T(8,128)(2,1)S(1)}, bf16[384,384]{1,0:T(8,128)(2,1)S(1)}, u32[]{:S(2)}, u32[]{:S(2)}) collective-permute-start(bf16[384,384]{1,0:T(8,128)(2,1)S(1)} %shard_map.138.refs_1_), channel_id=1, source_target_pairs={{448,192},{449,193},{450,194},{451,195},{452,196},{453,197},{454,1... | collective-permute-start | bytes 884744 | tf_op jit(solution)/shard_map/ppermute | solution.py:387
  19.5 17.0 %collective-permute-start.10 = (bf16[384,384]{1,0:T(8,128)(2,1)S(1)}, bf16[384,384]{1,0:T(8,128)(2,1)S(1)}, u32[]{:S(2)}, u32[]{:S(2)}) collective-permute-start(bf16[384,384]{1,0:T(8,128)(2,1)S(1)} %shard_map.138.refs_1_), channel_id=1, source_target_pairs={{320,192},{321,193},{322,194},{323,195},{324,196},{325,197},{326,1... | collective-permute-start | bytes 884744 | tf_op jit(solution)/shard_map/ppermute | solution.py:387
  20.2 16.3 %collective-permute-start.9 = (bf16[384,384]{1,0:T(8,128)(2,1)S(1)}, bf16[384,384]{1,0:T(8,128)(2,1)S(1)}, u32[]{:S(2)}, u32[]{:S(2)}) collective-permute-start(bf16[384,384]{1,0:T(8,128)(2,1)S(1)} %shard_map.138.refs_1_), channel_id=1, source_target_pairs={{64,192},{65,193},{66,194},{67,195},{68,196},{69,197},{70,198},{71... | collective-permute-start | bytes 884744 | tf_op jit(solution)/shard_map/ppermute | solution.py:387
  22.6 9.9 %collective-permute-start.2 = (bf16[64,1536]{1,0:T(8,128)(2,1)S(1)}, bf16[64,1536]{1,0:T(8,128)(2,1)S(1)}, u32[]{:S(2)}, u32[]{:S(2)}) collective-permute-start(bf16[64,1536]{1,0:T(8,128)(2,1)S(1)} %get-tuple-element.248), channel_id=1, source_target_pairs={{64,0},{128,64},{192,128},{256,192},{320,256},{384,320},{448,384},... | collective-permute-start | bytes 589832 | tf_op jit(solution)/shard_map/ppermute | solution.py:494
  25.9 10.0 %collective-permute-start.3 = (bf16[64,1536]{1,0:T(8,128)(2,1)S(1)}, bf16[64,1536]{1,0:T(8,128)(2,1)S(1)}, u32[]{:S(2)}, u32[]{:S(2)}) collective-permute-start(bf16[64,1536]{1,0:T(8,128)(2,1)S(1)} %get-tuple-element.256), channel_id=1, source_target_pairs={{64,0},{128,64},{192,128},{256,192},{320,256},{384,320},{448,384},... | collective-permute-start | bytes 589832 | tf_op jit(solution)/shard_map/ppermute | solution.py:494
  36.5 28.4 %collective-permute-start.12 = (bf16[1536,384]{1,0:T(8,128)(2,1)S(1)}, bf16[1536,384]{1,0:T(8,128)(2,1)S(1)}, u32[]{:S(2)}, u32[]{:S(2)}) collective-permute-start(bf16[1536,384]{1,0:T(8,128)(2,1)S(1)} %shard_map.139.own_ref), channel_id=1, source_target_pairs={{192,193},{193,192},{194,195},{195,194},{196,197},{197,196},{198,1... | collective-permute-start | bytes 3538952 | tf_op jit(solution)/shard_map/ppermute | solution.py:394
  37.3 11.6 %collective-permute-start.4 = (bf16[64,1536]{1,0:T(8,128)(2,1)S(1)}, bf16[64,1536]{1,0:T(8,128)(2,1)S(1)}, u32[]{:S(2)}, u32[]{:S(2)}) collective-permute-start(bf16[64,1536]{1,0:T(8,128)(2,1)S(1)} %get-tuple-element.264), channel_id=1, source_target_pairs={{64,0},{128,64},{192,128},{256,192},{320,256},{384,320},{448,384},... | collective-permute-start | bytes 589832 | tf_op jit(solution)/shard_map/ppermute | solution.py:494
  43.6 12.7 %collective-permute-start.5 = (bf16[64,1536]{1,0:T(8,128)(2,1)S(1)}, bf16[64,1536]{1,0:T(8,128)(2,1)S(1)}, u32[]{:S(2)}, u32[]{:S(2)}) collective-permute-start(bf16[64,1536]{1,0:T(8,128)(2,1)S(1)} %get-tuple-element.272), channel_id=1, source_target_pairs={{64,0},{128,64},{192,128},{256,192},{320,256},{384,320},{448,384},... | collective-permute-start | bytes 589832 | tf_op jit(solution)/shard_map/ppermute | solution.py:494
  50.1 15.4 %collective-permute-start.6 = (bf16[64,1536]{1,0:T(8,128)(2,1)S(1)}, bf16[64,1536]{1,0:T(8,128)(2,1)S(1)}, u32[]{:S(2)}, u32[]{:S(2)}) collective-permute-start(bf16[64,1536]{1,0:T(8,128)(2,1)S(1)} %get-tuple-element.280), channel_id=1, source_target_pairs={{64,0},{128,64},{192,128},{256,192},{320,256},{384,320},{448,384},... | collective-permute-start | bytes 589832 | tf_op jit(solution)/shard_map/ppermute | solution.py:494
  56.2 8.7 %copy-start.6 = (bf16[768,29]{0,1:T(8,128)(2,1)S(1)}, bf16[768,29]{0,1:T(8,128)(2,1)}, u32[]{:S(2)}) copy-start(bf16[768,29]{0,1:T(8,128)(2,1)} %param.17) | copy-start | bytes 133636
  56.3 8.7 %copy-start.7 = (s32[4,1]{0,1:T(1,128)S(1)}, s32[4,1]{0,1:T(1,128)}, u32[]{:S(2)}) copy-start(s32[4,1]{0,1:T(1,128)} %param.12) | copy-start | bytes 52
  57.5 17.7 %collective-permute-start.13 = (bf16[64,1536]{1,0:T(8,128)(2,1)S(1)}, bf16[64,1536]{1,0:T(8,128)(2,1)S(1)}, u32[]{:S(2)}, u32[]{:S(2)}) collective-permute-start(bf16[64,1536]{1,0:T(8,128)(2,1)S(1)} %get-tuple-element.281), channel_id=1, source_target_pairs={{64,0},{128,64},{192,128},{256,192},{320,256},{384,320},{448,384},... | collective-permute-start | bytes 589832 | tf_op jit(solution)/shard_map/ppermute | solution.py:494
  60.0 5.0 %collective-permute-start.7 = (f32[8,1536]{1,0:T(8,128)S(1)}, f32[8,1536]{1,0:T(8,128)S(1)}, u32[]{:S(2)}, u32[]{:S(2)}) collective-permute-start(f32[8,1536]{1,0:T(8,128)S(1)} %get-tuple-element.284), channel_id=1, source_target_pairs={{256,192},{257,193},{258,194},{259,195},{260,196},{261,197},{262,1... | collective-permute-start | bytes 147464 | tf_op jit(solution)/shard_map/ppermute | solution.py:389
  66.8 12.7 %collective-permute-start.14 = (bf16[64,1536]{1,0:T(8,128)(2,1)S(1)}, bf16[64,1536]{1,0:T(8,128)(2,1)S(1)}, u32[]{:S(2)}, u32[]{:S(2)}) collective-permute-start(bf16[64,1536]{1,0:T(8,128)(2,1)S(1)} %get-tuple-element.302), channel_id=1, source_target_pairs={{64,0},{128,64},{192,128},{256,192},{320,256},{384,320},{448,384},... | collective-permute-start | bytes 589832 | tf_op jit(solution)/shard_map/ppermute | solution.py:494
  76.5 11.0 %collective-permute-start.15 = (bf16[64,1536]{1,0:T(8,128)(2,1)S(1)}, bf16[64,1536]{1,0:T(8,128)(2,1)S(1)}, u32[]{:S(2)}, u32[]{:S(2)}) collective-permute-start(bf16[64,1536]{1,0:T(8,128)(2,1)S(1)} %get-tuple-element.310), channel_id=1, source_target_pairs={{64,0},{128,64},{192,128},{256,192},{320,256},{384,320},{448,384},... | collective-permute-start | bytes 589832 | tf_op jit(solution)/shard_map/ppermute | solution.py:494
  80.7 11.0 %collective-permute-start.16 = (bf16[64,1536]{1,0:T(8,128)(2,1)S(1)}, bf16[64,1536]{1,0:T(8,128)(2,1)S(1)}, u32[]{:S(2)}, u32[]{:S(2)}) collective-permute-start(bf16[64,1536]{1,0:T(8,128)(2,1)S(1)} %get-tuple-element.318), channel_id=1, source_target_pairs={{64,0},{128,64},{192,128},{256,192},{320,256},{384,320},{448,384},... | collective-permute-start | bytes 589832 | tf_op jit(solution)/shard_map/ppermute | solution.py:494
  88.8 10.9 %collective-permute-start.17 = (bf16[64,1536]{1,0:T(8,128)(2,1)S(1)}, bf16[64,1536]{1,0:T(8,128)(2,1)S(1)}, u32[]{:S(2)}, u32[]{:S(2)}) collective-permute-start(bf16[64,1536]{1,0:T(8,128)(2,1)S(1)} %get-tuple-element.326), channel_id=1, source_target_pairs={{64,0},{128,64},{192,128},{256,192},{320,256},{384,320},{448,384},... | collective-permute-start | bytes 589832 | tf_op jit(solution)/shard_map/ppermute | solution.py:494
  92.9 10.8 %collective-permute-start.18 = (bf16[64,1536]{1,0:T(8,128)(2,1)S(1)}, bf16[64,1536]{1,0:T(8,128)(2,1)S(1)}, u32[]{:S(2)}, u32[]{:S(2)}) collective-permute-start(bf16[64,1536]{1,0:T(8,128)(2,1)S(1)} %get-tuple-element.334), channel_id=1, source_target_pairs={{64,0},{128,64},{192,128},{256,192},{320,256},{384,320},{448,384},... | collective-permute-start | bytes 589832 | tf_op jit(solution)/shard_map/ppermute | solution.py:494
  101.0 10.9 %collective-permute-start.19 = (bf16[64,1536]{1,0:T(8,128)(2,1)S(1)}, bf16[64,1536]{1,0:T(8,128)(2,1)S(1)}, u32[]{:S(2)}, u32[]{:S(2)}) collective-permute-start(bf16[64,1536]{1,0:T(8,128)(2,1)S(1)} %get-tuple-element.342), channel_id=1, source_target_pairs={{64,0},{128,64},{192,128},{256,192},{320,256},{384,320},{448,384},... | collective-permute-start | bytes 589832 | tf_op jit(solution)/shard_map/ppermute | solution.py:494
  104.3 12.7 %collective-permute-start.20 = (bf16[64,1536]{1,0:T(8,128)(2,1)S(1)}, bf16[64,1536]{1,0:T(8,128)(2,1)S(1)}, u32[]{:S(2)}, u32[]{:S(2)}) collective-permute-start(bf16[64,1536]{1,0:T(8,128)(2,1)S(1)} %get-tuple-element.350), channel_id=1, source_target_pairs={{64,0},{128,64},{192,128},{256,192},{320,256},{384,320},{448,384},... | collective-permute-start | bytes 589832 | tf_op jit(solution)/shard_map/ppermute | solution.py:494
  112.5 11.5 %collective-permute-start.21 = (bf16[64,1536]{1,0:T(8,128)(2,1)S(1)}, bf16[64,1536]{1,0:T(8,128)(2,1)S(1)}, u32[]{:S(2)}, u32[]{:S(2)}) collective-permute-start(bf16[64,1536]{1,0:T(8,128)(2,1)S(1)} %get-tuple-element.358), channel_id=1, source_target_pairs={{64,0},{128,64},{192,128},{256,192},{320,256},{384,320},{448,384},... | collective-permute-start | bytes 589832 | tf_op jit(solution)/shard_map/ppermute | solution.py:494
  117.8 11.4 %collective-permute-start.22 = (bf16[64,1536]{1,0:T(8,128)(2,1)S(1)}, bf16[64,1536]{1,0:T(8,128)(2,1)S(1)}, u32[]{:S(2)}, u32[]{:S(2)}) collective-permute-start(bf16[64,1536]{1,0:T(8,128)(2,1)S(1)} %get-tuple-element.366), channel_id=1, source_target_pairs={{64,0},{128,64},{192,128},{256,192},{320,256},{384,320},{448,384},... | collective-permute-start | bytes 589832 | tf_op jit(solution)/shard_map/ppermute | solution.py:494
  124.5 12.1 %collective-permute-start.23 = (bf16[64,1536]{1,0:T(8,128)(2,1)S(1)}, bf16[64,1536]{1,0:T(8,128)(2,1)S(1)}, u32[]{:S(2)}, u32[]{:S(2)}) collective-permute-start(bf16[64,1536]{1,0:T(8,128)(2,1)S(1)} %get-tuple-element.374), channel_id=1, source_target_pairs={{64,0},{128,64},{192,128},{256,192},{320,256},{384,320},{448,384},... | collective-permute-start | bytes 589832 | tf_op jit(solution)/shard_map/ppermute | solution.py:494
  129.8 10.5 %collective-permute-start.24 = (bf16[64,1536]{1,0:T(8,128)(2,1)S(1)}, bf16[64,1536]{1,0:T(8,128)(2,1)S(1)}, u32[]{:S(2)}, u32[]{:S(2)}) collective-permute-start(bf16[64,1536]{1,0:T(8,128)(2,1)S(1)} %get-tuple-element.382), channel_id=1, source_target_pairs={{64,0},{128,64},{192,128},{256,192},{320,256},{384,320},{448,384},... | collective-permute-start | bytes 589832 | tf_op jit(solution)/shard_map/ppermute | solution.py:494
  137.1 9.1 %collective-permute-start.25 = (bf16[64,1536]{1,0:T(8,128)(2,1)S(1)}, bf16[64,1536]{1,0:T(8,128)(2,1)S(1)}, u32[]{:S(2)}, u32[]{:S(2)}) collective-permute-start(bf16[64,1536]{1,0:T(8,128)(2,1)S(1)} %get-tuple-element.390), channel_id=1, source_target_pairs={{64,0},{128,64},{192,128},{256,192},{320,256},{384,320},{448,384},... | collective-permute-start | bytes 589832 | tf_op jit(solution)/shard_map/ppermute | solution.py:494
  148.8 4.3 %collective-permute-start.27 = (bf16[16,48,256]{2,1,0:T(8,128)(2,1)S(1)}, bf16[16,48,256]{2,1,0:T(8,128)(2,1)S(1)}, u32[]{:S(2)}, u32[]{:S(2)}) collective-permute-start(bf16[16,48,256]{2,1,0:T(8,128)(2,1)S(1)} %get-tuple-element.399), channel_id=1, source_target_pairs={{0,1},{1,0},{2,3},{3,2},{4,5},{5,4},{6,7},{7,6},{8,9},{9,8},{10,11... | collective-permute-start | bytes 1179656 | tf_op jit(solution)/shard_map/ppermute | solution.py:310
  150.7 6.1 %collective-permute-start.26 = (bf16[16,48,256]{2,1,0:T(8,128)(2,1)S(1)}, bf16[16,48,256]{2,1,0:T(8,128)(2,1)S(1)}, u32[]{:S(2)}, u32[]{:S(2)}) collective-permute-start(bf16[16,48,256]{2,1,0:T(8,128)(2,1)S(1)} %get-tuple-element.397), channel_id=1, source_target_pairs={{0,1},{1,0},{2,3},{3,2},{4,5},{5,4},{6,7},{7,6},{8,9},{9,8},{10,11... | collective-permute-start | bytes 1179656 | tf_op jit(solution)/shard_map/ppermute | solution.py:310
  153.3 12.9 %collective-permute-start.28 = (bf16[16,48,256]{2,1,0:T(8,128)(2,1)S(1)}, bf16[16,48,256]{2,1,0:T(8,128)(2,1)S(1)}, u32[]{:S(2)}, u32[]{:S(2)}) collective-permute-start(bf16[16,48,256]{2,1,0:T(8,128)(2,1)S(1)} %shard_map.157), channel_id=1, source_target_pairs={{0,32},{32,0},{1,33},{33,1},{2,34},{34,2},{3,35},{35,3},{4,36},{36... | collective-permute-start | bytes 1179656 | tf_op jit(solution)/shard_map/ppermute | solution.py:310
  167.0 84.2 %all-to-all-start = ((bf16[16,48,256]{2,1,0:T(8,128)(2,1)}), bf16[16,48,256]{2,1,0:T(8,128)(2,1)S(1)}, u32[]{:S(2)}, u32[]{:S(2)}) async-start(bf16[16,48,256]{2,1,0:T(8,128)(2,1)} %shard_map.158), calls=%async_computation | async-start | bytes 786432 | tf_op jit(solution)/shard_map/all_to_all | solution.py:524
  183.2 0.7 collective-permute-start.29
  183.9 0.7 collective-permute-start.30
  184.6 15.5 %collective-permute-start.31 = (bf16[32,1536]{1,0:T(8,128)(2,1)S(1)}, bf16[32,1536]{1,0:T(8,128)(2,1)S(1)}, u32[]{:S(2)}, u32[]{:S(2)}) collective-permute-start(bf16[32,1536]{1,0:T(8,128)(2,1)S(1)} %shard_map.160.held_ref), channel_id=1, source_target_pairs={{64,0},{192,128},{320,256},{448,384},{65,1},{193,129},{321,257},{4... | collective-permute-start | bytes 294920 | tf_op jit(solution)/shard_map/ppermute | solution.py:432
  201.4 3.4 %collective-permute-start.32 = (bf16[2,16,16,256]{3,2,1,0:T(8,128)(2,1)S(1)}, bf16[2,16,16,256]{3,2,1,0:T(8,128)(2,1)S(1)}, u32[]{:S(2)}, u32[]{:S(2)}) collective-permute-start(bf16[2,16,16,256]{3,2,1,0:T(8,128)(2,1)S(1)} %get-tuple-element.409), channel_id=1, source_target_pairs={{0,1},{1,0},{2,3},{3,2},{4,5},{5,4},{6,7},{7,6},{8,9},{9,8},{10,11... | collective-permute-start | bytes 786440 | tf_op jit(solution)/shard_map/ppermute | solution.py:310
  204.9 7.4 %collective-permute-start.33 = (bf16[16,16,256]{2,1,0:T(8,128)(2,1)S(1)}, bf16[16,16,256]{2,1,0:T(8,128)(2,1)S(1)}, u32[]{:S(2)}, u32[]{:S(2)}) collective-permute-start(bf16[16,16,256]{2,1,0:T(8,128)(2,1)S(1)} %get-tuple-element.412), channel_id=1, source_target_pairs={{0,32},{32,0},{1,33},{33,1},{2,34},{34,2},{3,35},{35,3},{4,36},{36... | collective-permute-start | bytes 393224 | tf_op jit(solution)/shard_map/ppermute | solution.py:310
  212.4 6.3 %collective-permute-start.34 = (bf16[8,16,256]{2,1,0:T(8,128)(2,1)S(1)}, bf16[8,16,256]{2,1,0:T(8,128)(2,1)S(1)}, u32[]{:S(2)}, u32[]{:S(2)}) collective-permute-start(bf16[8,16,256]{2,1,0:T(8,128)(2,1)S(1)} %get-tuple-element.414), channel_id=1, source_target_pairs={{0,2},{2,0},{4,6},{6,4},{8,10},{10,8},{12,14},{14,12},{16,18},{18,... | collective-permute-start | bytes 196616 | tf_op jit(solution)/shard_map/ppermute | solution.py:462
  218.7 6.7 %collective-permute-start.35 = (bf16[4,16,256]{2,1,0:T(8,128)(2,1)S(1)}, bf16[4,16,256]{2,1,0:T(8,128)(2,1)S(1)}, u32[]{:S(2)}, u32[]{:S(2)}) collective-permute-start(bf16[4,16,256]{2,1,0:T(8,128)(2,1)S(1)} %get-tuple-element.416), channel_id=1, source_target_pairs={{0,4},{2,6},{4,0},{6,2},{8,12},{10,14},{12,8},{14,10},{16,20},{18,... | collective-permute-start | bytes 98312 | tf_op jit(solution)/shard_map/ppermute | solution.py:462
  225.4 9.5 %collective-permute-start.36 = (bf16[2,16,256]{2,1,0:T(8,128)(2,1)S(1)}, bf16[2,16,256]{2,1,0:T(8,128)(2,1)S(1)}, u32[]{:S(2)}, u32[]{:S(2)}) collective-permute-start(bf16[2,16,256]{2,1,0:T(8,128)(2,1)S(1)} %get-tuple-element.418), channel_id=1, source_target_pairs={{0,8},{2,10},{4,12},{6,14},{8,0},{10,2},{12,4},{14,6},{16,24},{18,... | collective-permute-start | bytes 49160 | tf_op jit(solution)/shard_map/ppermute | solution.py:462
  235.0 14.9 %collective-permute-start.37 = (bf16[1,16,256]{2,1,0:T(8,128)(2,1)S(1)}, bf16[1,16,256]{2,1,0:T(8,128)(2,1)S(1)}, u32[]{:S(2)}, u32[]{:S(2)}) collective-permute-start(bf16[1,16,256]{2,1,0:T(8,128)(2,1)S(1)} %get-tuple-element.420), channel_id=1, source_target_pairs={{0,16},{2,18},{4,20},{6,22},{8,24},{10,26},{12,28},{14,30},{16,0},... | collective-permute-start | bytes 24584 | tf_op jit(solution)/shard_map/ppermute | solution.py:462

commit v6 on v5

--- a/solution.py
+++ b/solution.py
@@ -217,7 +217,7 @@
     crit[...] += lax.dot_general(hid, gl, dims, preferred_element_type=F32)
 
     for i in range(n_z):
-        for dy, dc, dest in places(parts, yl_ref, core_ref, jnp.bitwise_xor(z_ref[0], mirrored(i, n_z))):
+        for dy, dc, dest in places(parts, yl_ref, core_ref, jnp.bitwise_xor(z_ref[0], i)):
             piece = crit[pl.ds(pl.multiple_of(dest * padded, 16), padded), :].astype(BF16)
             (sent_ref if dc else kept_ref)[dy, i] = piece
 
@@ -231,10 +231,6 @@
             c = core_ref[0] if dc == 0 else n_c - 1 - core_ref[0]
             found.append((dy, dc, (yl * n_z + z) * n_c + c))
     return found
-
-
-def mirrored(i, n):
-    return sum(((i >> b) & 1) * (n >> (b + 1)) for b in range(n.bit_length() - 1))
 
 
 def plus(left, right):
@@ -450,7 +446,7 @@
             if n_yl == 2:
                 held["other_sum"] = swap(other, "yl", n_yl)
         elif step == 18 and n_yl == 2:
-            fold(after(held["own_sum"], token), held["other_sum"], 1)
+            fold(after(held["own_sum"], token), held["other_sum"], n_z // 2)
 
     def fold(left, right, bit):
         size = left.shape[0]
@@ -515,10 +511,10 @@
     summed = halves[0]
     if n_yl == 2:
         arrived = swap(halves[1], "yl", n_yl)
-        bit = 2
-        while bit <= n_z:
+        bit = n_z // 2
+        while bit:
+            bit //= 2
             fold(held["own_sum"], held["other_sum"], bit)
-            bit *= 2
         summed = call(add_kernel, sds(arrived.shape, BF16), [VM, VM], (summed, arrived), 0, 2 << 20)
     if n_z > 1:
         summed = lax.all_to_all(summed, "z", 0, 0, tiled=True)

time: 254 us -> 256 us (level)
  waiting for transfers between devices: 55.1 us -> 60.6 us
  starting transfers between devices: 165 us -> 162 us
    ppermute x4, waiting for transfers between devices: 7.51 us -> 13 us  [fold(): lax.ppermute(high, 'z', [(i, i ^ bit) for i in range(n_z)])]
    ppermute x4, starting transfers between devices: 29.9 us -> 26.6 us  [fold(): lax.ppermute(high, 'z', [(i, i ^ bit) for i in range(n_z)])]
where the time goes in v6:
time: 256 us; the launch traced here: 255 us
  starting transfers between devices  162 us (63%)
  waiting for transfers between devices  60.6 us (24%)
  Pallas kernels  25.9 us (10%)
  local copies, waits for them, and re-layouts  3.8 us (1%)
    ppermute x20, starting transfers between devices, whole(): received[step] = lax.ppermute(outgoing, SEC, relay_route)  93 us
    ppermute x4, starting transfers between devices, fold(): lax.ppermute(high, 'z', [(i, i ^ bit) for i in range(n_z)])  26.6 us
    pallas_call x41, Pallas kernels, call(): pl.pallas_call(kernel, out_shape=out_shape, in_specs=in_specs, out_specs=...  25.9 us
    all_to_all x1, starting transfers between devices, whole(): summed = lax.all_to_all(summed, 'z', 0, 0, tiled=True)  16.1 us
    ppermute x20, waiting for transfers between devices, whole(): received[step] = lax.ppermute(outgoing, SEC, relay_route)  15.9 us
    ppermute x5, waiting for transfers between devices, swap(): return lax.ppermute(block, axis, [(i, size - 1 - i) for i in range(size)])  15.6 us
    ppermute x3, waiting for transfers between devices, side_work(): moved = lax.ppermute(lines, SEC, route)  14.2 us
    ppermute x4, waiting for transfers between devices, fold(): lax.ppermute(high, 'z', [(i, i ^ bit) for i in range(n_z)])  13 us
  transfers between devices with their start and end apart: 39, of which 18 were waited for; matrix products, arithmetic and copies ran while one was open for 1% of the time, Pallas kernels for 9%

profile of v6, /device:TPU:4, one launch (start us, length us, event | category | flops | bytes accessed | tf_op | source)
XLA Modules:
  0.0 254.8 jit_solution(17938776767321923152)
XLA Ops:
  0.7 1.5 copy.323
  2.2 1.0 copy-done.4
  3.2 5.1 %collective-permute-start.8 = (bf16[192,384]{1,0:T(8,128)(2,1)S(1)}, bf16[192,384]{1,0:T(8,128)(2,1)S(1)}, u32[]{:S(2)}, u32[]{:S(2)}) collective-permute-start(bf16[192,384]{1,0:T(8,128)(2,1)S(1)} %shard_map.137.refs_1_), channel_id=1, source_target_pairs={{0,64},{128,192},{256,320},{384,448},{1,65},{129,193},{257,321},{3... | collective-permute-start | bytes 442376 | tf_op jit(solution)/shard_map/ppermute | solution.py:343
  8.4 1.9 shard_map.128
  10.9 1.9 collective-permute-start
  13.4 5.4 %collective-permute-start.1 = (bf16[64,1536]{1,0:T(8,128)(2,1)S(1)}, bf16[64,1536]{1,0:T(8,128)(2,1)S(1)}, u32[]{:S(2)}, u32[]{:S(2)}) collective-permute-start(bf16[64,1536]{1,0:T(8,128)(2,1)S(1)} %get-tuple-element.240), channel_id=1, source_target_pairs={{64,0},{128,64},{192,128},{256,192},{320,256},{384,320},{448,384},... | collective-permute-start | bytes 589832 | tf_op jit(solution)/shard_map/ppermute | solution.py:490
  20.9 1.2 collective-permute-done.refs_9_
  22.6 2.6 %collective-permute-start.2 = (bf16[64,1536]{1,0:T(8,128)(2,1)S(1)}, bf16[64,1536]{1,0:T(8,128)(2,1)S(1)}, u32[]{:S(2)}, u32[]{:S(2)}) collective-permute-start(bf16[64,1536]{1,0:T(8,128)(2,1)S(1)} %get-tuple-element.248), channel_id=1, source_target_pairs={{64,0},{128,64},{192,128},{256,192},{320,256},{384,320},{448,384},... | collective-permute-start | bytes 589832 | tf_op jit(solution)/shard_map/ppermute | solution.py:490
  25.9 5.1 %collective-permute-start.3 = (bf16[64,1536]{1,0:T(8,128)(2,1)S(1)}, bf16[64,1536]{1,0:T(8,128)(2,1)S(1)}, u32[]{:S(2)}, u32[]{:S(2)}) collective-permute-start(bf16[64,1536]{1,0:T(8,128)(2,1)S(1)} %get-tuple-element.256), channel_id=1, source_target_pairs={{64,0},{128,64},{192,128},{256,192},{320,256},{384,320},{448,384},... | collective-permute-start | bytes 589832 | tf_op jit(solution)/shard_map/ppermute | solution.py:490
  31.0 1.6 collective-permute-done.2.refs_9_
  33.1 2.8 %collective-permute-done.3.refs_9_ = bf16[64,1536]{1,0:T(8,128)(2,1)S(1)} collective-permute-done((bf16[64,1536]{1,0:T(8,128)(2,1)S(1)}, bf16[64,1536]{1,0:T(8,128)(2,1)S(1)}, u32[]{:S(2)}, u32[]{:S(2)}) %collective-permute-start.3) | collective-permute-done | bytes 196640 | tf_op jit(solution)/shard_map/ppermute | solution.py:490
  37.3 6.3 %collective-permute-start.4 = (bf16[64,1536]{1,0:T(8,128)(2,1)S(1)}, bf16[64,1536]{1,0:T(8,128)(2,1)S(1)}, u32[]{:S(2)}, u32[]{:S(2)}) collective-permute-start(bf16[64,1536]{1,0:T(8,128)(2,1)S(1)} %get-tuple-element.264), channel_id=1, source_target_pairs={{64,0},{128,64},{192,128},{256,192},{320,256},{384,320},{448,384},... | collective-permute-start | bytes 589832 | tf_op jit(solution)/shard_map/ppermute | solution.py:490
  43.6 2.2 collective-permute-start.5
  45.8 3.1 %collective-permute-done.4.refs_9_ = bf16[64,1536]{1,0:T(8,128)(2,1)S(1)} collective-permute-done((bf16[64,1536]{1,0:T(8,128)(2,1)S(1)}, bf16[64,1536]{1,0:T(8,128)(2,1)S(1)}, u32[]{:S(2)}, u32[]{:S(2)}) %collective-permute-start.4) | collective-permute-done | bytes 196640 | tf_op jit(solution)/shard_map/ppermute | solution.py:490
  48.9 1.2 shard_map.135
  50.1 6.1 %collective-permute-start.6 = (bf16[64,1536]{1,0:T(8,128)(2,1)S(1)}, bf16[64,1536]{1,0:T(8,128)(2,1)S(1)}, u32[]{:S(2)}, u32[]{:S(2)}) collective-permute-start(bf16[64,1536]{1,0:T(8,128)(2,1)S(1)} %get-tuple-element.280), channel_id=1, source_target_pairs={{64,0},{128,64},{192,128},{256,192},{320,256},{384,320},{448,384},... | collective-permute-start | bytes 589832 | tf_op jit(solution)/shard_map/ppermute | solution.py:490
  56.3 1.3 shard_map.136
  57.5 2.4 collective-permute-start.13
  60.0 3.0 %collective-permute-start.7 = (f32[8,1536]{1,0:T(8,128)S(1)}, f32[8,1536]{1,0:T(8,128)S(1)}, u32[]{:S(2)}, u32[]{:S(2)}) collective-permute-start(f32[8,1536]{1,0:T(8,128)S(1)} %get-tuple-element.284), channel_id=1, source_target_pairs={{256,192},{257,193},{258,194},{259,195},{260,196},{261,197},{262,1... | collective-permute-start | bytes 147464 | tf_op jit(solution)/shard_map/ppermute | solution.py:385
  63.0 2.0 collective-permute-done.7.pooled_ref
  65.5 1.2 shard_map.141
  66.8 8.4 %collective-permute-start.14 = (bf16[64,1536]{1,0:T(8,128)(2,1)S(1)}, bf16[64,1536]{1,0:T(8,128)(2,1)S(1)}, u32[]{:S(2)}, u32[]{:S(2)}) collective-permute-start(bf16[64,1536]{1,0:T(8,128)(2,1)S(1)} %get-tuple-element.302), channel_id=1, source_target_pairs={{64,0},{128,64},{192,128},{256,192},{320,256},{384,320},{448,384},... | collective-permute-start | bytes 589832 | tf_op jit(solution)/shard_map/ppermute | solution.py:490
  75.3 1.2 shard_map.142
  76.5 2.0 collective-permute-start.15
  78.5 1.0 collective-permute-done.14.refs_8_
  79.5 1.2 shard_map.143
  80.7 6.8 %collective-permute-start.16 = (bf16[64,1536]{1,0:T(8,128)(2,1)S(1)}, bf16[64,1536]{1,0:T(8,128)(2,1)S(1)}, u32[]{:S(2)}, u32[]{:S(2)}) collective-permute-start(bf16[64,1536]{1,0:T(8,128)(2,1)S(1)} %get-tuple-element.318), channel_id=1, source_target_pairs={{64,0},{128,64},{192,128},{256,192},{320,256},{384,320},{448,384},... | collective-permute-start | bytes 589832 | tf_op jit(solution)/shard_map/ppermute | solution.py:490
  87.6 1.2 shard_map.144
  88.8 2.0 collective-permute-start.17
  90.8 0.9 collective-permute-done.16.refs_8_
  91.7 1.2 shard_map.145
  92.9 6.8 %collective-permute-start.18 = (bf16[64,1536]{1,0:T(8,128)(2,1)S(1)}, bf16[64,1536]{1,0:T(8,128)(2,1)S(1)}, u32[]{:S(2)}, u32[]{:S(2)}) collective-permute-start(bf16[64,1536]{1,0:T(8,128)(2,1)S(1)} %get-tuple-element.334), channel_id=1, source_target_pairs={{64,0},{128,64},{192,128},{256,192},{320,256},{384,320},{448,384},... | collective-permute-start | bytes 589832 | tf_op jit(solution)/shard_map/ppermute | solution.py:490
  99.8 1.2 shard_map.146
  101.0 2.6 %collective-permute-start.19 = (bf16[64,1536]{1,0:T(8,128)(2,1)S(1)}, bf16[64,1536]{1,0:T(8,128)(2,1)S(1)}, u32[]{:S(2)}, u32[]{:S(2)}) collective-permute-start(bf16[64,1536]{1,0:T(8,128)(2,1)S(1)} %get-tuple-element.342), channel_id=1, source_target_pairs={{64,0},{128,64},{192,128},{256,192},{320,256},{384,320},{448,384},... | collective-permute-start | bytes 589832 | tf_op jit(solution)/shard_map/ppermute | solution.py:490
  104.3 7.5 %collective-permute-start.20 = (bf16[64,1536]{1,0:T(8,128)(2,1)S(1)}, bf16[64,1536]{1,0:T(8,128)(2,1)S(1)}, u32[]{:S(2)}, u32[]{:S(2)}) collective-permute-start(bf16[64,1536]{1,0:T(8,128)(2,1)S(1)} %get-tuple-element.350), channel_id=1, source_target_pairs={{64,0},{128,64},{192,128},{256,192},{320,256},{384,320},{448,384},... | collective-permute-start | bytes 589832 | tf_op jit(solution)/shard_map/ppermute | solution.py:490
  112.5 4.5 %collective-permute-start.21 = (bf16[64,1536]{1,0:T(8,128)(2,1)S(1)}, bf16[64,1536]{1,0:T(8,128)(2,1)S(1)}, u32[]{:S(2)}, u32[]{:S(2)}) collective-permute-start(bf16[64,1536]{1,0:T(8,128)(2,1)S(1)} %get-tuple-element.358), channel_id=1, source_target_pairs={{64,0},{128,64},{192,128},{256,192},{320,256},{384,320},{448,384},... | collective-permute-start | bytes 589832 | tf_op jit(solution)/shard_map/ppermute | solution.py:490
  117.8 6.1 %collective-permute-start.22 = (bf16[64,1536]{1,0:T(8,128)(2,1)S(1)}, bf16[64,1536]{1,0:T(8,128)(2,1)S(1)}, u32[]{:S(2)}, u32[]{:S(2)}) collective-permute-start(bf16[64,1536]{1,0:T(8,128)(2,1)S(1)} %get-tuple-element.366), channel_id=1, source_target_pairs={{64,0},{128,64},{192,128},{256,192},{320,256},{384,320},{448,384},... | collective-permute-start | bytes 589832 | tf_op jit(solution)/shard_map/ppermute | solution.py:490
  124.5 4.2 %collective-permute-start.23 = (bf16[64,1536]{1,0:T(8,128)(2,1)S(1)}, bf16[64,1536]{1,0:T(8,128)(2,1)S(1)}, u32[]{:S(2)}, u32[]{:S(2)}) collective-permute-start(bf16[64,1536]{1,0:T(8,128)(2,1)S(1)} %get-tuple-element.374), channel_id=1, source_target_pairs={{64,0},{128,64},{192,128},{256,192},{320,256},{384,320},{448,384},... | collective-permute-start | bytes 589832 | tf_op jit(solution)/shard_map/ppermute | solution.py:490
  129.8 6.8 %collective-permute-start.24 = (bf16[64,1536]{1,0:T(8,128)(2,1)S(1)}, bf16[64,1536]{1,0:T(8,128)(2,1)S(1)}, u32[]{:S(2)}, u32[]{:S(2)}) collective-permute-start(bf16[64,1536]{1,0:T(8,128)(2,1)S(1)} %get-tuple-element.382), channel_id=1, source_target_pairs={{64,0},{128,64},{192,128},{256,192},{320,256},{384,320},{448,384},... | collective-permute-start | bytes 589832 | tf_op jit(solution)/shard_map/ppermute | solution.py:490
  137.1 3.1 %collective-permute-start.25 = (bf16[64,1536]{1,0:T(8,128)(2,1)S(1)}, bf16[64,1536]{1,0:T(8,128)(2,1)S(1)}, u32[]{:S(2)}, u32[]{:S(2)}) collective-permute-start(bf16[64,1536]{1,0:T(8,128)(2,1)S(1)} %get-tuple-element.390), channel_id=1, source_target_pairs={{64,0},{128,64},{192,128},{256,192},{320,256},{384,320},{448,384},... | collective-permute-start | bytes 589832 | tf_op jit(solution)/shard_map/ppermute | solution.py:490
  140.2 1.3 shard_map.153
  141.5 4.7 %collective-permute-done.25.refs_8_ = bf16[64,1536]{1,0:T(8,128)(2,1)S(1)} collective-permute-done((bf16[64,1536]{1,0:T(8,128)(2,1)S(1)}, bf16[64,1536]{1,0:T(8,128)(2,1)S(1)}, u32[]{:S(2)}, u32[]{:S(2)}) %collective-permute-start.25) | collective-permute-done | bytes 196640 | tf_op jit(solution)/shard_map/ppermute | solution.py:490
  146.2 1.2 shard_map.154
  147.5 1.3 shard_map.155
  148.8 1.9 collective-permute-start.27
  150.7 2.4 collective-permute-start.26
  153.3 3.5 %collective-permute-start.28 = (bf16[16,48,256]{2,1,0:T(8,128)(2,1)S(1)}, bf16[16,48,256]{2,1,0:T(8,128)(2,1)S(1)}, u32[]{:S(2)}, u32[]{:S(2)}) collective-permute-start(bf16[16,48,256]{2,1,0:T(8,128)(2,1)S(1)} %shard_map.157), channel_id=1, source_target_pairs={{0,32},{32,0},{1,33},{33,1},{2,34},{34,2},{3,35},{35,3},{4,36},{36... | collective-permute-start | bytes 1179656 | tf_op jit(solution)/shard_map/ppermute | solution.py:306
  156.9 9.3 %collective-permute-done.28.right_ref = bf16[16,48,256]{2,1,0:T(8,128)(2,1)S(1)} collective-permute-done((bf16[16,48,256]{2,1,0:T(8,128)(2,1)S(1)}, bf16[16,48,256]{2,1,0:T(8,128)(2,1)S(1)}, u32[]{:S(2)}, u32[]{:S(2)}) %collective-permute-start.28) | collective-permute-done | bytes 393248 | tf_op jit(solution)/shard_map/ppermute | solution.py:306
  167.0 16.1 %all-to-all-start = ((bf16[16,48,256]{2,1,0:T(8,128)(2,1)}), bf16[16,48,256]{2,1,0:T(8,128)(2,1)S(1)}, u32[]{:S(2)}, u32[]{:S(2)}) async-start(bf16[16,48,256]{2,1,0:T(8,128)(2,1)} %shard_map.158), calls=%async_computation | async-start | bytes 786432 | tf_op jit(solution)/shard_map/all_to_all | solution.py:520
  184.6 1.3 collective-permute-start.31
  185.9 14.2 %collective-permute-done.31.moved_ref = bf16[32,1536]{1,0:T(8,128)(2,1)S(1)} collective-permute-done((bf16[32,1536]{1,0:T(8,128)(2,1)S(1)}, bf16[32,1536]{1,0:T(8,128)(2,1)S(1)}, u32[]{:S(2)}, u32[]{:S(2)}) %collective-permute-start.31) | collective-permute-done | bytes 98336 | tf_op jit(solution)/shard_map/ppermute | solution.py:428
  200.0 1.4 shard_map.162
  201.4 1.9 collective-permute-start.32
  203.4 1.5 collective-permute-done.32.got_ref
  204.9 2.6 %collective-permute-start.33 = (bf16[16,16,256]{2,1,0:T(8,128)(2,1)S(1)}, bf16[16,16,256]{2,1,0:T(8,128)(2,1)S(1)}, u32[]{:S(2)}, u32[]{:S(2)}) collective-permute-start(bf16[16,16,256]{2,1,0:T(8,128)(2,1)S(1)} %get-tuple-element.412), channel_id=1, source_target_pairs={{0,32},{32,0},{1,33},{33,1},{2,34},{34,2},{3,35},{35,3},{4,36},{36... | collective-permute-start | bytes 393224 | tf_op jit(solution)/shard_map/ppermute | solution.py:306
  207.6 4.8 %collective-permute-done.33.right_ref = bf16[16,16,256]{2,1,0:T(8,128)(2,1)S(1)} collective-permute-done((bf16[16,16,256]{2,1,0:T(8,128)(2,1)S(1)}, bf16[16,16,256]{2,1,0:T(8,128)(2,1)S(1)}, u32[]{:S(2)}, u32[]{:S(2)}) %collective-permute-start.33) | collective-permute-done | bytes 131104 | tf_op jit(solution)/shard_map/ppermute | solution.py:306
  212.4 12.8 %collective-permute-start.34 = (bf16[8,16,256]{2,1,0:T(8,128)(2,1)S(1)}, bf16[8,16,256]{2,1,0:T(8,128)(2,1)S(1)}, u32[]{:S(2)}, u32[]{:S(2)}) collective-permute-start(bf16[8,16,256]{2,1,0:T(8,128)(2,1)S(1)} %get-tuple-element.414), channel_id=1, source_target_pairs={{0,16},{2,18},{4,20},{6,22},{8,24},{10,26},{12,28},{14,30},{16,0},... | collective-permute-start | bytes 196616 | tf_op jit(solution)/shard_map/ppermute | solution.py:458
  225.2 5.1 %collective-permute-done.34.right_ref = bf16[8,16,256]{2,1,0:T(8,128)(2,1)S(1)} collective-permute-done((bf16[8,16,256]{2,1,0:T(8,128)(2,1)S(1)}, bf16[8,16,256]{2,1,0:T(8,128)(2,1)S(1)}, u32[]{:S(2)}, u32[]{:S(2)}) %collective-permute-start.34) | collective-permute-done | bytes 65568 | tf_op jit(solution)/shard_map/ppermute | solution.py:458
  230.3 7.4 %collective-permute-start.35 = (bf16[4,16,256]{2,1,0:T(8,128)(2,1)S(1)}, bf16[4,16,256]{2,1,0:T(8,128)(2,1)S(1)}, u32[]{:S(2)}, u32[]{:S(2)}) collective-permute-start(bf16[4,16,256]{2,1,0:T(8,128)(2,1)S(1)} %get-tuple-element.416), channel_id=1, source_target_pairs={{0,8},{2,10},{4,12},{6,14},{8,0},{10,2},{12,4},{14,6},{16,24},{18,... | collective-permute-start | bytes 98312 | tf_op jit(solution)/shard_map/ppermute | solution.py:458
  237.8 2.3 collective-permute-done.35.right_ref
  240.0 4.4 %collective-permute-start.36 = (bf16[2,16,256]{2,1,0:T(8,128)(2,1)S(1)}, bf16[2,16,256]{2,1,0:T(8,128)(2,1)S(1)}, u32[]{:S(2)}, u32[]{:S(2)}) collective-permute-start(bf16[2,16,256]{2,1,0:T(8,128)(2,1)S(1)} %get-tuple-element.418), channel_id=1, source_target_pairs={{0,4},{2,6},{4,0},{6,2},{8,12},{10,14},{12,8},{14,10},{16,20},{18,... | collective-permute-start | bytes 49160 | tf_op jit(solution)/shard_map/ppermute | solution.py:458
  244.5 2.1 collective-permute-done.36.right_ref
  246.6 1.9 collective-permute-start.37
  248.5 3.6 %collective-permute-done.37.right_ref = bf16[1,16,256]{2,1,0:T(8,128)(2,1)S(1)} collective-permute-done((bf16[1,16,256]{2,1,0:T(8,128)(2,1)S(1)}, bf16[1,16,256]{2,1,0:T(8,128)(2,1)S(1)}, u32[]{:S(2)}, u32[]{:S(2)}) %collective-permute-start.37) | collective-permute-done | bytes 8224 | tf_op jit(solution)/shard_map/ppermute | solution.py:458
  (78 shorter events, 16.3 us)
Async XLA Ops:
  0.6 7.7 %copy-start.5 = (s32[4,1]{0,1:T(1,128)S(1)}, s32[4,1]{0,1:T(1,128)}, u32[]{:S(2)}) copy-start(s32[4,1]{0,1:T(1,128)} %param.11) | copy-start | bytes 52
  0.6 7.7 %copy-start.1 = (f32[1,1536]{1,0:T(1,128)S(1)}, f32[1,1536]{1,0:T(1,128)}, u32[]{:S(2)}) copy-start(f32[1,1536]{1,0:T(1,128)} %refs_5_.43) | copy-start | bytes 18436
  0.7 7.7 %copy-start.2 = (bf16[1,1536,256]{2,1,0:T(8,128)(2,1)S(1)}, bf16[1,1536,256]{2,1,0:T(8,128)(2,1)}, u32[]{:S(2)}) copy-start(bf16[1,1536,256]{2,1,0:T(8,128)(2,1)} %param.14) | copy-start | bytes 2359300
  0.7 7.7 %copy-start.3 = (bf16[1,256,1536]{2,1,0:T(8,128)(2,1)S(1)}, bf16[1,256,1536]{2,1,0:T(8,128)(2,1)}, u32[]{:S(2)}) copy-start(bf16[1,256,1536]{2,1,0:T(8,128)(2,1)} %param.15) | copy-start | bytes 2359300
  2.2 1.0 copy-start.4
  3.2 15.6 %collective-permute-start.8 = (bf16[192,384]{1,0:T(8,128)(2,1)S(1)}, bf16[192,384]{1,0:T(8,128)(2,1)S(1)}, u32[]{:S(2)}, u32[]{:S(2)}) collective-permute-start(bf16[192,384]{1,0:T(8,128)(2,1)S(1)} %shard_map.137.refs_1_), channel_id=1, source_target_pairs={{0,64},{128,192},{256,320},{384,448},{1,65},{129,193},{257,321},{3... | collective-permute-start | bytes 442376 | tf_op jit(solution)/shard_map/ppermute | solution.py:343
  8.4 2.0 copy-start
  10.9 11.2 %collective-permute-start = (bf16[64,1536]{1,0:T(8,128)(2,1)S(1)}, bf16[64,1536]{1,0:T(8,128)(2,1)S(1)}, u32[]{:S(2)}, u32[]{:S(2)}) collective-permute-start(bf16[64,1536]{1,0:T(8,128)(2,1)S(1)} %get-tuple-element.232), channel_id=1, source_target_pairs={{64,0},{128,64},{192,128},{256,192},{320,256},{384,320},{448,384},... | collective-permute-start | bytes 589832 | tf_op jit(solution)/shard_map/ppermute | solution.py:490
  13.4 11.9 %collective-permute-start.1 = (bf16[64,1536]{1,0:T(8,128)(2,1)S(1)}, bf16[64,1536]{1,0:T(8,128)(2,1)S(1)}, u32[]{:S(2)}, u32[]{:S(2)}) collective-permute-start(bf16[64,1536]{1,0:T(8,128)(2,1)S(1)} %get-tuple-element.240), channel_id=1, source_target_pairs={{64,0},{128,64},{192,128},{256,192},{320,256},{384,320},{448,384},... | collective-permute-start | bytes 589832 | tf_op jit(solution)/shard_map/ppermute | solution.py:490
  18.8 17.7 %collective-permute-start.11 = (bf16[384,384]{1,0:T(8,128)(2,1)S(1)}, bf16[384,384]{1,0:T(8,128)(2,1)S(1)}, u32[]{:S(2)}, u32[]{:S(2)}) collective-permute-start(bf16[384,384]{1,0:T(8,128)(2,1)S(1)} %shard_map.138.refs_1_), channel_id=1, source_target_pairs={{448,192},{449,193},{450,194},{451,195},{452,196},{453,197},{454,1... | collective-permute-start | bytes 884744 | tf_op jit(solution)/shard_map/ppermute | solution.py:383
  19.5 17.0 %collective-permute-start.10 = (bf16[384,384]{1,0:T(8,128)(2,1)S(1)}, bf16[384,384]{1,0:T(8,128)(2,1)S(1)}, u32[]{:S(2)}, u32[]{:S(2)}) collective-permute-start(bf16[384,384]{1,0:T(8,128)(2,1)S(1)} %shard_map.138.refs_1_), channel_id=1, source_target_pairs={{320,192},{321,193},{322,194},{323,195},{324,196},{325,197},{326,1... | collective-permute-start | bytes 884744 | tf_op jit(solution)/shard_map/ppermute | solution.py:383
  20.2 16.3 %collective-permute-start.9 = (bf16[384,384]{1,0:T(8,128)(2,1)S(1)}, bf16[384,384]{1,0:T(8,128)(2,1)S(1)}, u32[]{:S(2)}, u32[]{:S(2)}) collective-permute-start(bf16[384,384]{1,0:T(8,128)(2,1)S(1)} %shard_map.138.refs_1_), channel_id=1, source_target_pairs={{64,192},{65,193},{66,194},{67,195},{68,196},{69,197},{70,198},{71... | collective-permute-start | bytes 884744 | tf_op jit(solution)/shard_map/ppermute | solution.py:383
  22.6 9.9 %collective-permute-start.2 = (bf16[64,1536]{1,0:T(8,128)(2,1)S(1)}, bf16[64,1536]{1,0:T(8,128)(2,1)S(1)}, u32[]{:S(2)}, u32[]{:S(2)}) collective-permute-start(bf16[64,1536]{1,0:T(8,128)(2,1)S(1)} %get-tuple-element.248), channel_id=1, source_target_pairs={{64,0},{128,64},{192,128},{256,192},{320,256},{384,320},{448,384},... | collective-permute-start | bytes 589832 | tf_op jit(solution)/shard_map/ppermute | solution.py:490
  25.9 10.0 %collective-permute-start.3 = (bf16[64,1536]{1,0:T(8,128)(2,1)S(1)}, bf16[64,1536]{1,0:T(8,128)(2,1)S(1)}, u32[]{:S(2)}, u32[]{:S(2)}) collective-permute-start(bf16[64,1536]{1,0:T(8,128)(2,1)S(1)} %get-tuple-element.256), channel_id=1, source_target_pairs={{64,0},{128,64},{192,128},{256,192},{320,256},{384,320},{448,384},... | collective-permute-start | bytes 589832 | tf_op jit(solution)/shard_map/ppermute | solution.py:490
  36.5 28.4 %collective-permute-start.12 = (bf16[1536,384]{1,0:T(8,128)(2,1)S(1)}, bf16[1536,384]{1,0:T(8,128)(2,1)S(1)}, u32[]{:S(2)}, u32[]{:S(2)}) collective-permute-start(bf16[1536,384]{1,0:T(8,128)(2,1)S(1)} %shard_map.139.own_ref), channel_id=1, source_target_pairs={{192,193},{193,192},{194,195},{195,194},{196,197},{197,196},{198,1... | collective-permute-start | bytes 3538952 | tf_op jit(solution)/shard_map/ppermute | solution.py:390
  37.3 11.6 %collective-permute-start.4 = (bf16[64,1536]{1,0:T(8,128)(2,1)S(1)}, bf16[64,1536]{1,0:T(8,128)(2,1)S(1)}, u32[]{:S(2)}, u32[]{:S(2)}) collective-permute-start(bf16[64,1536]{1,0:T(8,128)(2,1)S(1)} %get-tuple-element.264), channel_id=1, source_target_pairs={{64,0},{128,64},{192,128},{256,192},{320,256},{384,320},{448,384},... | collective-permute-start | bytes 589832 | tf_op jit(solution)/shard_map/ppermute | solution.py:490
  43.6 12.7 %collective-permute-start.5 = (bf16[64,1536]{1,0:T(8,128)(2,1)S(1)}, bf16[64,1536]{1,0:T(8,128)(2,1)S(1)}, u32[]{:S(2)}, u32[]{:S(2)}) collective-permute-start(bf16[64,1536]{1,0:T(8,128)(2,1)S(1)} %get-tuple-element.272), channel_id=1, source_target_pairs={{64,0},{128,64},{192,128},{256,192},{320,256},{384,320},{448,384},... | collective-permute-start | bytes 589832 | tf_op jit(solution)/shard_map/ppermute | solution.py:490
  50.1 15.4 %collective-permute-start.6 = (bf16[64,1536]{1,0:T(8,128)(2,1)S(1)}, bf16[64,1536]{1,0:T(8,128)(2,1)S(1)}, u32[]{:S(2)}, u32[]{:S(2)}) collective-permute-start(bf16[64,1536]{1,0:T(8,128)(2,1)S(1)} %get-tuple-element.280), channel_id=1, source_target_pairs={{64,0},{128,64},{192,128},{256,192},{320,256},{384,320},{448,384},... | collective-permute-start | bytes 589832 | tf_op jit(solution)/shard_map/ppermute | solution.py:490
  56.2 8.7 %copy-start.6 = (bf16[768,29]{0,1:T(8,128)(2,1)S(1)}, bf16[768,29]{0,1:T(8,128)(2,1)}, u32[]{:S(2)}) copy-start(bf16[768,29]{0,1:T(8,128)(2,1)} %param.17) | copy-start | bytes 133636
  56.3 8.7 %copy-start.7 = (s32[4,1]{0,1:T(1,128)S(1)}, s32[4,1]{0,1:T(1,128)}, u32[]{:S(2)}) copy-start(s32[4,1]{0,1:T(1,128)} %param.12) | copy-start | bytes 52
  57.5 17.7 %collective-permute-start.13 = (bf16[64,1536]{1,0:T(8,128)(2,1)S(1)}, bf16[64,1536]{1,0:T(8,128)(2,1)S(1)}, u32[]{:S(2)}, u32[]{:S(2)}) collective-permute-start(bf16[64,1536]{1,0:T(8,128)(2,1)S(1)} %get-tuple-element.281), channel_id=1, source_target_pairs={{64,0},{128,64},{192,128},{256,192},{320,256},{384,320},{448,384},... | collective-permute-start | bytes 589832 | tf_op jit(solution)/shard_map/ppermute | solution.py:490
  60.0 5.0 %collective-permute-start.7 = (f32[8,1536]{1,0:T(8,128)S(1)}, f32[8,1536]{1,0:T(8,128)S(1)}, u32[]{:S(2)}, u32[]{:S(2)}) collective-permute-start(f32[8,1536]{1,0:T(8,128)S(1)} %get-tuple-element.284), channel_id=1, source_target_pairs={{256,192},{257,193},{258,194},{259,195},{260,196},{261,197},{262,1... | collective-permute-start | bytes 147464 | tf_op jit(solution)/shard_map/ppermute | solution.py:385
  66.8 12.7 %collective-permute-start.14 = (bf16[64,1536]{1,0:T(8,128)(2,1)S(1)}, bf16[64,1536]{1,0:T(8,128)(2,1)S(1)}, u32[]{:S(2)}, u32[]{:S(2)}) collective-permute-start(bf16[64,1536]{1,0:T(8,128)(2,1)S(1)} %get-tuple-element.302), channel_id=1, source_target_pairs={{64,0},{128,64},{192,128},{256,192},{320,256},{384,320},{448,384},... | collective-permute-start | bytes 589832 | tf_op jit(solution)/shard_map/ppermute | solution.py:490
  76.5 11.0 %collective-permute-start.15 = (bf16[64,1536]{1,0:T(8,128)(2,1)S(1)}, bf16[64,1536]{1,0:T(8,128)(2,1)S(1)}, u32[]{:S(2)}, u32[]{:S(2)}) collective-permute-start(bf16[64,1536]{1,0:T(8,128)(2,1)S(1)} %get-tuple-element.310), channel_id=1, source_target_pairs={{64,0},{128,64},{192,128},{256,192},{320,256},{384,320},{448,384},... | collective-permute-start | bytes 589832 | tf_op jit(solution)/shard_map/ppermute | solution.py:490
  80.7 11.0 %collective-permute-start.16 = (bf16[64,1536]{1,0:T(8,128)(2,1)S(1)}, bf16[64,1536]{1,0:T(8,128)(2,1)S(1)}, u32[]{:S(2)}, u32[]{:S(2)}) collective-permute-start(bf16[64,1536]{1,0:T(8,128)(2,1)S(1)} %get-tuple-element.318), channel_id=1, source_target_pairs={{64,0},{128,64},{192,128},{256,192},{320,256},{384,320},{448,384},... | collective-permute-start | bytes 589832 | tf_op jit(solution)/shard_map/ppermute | solution.py:490
  88.8 10.9 %collective-permute-start.17 = (bf16[64,1536]{1,0:T(8,128)(2,1)S(1)}, bf16[64,1536]{1,0:T(8,128)(2,1)S(1)}, u32[]{:S(2)}, u32[]{:S(2)}) collective-permute-start(bf16[64,1536]{1,0:T(8,128)(2,1)S(1)} %get-tuple-element.326), channel_id=1, source_target_pairs={{64,0},{128,64},{192,128},{256,192},{320,256},{384,320},{448,384},... | collective-permute-start | bytes 589832 | tf_op jit(solution)/shard_map/ppermute | solution.py:490
  92.9 10.8 %collective-permute-start.18 = (bf16[64,1536]{1,0:T(8,128)(2,1)S(1)}, bf16[64,1536]{1,0:T(8,128)(2,1)S(1)}, u32[]{:S(2)}, u32[]{:S(2)}) collective-permute-start(bf16[64,1536]{1,0:T(8,128)(2,1)S(1)} %get-tuple-element.334), channel_id=1, source_target_pairs={{64,0},{128,64},{192,128},{256,192},{320,256},{384,320},{448,384},... | collective-permute-start | bytes 589832 | tf_op jit(solution)/shard_map/ppermute | solution.py:490
  101.0 10.9 %collective-permute-start.19 = (bf16[64,1536]{1,0:T(8,128)(2,1)S(1)}, bf16[64,1536]{1,0:T(8,128)(2,1)S(1)}, u32[]{:S(2)}, u32[]{:S(2)}) collective-permute-start(bf16[64,1536]{1,0:T(8,128)(2,1)S(1)} %get-tuple-element.342), channel_id=1, source_target_pairs={{64,0},{128,64},{192,128},{256,192},{320,256},{384,320},{448,384},... | collective-permute-start | bytes 589832 | tf_op jit(solution)/shard_map/ppermute | solution.py:490
  104.3 12.7 %collective-permute-start.20 = (bf16[64,1536]{1,0:T(8,128)(2,1)S(1)}, bf16[64,1536]{1,0:T(8,128)(2,1)S(1)}, u32[]{:S(2)}, u32[]{:S(2)}) collective-permute-start(bf16[64,1536]{1,0:T(8,128)(2,1)S(1)} %get-tuple-element.350), channel_id=1, source_target_pairs={{64,0},{128,64},{192,128},{256,192},{320,256},{384,320},{448,384},... | collective-permute-start | bytes 589832 | tf_op jit(solution)/shard_map/ppermute | solution.py:490
  112.5 11.5 %collective-permute-start.21 = (bf16[64,1536]{1,0:T(8,128)(2,1)S(1)}, bf16[64,1536]{1,0:T(8,128)(2,1)S(1)}, u32[]{:S(2)}, u32[]{:S(2)}) collective-permute-start(bf16[64,1536]{1,0:T(8,128)(2,1)S(1)} %get-tuple-element.358), channel_id=1, source_target_pairs={{64,0},{128,64},{192,128},{256,192},{320,256},{384,320},{448,384},... | collective-permute-start | bytes 589832 | tf_op jit(solution)/shard_map/ppermute | solution.py:490
  117.8 11.4 %collective-permute-start.22 = (bf16[64,1536]{1,0:T(8,128)(2,1)S(1)}, bf16[64,1536]{1,0:T(8,128)(2,1)S(1)}, u32[]{:S(2)}, u32[]{:S(2)}) collective-permute-start(bf16[64,1536]{1,0:T(8,128)(2,1)S(1)} %get-tuple-element.366), channel_id=1, source_target_pairs={{64,0},{128,64},{192,128},{256,192},{320,256},{384,320},{448,384},... | collective-permute-start | bytes 589832 | tf_op jit(solution)/shard_map/ppermute | solution.py:490
  124.5 12.1 %collective-permute-start.23 = (bf16[64,1536]{1,0:T(8,128)(2,1)S(1)}, bf16[64,1536]{1,0:T(8,128)(2,1)S(1)}, u32[]{:S(2)}, u32[]{:S(2)}) collective-permute-start(bf16[64,1536]{1,0:T(8,128)(2,1)S(1)} %get-tuple-element.374), channel_id=1, source_target_pairs={{64,0},{128,64},{192,128},{256,192},{320,256},{384,320},{448,384},... | collective-permute-start | bytes 589832 | tf_op jit(solution)/shard_map/ppermute | solution.py:490
  129.8 10.5 %collective-permute-start.24 = (bf16[64,1536]{1,0:T(8,128)(2,1)S(1)}, bf16[64,1536]{1,0:T(8,128)(2,1)S(1)}, u32[]{:S(2)}, u32[]{:S(2)}) collective-permute-start(bf16[64,1536]{1,0:T(8,128)(2,1)S(1)} %get-tuple-element.382), channel_id=1, source_target_pairs={{64,0},{128,64},{192,128},{256,192},{320,256},{384,320},{448,384},... | collective-permute-start | bytes 589832 | tf_op jit(solution)/shard_map/ppermute | solution.py:490
  137.1 9.1 %collective-permute-start.25 = (bf16[64,1536]{1,0:T(8,128)(2,1)S(1)}, bf16[64,1536]{1,0:T(8,128)(2,1)S(1)}, u32[]{:S(2)}, u32[]{:S(2)}) collective-permute-start(bf16[64,1536]{1,0:T(8,128)(2,1)S(1)} %get-tuple-element.390), channel_id=1, source_target_pairs={{64,0},{128,64},{192,128},{256,192},{320,256},{384,320},{448,384},... | collective-permute-start | bytes 589832 | tf_op jit(solution)/shard_map/ppermute | solution.py:490
  148.8 4.3 %collective-permute-start.27 = (bf16[16,48,256]{2,1,0:T(8,128)(2,1)S(1)}, bf16[16,48,256]{2,1,0:T(8,128)(2,1)S(1)}, u32[]{:S(2)}, u32[]{:S(2)}) collective-permute-start(bf16[16,48,256]{2,1,0:T(8,128)(2,1)S(1)} %get-tuple-element.399), channel_id=1, source_target_pairs={{0,1},{1,0},{2,3},{3,2},{4,5},{5,4},{6,7},{7,6},{8,9},{9,8},{10,11... | collective-permute-start | bytes 1179656 | tf_op jit(solution)/shard_map/ppermute | solution.py:306
  150.7 6.1 %collective-permute-start.26 = (bf16[16,48,256]{2,1,0:T(8,128)(2,1)S(1)}, bf16[16,48,256]{2,1,0:T(8,128)(2,1)S(1)}, u32[]{:S(2)}, u32[]{:S(2)}) collective-permute-start(bf16[16,48,256]{2,1,0:T(8,128)(2,1)S(1)} %get-tuple-element.397), channel_id=1, source_target_pairs={{0,1},{1,0},{2,3},{3,2},{4,5},{5,4},{6,7},{7,6},{8,9},{9,8},{10,11... | collective-permute-start | bytes 1179656 | tf_op jit(solution)/shard_map/ppermute | solution.py:306
  153.3 12.9 %collective-permute-start.28 = (bf16[16,48,256]{2,1,0:T(8,128)(2,1)S(1)}, bf16[16,48,256]{2,1,0:T(8,128)(2,1)S(1)}, u32[]{:S(2)}, u32[]{:S(2)}) collective-permute-start(bf16[16,48,256]{2,1,0:T(8,128)(2,1)S(1)} %shard_map.157), channel_id=1, source_target_pairs={{0,32},{32,0},{1,33},{33,1},{2,34},{34,2},{3,35},{35,3},{4,36},{36... | collective-permute-start | bytes 1179656 | tf_op jit(solution)/shard_map/ppermute | solution.py:306
  167.0 86.4 %all-to-all-start = ((bf16[16,48,256]{2,1,0:T(8,128)(2,1)}), bf16[16,48,256]{2,1,0:T(8,128)(2,1)S(1)}, u32[]{:S(2)}, u32[]{:S(2)}) async-start(bf16[16,48,256]{2,1,0:T(8,128)(2,1)} %shard_map.158), calls=%async_computation | async-start | bytes 786432 | tf_op jit(solution)/shard_map/all_to_all | solution.py:520
  183.2 0.7 collective-permute-start.29
  183.9 0.7 collective-permute-start.30
  184.6 15.5 %collective-permute-start.31 = (bf16[32,1536]{1,0:T(8,128)(2,1)S(1)}, bf16[32,1536]{1,0:T(8,128)(2,1)S(1)}, u32[]{:S(2)}, u32[]{:S(2)}) collective-permute-start(bf16[32,1536]{1,0:T(8,128)(2,1)S(1)} %shard_map.160.held_ref), channel_id=1, source_target_pairs={{64,0},{192,128},{320,256},{448,384},{65,1},{193,129},{321,257},{4... | collective-permute-start | bytes 294920 | tf_op jit(solution)/shard_map/ppermute | solution.py:428
  201.4 3.4 %collective-permute-start.32 = (bf16[2,16,16,256]{3,2,1,0:T(8,128)(2,1)S(1)}, bf16[2,16,16,256]{3,2,1,0:T(8,128)(2,1)S(1)}, u32[]{:S(2)}, u32[]{:S(2)}) collective-permute-start(bf16[2,16,16,256]{3,2,1,0:T(8,128)(2,1)S(1)} %get-tuple-element.409), channel_id=1, source_target_pairs={{0,1},{1,0},{2,3},{3,2},{4,5},{5,4},{6,7},{7,6},{8,9},{9,8},{10,11... | collective-permute-start | bytes 786440 | tf_op jit(solution)/shard_map/ppermute | solution.py:306
  204.9 7.4 %collective-permute-start.33 = (bf16[16,16,256]{2,1,0:T(8,128)(2,1)S(1)}, bf16[16,16,256]{2,1,0:T(8,128)(2,1)S(1)}, u32[]{:S(2)}, u32[]{:S(2)}) collective-permute-start(bf16[16,16,256]{2,1,0:T(8,128)(2,1)S(1)} %get-tuple-element.412), channel_id=1, source_target_pairs={{0,32},{32,0},{1,33},{33,1},{2,34},{34,2},{3,35},{35,3},{4,36},{36... | collective-permute-start | bytes 393224 | tf_op jit(solution)/shard_map/ppermute | solution.py:306
  212.4 17.9 %collective-permute-start.34 = (bf16[8,16,256]{2,1,0:T(8,128)(2,1)S(1)}, bf16[8,16,256]{2,1,0:T(8,128)(2,1)S(1)}, u32[]{:S(2)}, u32[]{:S(2)}) collective-permute-start(bf16[8,16,256]{2,1,0:T(8,128)(2,1)S(1)} %get-tuple-element.414), channel_id=1, source_target_pairs={{0,16},{2,18},{4,20},{6,22},{8,24},{10,26},{12,28},{14,30},{16,0},... | collective-permute-start | bytes 196616 | tf_op jit(solution)/shard_map/ppermute | solution.py:458
  230.3 9.7 %collective-permute-start.35 = (bf16[4,16,256]{2,1,0:T(8,128)(2,1)S(1)}, bf16[4,16,256]{2,1,0:T(8,128)(2,1)S(1)}, u32[]{:S(2)}, u32[]{:S(2)}) collective-permute-start(bf16[4,16,256]{2,1,0:T(8,128)(2,1)S(1)} %get-tuple-element.416), channel_id=1, source_target_pairs={{0,8},{2,10},{4,12},{6,14},{8,0},{10,2},{12,4},{14,6},{16,24},{18,... | collective-permute-start | bytes 98312 | tf_op jit(solution)/shard_map/ppermute | solution.py:458
  240.0 6.5 %collective-permute-start.36 = (bf16[2,16,256]{2,1,0:T(8,128)(2,1)S(1)}, bf16[2,16,256]{2,1,0:T(8,128)(2,1)S(1)}, u32[]{:S(2)}, u32[]{:S(2)}) collective-permute-start(bf16[2,16,256]{2,1,0:T(8,128)(2,1)S(1)} %get-tuple-element.418), channel_id=1, source_target_pairs={{0,4},{2,6},{4,0},{6,2},{8,12},{10,14},{12,8},{14,10},{16,20},{18,... | collective-permute-start | bytes 49160 | tf_op jit(solution)/shard_map/ppermute | solution.py:458
  246.6 5.5 %collective-permute-start.37 = (bf16[1,16,256]{2,1,0:T(8,128)(2,1)S(1)}, bf16[1,16,256]{2,1,0:T(8,128)(2,1)S(1)}, u32[]{:S(2)}, u32[]{:S(2)}) collective-permute-start(bf16[1,16,256]{2,1,0:T(8,128)(2,1)S(1)} %get-tuple-element.420), channel_id=1, source_target_pairs={{0,2},{2,0},{4,6},{6,4},{8,10},{10,8},{12,14},{14,12},{16,18},{18,... | collective-permute-start | bytes 24584 | tf_op jit(solution)/shard_map/ppermute | solution.py:458
